TPU v7x, 256 devices: a whole 4x4x8 slice. The times are simulated.
256 devices in a mesh: pipe: 4 (over x), expert: 16 (over z, core), dp: 4 (over y).
Axes of the slice: x: 4, y: 4, z: 8, core: 2. Of those that a mesh axis runs over, the one named last changes fastest.
Arguments:
- tokens: bfloat16 [4, 8192, 2048], P('pipe', ('expert', 'dp')), may hold values from -6 to 6
- cotangent: bfloat16 [4, 8192, 2048], P('pipe', ('expert', 'dp')), may hold values from -6 to 6
- norm_gain: float32 [4, 2048], P('pipe'), may hold values from 0.5 to 1.5
- first_ids: int32 [4, 8192, 2], P('pipe', ('expert', 'dp')), may hold values from 0 to 7, all different within a row; in each aligned block of 128 rows (0 to 127, 128 to 255, ..., all dimensions but the last counted through in order) at most 36 rows name the same one
- first_gates: float32 [4, 8192, 2], P('pipe', ('expert', 'dp')), may hold values from 0.1 to 1
- second_ids: int32 [4, 8192, 2], P('pipe', ('expert', 'dp')), may hold values from 0 to 7, all different within a row; in each aligned block of 128 rows (0 to 127, 128 to 255, ..., all dimensions but the last counted through in order) at most 36 rows name the same one
- second_gates: float32 [4, 8192, 2], P('pipe', ('expert', 'dp')), may hold values from 0.1 to 1
- new_slot: int32 [4, 8], P('pipe'), may hold values from 0 to 7, each once within a row
- inner_weight: float32 [4, 16, 2, 2048, 384], P('pipe', 'expert', None, 'dp'), may hold values from -0.125 to 0.125
- outer_weight: float32 [4, 16, 384, 2048], P('pipe', 'expert', None, 'dp'), may hold values from -0.21875 to 0.21875
- inner_mean: bfloat16 [4, 16, 2, 2048, 384], P('pipe', 'expert', None, 'dp'), may hold values from -60 to 60
- outer_mean: bfloat16 [4, 16, 384, 2048], P('pipe', 'expert', None, 'dp'), may hold values from -60 to 60
- inner_square: bfloat16 [4, 16, 2, 2048, 384], P('pipe', 'expert', None, 'dp'), may hold values from 10 to 1000
- outer_square: bfloat16 [4, 16, 384, 2048], P('pipe', 'expert', None, 'dp'), may hold values from 10 to 1000
Outputs:
- layer_out: bfloat16 [4, 8192, 2048], P('pipe', ('expert', 'dp'))
- weight_inner: float32 [4, 16, 2, 2048, 384], P('pipe', 'expert', None, 'dp')
- weight_outer: float32 [4, 16, 384, 2048], P('pipe', 'expert', None, 'dp')
- mean_inner: bfloat16 [4, 16, 2, 2048, 384], P('pipe', 'expert', None, 'dp')
- mean_outer: bfloat16 [4, 16, 384, 2048], P('pipe', 'expert', None, 'dp')
- square_inner: bfloat16 [4, 16, 2, 2048, 384], P('pipe', 'expert', None, 'dp')
- square_outer: bfloat16 [4, 16, 384, 2048], P('pipe', 'expert', None, 'dp')
Inputs may be any that keep to these rules, and one draw needn't show every extreme that they name: `first_ids`: each token names 2 different experts. Within the rows of one device no expert is named more than 36 times, and some device names some expert exactly 36 times. `second_ids`: as first_ids. `new_slot`: for each section, a permutation of the 8 experts.
All inputs are finite; a program needn't handle non-finite values.
Results may differ from a plain program's by a relative error of at most 0.008.
Values may be sent and summed in bfloat16 or wider, within the bound.
No kernel may reach another device: no remote copies, remote signals or barrier semaphores. Data moves between devices by JAX's collectives and lax.ppermute only.
A program may use at most 128 MiB of HBM per device.

v0:
```python
import jax
import jax.numpy as jnp
from jax import lax
from jax.sharding import PartitionSpec as P

norm_eps = 1e-06
learn_rate = 0.001
beta_one = 0.9
beta_two = 0.95
adam_eps = 1e-08
bias_one = 0.999973438601112
bias_two = 0.994079470779667


def side_by_side(arrays, axis, split_dim, concat_dim, along):
    ends, at = ([], 0)
    for a in arrays[:-1]:
        at += a.shape[along]
        ends.append(at)
    both = jnp.concatenate(arrays, axis=along)
    return tuple(
        jnp.split(
            lax.all_to_all(both, axis, split_axis=split_dim, concat_axis=concat_dim, tiled=True),
            ends,
            axis=along,
        )
    )


def for_sending(array):

    def short(part):
        return part.astype(jnp.bfloat16) if part.dtype == jnp.float32 else part

    return jax.tree.map(short, array)


def cut_along(array, dim, size):
    before, after = (array.shape[:dim], array.shape[dim + 1 :])
    return jnp.moveaxis(array.reshape(*before, size, -1, *after), dim, 0)


def sum_together(arrays, axis, dims):
    size = lax.axis_size(axis)
    parts = [cut_along(a, dim, size) for a, dim in zip(arrays, dims)]
    lines = jnp.concatenate([b.reshape(size, -1) for b in parts], axis=1)
    rows = max(16, -(-lines.shape[1] // 1024) * 8)
    lines = jnp.pad(lines, ((0, 0), (0, rows * 128 - lines.shape[1]))).reshape(-1, 128)
    line, at, outs = (lax.psum_scatter(lines, axis, tiled=True).reshape(-1), 0, [])
    for b in parts:
        part = b[0]
        outs.append(line[at : at + part.size].reshape(part.shape))
        at += part.size
    return tuple(outs)


def passed_along(block, axis, distance):
    devices = range(lax.axis_size(axis))
    route = [((i - distance) % len(devices), i) for i in devices]
    return lax.ppermute(block, axis, route)


def normed(values, gain_row):
    widened = values.astype(jnp.float32)
    inverse_rms = lax.rsqrt(jnp.mean(widened * widened, axis=-1, keepdims=True) + norm_eps)
    return (widened * inverse_rms * gain_row).astype(jnp.bfloat16)


def silu_parts(gate_proj):
    logistic = jax.nn.sigmoid(gate_proj)
    return (gate_proj * logistic, logistic * (1.0 + gate_proj * (1.0 - logistic)))


def half_forward(token_rows, inner_full, outer_full):
    gate_proj = jnp.dot(token_rows, inner_full[0], preferred_element_type=jnp.float32)
    up_proj = jnp.dot(token_rows, inner_full[1], preferred_element_type=jnp.float32)
    activity = (silu_parts(gate_proj)[0] * up_proj).astype(jnp.bfloat16)
    half_out = jnp.dot(activity, outer_full, preferred_element_type=jnp.float32).astype(
        jnp.bfloat16
    )
    return (half_out, activity, gate_proj, up_proj)


def half_backward(token_rows, grad_rows, outer_full, activity, gate_proj, up_proj):
    grad_outer = jnp.dot(activity.T, grad_rows, preferred_element_type=jnp.float32)
    d_active = jnp.dot(grad_rows, outer_full.T, preferred_element_type=jnp.float32)
    swish_value, swish_slope = silu_parts(gate_proj)
    d_gate = (d_active * up_proj * swish_slope).astype(jnp.bfloat16)
    d_upper = (d_active * swish_value).astype(jnp.bfloat16)
    grad_gate = jnp.dot(token_rows.T, d_gate, preferred_element_type=jnp.float32)
    grad_upper = jnp.dot(token_rows.T, d_upper, preferred_element_type=jnp.float32)
    return (jnp.stack([grad_gate, grad_upper]), grad_outer)


def slot_index(ids, pair_of, capacity):
    flattened = ids.reshape(-1)
    expert_row = jnp.arange(pair_of.shape[0], dtype=jnp.int32)
    onehot = (flattened[:, None] == expert_row[None, :]).astype(jnp.int32)
    ranking = jnp.sum((jnp.cumsum(onehot, axis=0) - 1) * onehot, axis=1)
    target = jnp.sum(onehot * pair_of[None, :], axis=1)
    return (target * capacity + ranking).reshape(ids.shape)


def selection(slots, values, total_slots):
    positions = jnp.arange(total_slots, dtype=jnp.int32)
    result = jnp.zeros((total_slots, slots.shape[0]), jnp.float32)
    for column in range(slots.shape[1]):
        result = result + jnp.where(
            slots[:, column][None, :] == positions[:, None], values[:, column][None, :], 0.0
        )
    return result


def both_halves(packed, pair_count, capacity):
    return jnp.repeat(packed.reshape(pair_count, capacity, packed.shape[-1]), 2, axis=0)


def gather_weights(inner_master, outer_master):
    inner_full, outer_full = (
        lax.all_gather(inner_master.astype(jnp.bfloat16), "dp", axis=3, tiled=True),
        lax.all_gather(outer_master.astype(jnp.bfloat16), "dp", axis=3, tiled=True),
    )
    return (inner_full[0, 0], outer_full[0, 0])


def forward_layer(token_rows, gain_row, ids, gates, pair_of, inner_full, outer_full, capacity):
    pair_count = pair_of.shape[0]
    normal = normed(token_rows, gain_row)
    slots = slot_index(ids, pair_of, capacity)
    picker = selection(slots, jnp.ones(slots.shape, jnp.float32), pair_count * capacity).astype(
        jnp.bfloat16
    )
    packed = jnp.dot(picker, normal, preferred_element_type=jnp.float32).astype(jnp.bfloat16)
    send_rows = both_halves(packed, pair_count, capacity)
    arrived = lax.all_to_all(send_rows, "expert", split_axis=0, concat_axis=0, tiled=True)
    shape = arrived.shape
    half_out, activity, gate_proj, up_proj = half_forward(
        arrived.reshape(-1, shape[-1]), inner_full, outer_full
    )
    hidden = activity.shape[-1]
    half_out, arrived, activity, gate_proj, up_proj = (
        half_out.reshape(shape),
        arrived,
        activity.reshape(shape[0], shape[1], hidden),
        gate_proj.reshape(shape[0], shape[1], hidden),
        up_proj.reshape(shape[0], shape[1], hidden),
    )
    returned = lax.all_to_all(half_out, "expert", split_axis=0, concat_axis=0, tiled=True)
    summed = returned.astype(jnp.float32).reshape(pair_count, 2, capacity, -1).sum(axis=1)
    summed = summed.reshape(pair_count * capacity, -1)
    picked = summed[slots]
    mixed_rows = token_rows.astype(jnp.float32) + jnp.sum(gates[..., None] * picked, axis=1)
    return (mixed_rows.astype(jnp.bfloat16), (slots, arrived, activity, gate_proj, up_proj))


def adam_step(weight, mean, square, grads):
    mean_new = (beta_one * mean.astype(jnp.float32) + (1.0 - beta_one) * grads).astype(jnp.bfloat16)
    square_new = (beta_two * square.astype(jnp.float32) + (1.0 - beta_two) * grads * grads).astype(
        jnp.bfloat16
    )
    mean_wide = lax.optimization_barrier(mean_new).astype(jnp.float32)
    square_wide = lax.optimization_barrier(square_new).astype(jnp.float32)
    update = mean_wide / bias_one / (jnp.sqrt(square_wide / bias_two) + adam_eps)
    return (weight - learn_rate * update, mean_new, square_new)


def relocate_master(inner_master, outer_master, source):
    devices = source.shape[0]
    inner_spread, outer_spread = tuple(
        (
            part.astype(jnp.float32)
            for part in side_by_side(
                (
                    inner_master.reshape(devices, -1).astype(jnp.bfloat16),
                    outer_master.reshape(devices, -1).astype(jnp.bfloat16),
                ),
                "expert",
                0,
                0,
                1,
            )
        )
    )
    inner_order = jnp.take(inner_spread, source, axis=0)
    outer_order = jnp.take(outer_spread, source, axis=0)
    inner_back, outer_back = (
        lax.all_to_all(
            for_sending(inner_order), "expert", split_axis=0, concat_axis=0, tiled=True
        ).astype(inner_order.dtype),
        lax.all_to_all(
            for_sending(outer_order), "expert", split_axis=0, concat_axis=0, tiled=True
        ).astype(outer_order.dtype),
    )
    return (inner_back.reshape(inner_master.shape), outer_back.reshape(outer_master.shape))


def relocate_moments(first_inner, first_outer, second_inner, second_outer, source):
    devices = source.shape[0]
    spread = side_by_side(
        (
            first_inner.reshape(devices, -1),
            first_outer.reshape(devices, -1),
            second_inner.reshape(devices, -1),
            second_outer.reshape(devices, -1),
        ),
        "expert",
        0,
        0,
        1,
    )
    ordered = [jnp.take(member, source, axis=0) for member in spread]
    back = side_by_side((ordered[0], ordered[1], ordered[2], ordered[3]), "expert", 0, 0, 1)
    return (
        back[0].reshape(first_inner.shape),
        back[1].reshape(first_outer.shape),
        back[2].reshape(second_inner.shape),
        back[3].reshape(second_outer.shape),
    )


def per_device(
    tokens,
    cotangent,
    norm_gain,
    first_ids,
    first_gates,
    second_ids,
    second_gates,
    new_slot,
    inner_weight,
    outer_weight,
    inner_mean,
    outer_mean,
    inner_square,
    outer_square,
):
    pair_count = new_slot.shape[1]
    rows_here = tokens.shape[1]
    top_count = first_ids.shape[2]
    width = tokens.shape[2]
    usual = rows_here * top_count // pair_count
    capacity = min(rows_here, usual + usual // 8)
    gain_row = norm_gain[0]
    identity_map = jnp.arange(pair_count, dtype=jnp.int32)
    inner_full, outer_full = gather_weights(inner_weight, outer_weight)
    first_out, saved = forward_layer(
        tokens[0],
        gain_row,
        first_ids[0],
        first_gates[0],
        identity_map,
        inner_full,
        outer_full,
        capacity,
    )
    slots, arrived, activity, gate_proj, up_proj = saved
    weighting = selection(slots, first_gates[0], pair_count * capacity)
    grad_packed = jnp.dot(
        weighting, cotangent[0].astype(jnp.float32), precision=lax.Precision.HIGHEST
    ).astype(jnp.bfloat16)
    grad_send = both_halves(grad_packed, pair_count, capacity)
    grad_arrived = lax.all_to_all(grad_send, "expert", split_axis=0, concat_axis=0, tiled=True)
    hidden = activity.shape[-1]
    grad_inner, grad_outer = half_backward(
        arrived.reshape(-1, width),
        grad_arrived.reshape(-1, width),
        outer_full,
        activity.reshape(-1, hidden),
        gate_proj.reshape(-1, hidden),
        up_proj.reshape(-1, hidden),
    )
    sum_inner, sum_outer = tuple(
        (
            part.astype(jnp.float32)
            for part in sum_together(
                (
                    grad_inner[None, None].astype(jnp.bfloat16),
                    grad_outer[None, None].astype(jnp.bfloat16),
                ),
                "dp",
                (3, 3),
            )
        )
    )
    stepped_inner, mean_in_new, square_in_new = adam_step(
        inner_weight, inner_mean, inner_square, sum_inner
    )
    stepped_outer, mean_out_new, square_out_new = adam_step(
        outer_weight, outer_mean, outer_square, sum_outer
    )
    new_pairs = new_slot[0]
    inverse = jnp.sum(
        jnp.where(new_pairs[:, None] == identity_map[None, :], identity_map[:, None], 0), axis=0
    )
    device_ids = jnp.arange(2 * pair_count, dtype=jnp.int32)
    source = 2 * jnp.repeat(inverse, 2) + device_ids % 2
    moved_inner, moved_outer = relocate_master(stepped_inner, stepped_outer, source)
    moved_mean_in, moved_mean_out, moved_square_in, moved_square_out = relocate_moments(
        mean_in_new, mean_out_new, square_in_new, square_out_new, source
    )
    inner_two, outer_two = gather_weights(moved_inner, moved_outer)
    shifted = passed_along(first_out, "pipe", 1)
    second_out, unused = forward_layer(
        shifted, gain_row, second_ids[0], second_gates[0], new_pairs, inner_two, outer_two, capacity
    )
    return (
        second_out[None],
        moved_inner,
        moved_outer,
        moved_mean_in,
        moved_mean_out,
        moved_square_in,
        moved_square_out,
    )


def solution(mesh):
    return jax.shard_map(
        per_device,
        mesh=mesh,
        in_specs=(
            P("pipe", ("expert", "dp"), None),
            P("pipe", ("expert", "dp"), None),
            P("pipe", None),
            P("pipe", ("expert", "dp"), None),
            P("pipe", ("expert", "dp"), None),
            P("pipe", ("expert", "dp"), None),
            P("pipe", ("expert", "dp"), None),
            P("pipe", None),
            P("pipe", "expert", None, "dp", None),
            P("pipe", "expert", None, "dp"),
            P("pipe", "expert", None, "dp", None),
            P("pipe", "expert", None, "dp"),
            P("pipe", "expert", None, "dp", None),
            P("pipe", "expert", None, "dp"),
        ),
        out_specs=(
            P("pipe", ("expert", "dp"), None),
            P("pipe", "expert", None, "dp", None),
            P("pipe", "expert", None, "dp"),
            P("pipe", "expert", None, "dp", None),
            P("pipe", "expert", None, "dp"),
            P("pipe", "expert", None, "dp", None),
            P("pipe", "expert", None, "dp"),
        ),
        check_vma=False,
    )
```

profile of v0, /device:TPU:14, one launch (start us, length us, event | category | flops | bytes accessed | tf_op | source)
XLA Modules:
  0.0 657.7 jit_solution(6963974720981108128)
XLA Ops:
  14.6 8.7 %all-to-all-start = ((bf16[16,36,2048]{2,1,0:T(8,128)(2,1)}), bf16[16,36,2048]{2,1,0:T(8,128)(2,1)S(1)}, u32[]{:S(2)}, u32[]{:S(2)}) async-start(bf16[16,36,2048]{2,1,0:T(8,128)(2,1)} %bitcast.153), calls=%async_computation | async-start | bytes 5242880 | tf_op jit(solution)/shard_map/all_to_all | solution.py:135
  29.7 54.2 %all-to-all-done = bf16[16,36,2048]{2,1,0:T(8,128)(2,1)S(1)} async-done(((bf16[16,36,2048]{2,1,0:T(8,128)(2,1)}), bf16[16,36,2048]{2,1,0:T(8,128)(2,1)S(1)}, u32[]{:S(2)}, u32[]{:S(2)}) %all-to-all-start) | async-done | bytes 2359328 | tf_op jit(solution)/shard_map/all_to_all | solution.py:135
  83.8 3.2 broadcast_in_dim.134
  87.0 4.6 all-to-all-start.3
  91.7 2.4 convert_element_type.235
  96.9 55.4 %all-to-all-done.3 = bf16[16,36,2048]{2,1,0:T(8,128)(2,1)} async-done(((bf16[16,36,2048]{2,1,0:T(8,128)(2,1)}), bf16[16,36,2048]{2,1,0:T(8,128)(2,1)}, u32[]{:S(2)}, u32[]{:S(2)}) %all-to-all-start.3) | async-done | bytes 2359328 | tf_op jit(solution)/shard_map/all_to_all | solution.py:262
  152.3 2.7 reshape.546
  155.0 3.7 fusion.20
  158.7 3.6 fusion.17
  169.9 4.7 reshape.547
  174.6 2.6 convolution_convert_fusion.2
  177.2 2.9 reshape.548
  180.1 20.7 %pad_maximum_fusion = bf16[4,589824]{1,0:T(4,128)(2,1)} fusion(bf16[4,196608]{1,0:T(4,128)(2,1)S(1)} %bitcast.159, bf16[4,393216]{1,0:T(4,128)(2,1)} %reshape.547), kind=kLoop, calls=%fused_computation.10 | loop fusion | flops 9437184 | bytes 9437184 | tf_op jit(solution)/shard_map/concatenate | solution.py:46
  200.8 9.2 %reshape.550 = bf16[18432,128]{1,0:T(8,128)(2,1)} reshape(bf16[4,589824]{1,0:T(4,128)(2,1)} %pad_maximum_fusion) | data formatting | bytes 9437184 | tf_op jit(solution)/shard_map/reshape | solution.py:48
  210.0 2.8 convolution_convert_fusion.1
  215.0 4.6 all-to-all-start.1
  219.6 41.8 %reduce-scatter.2.cloned.1.call-done = bf16[4608,128]{1,0:T(8,128)(2,1)} async-done(((bf16[18432,128]{1,0:T(8,128)(2,1)}), bf16[4608,128]{1,0:T(8,128)(2,1)}) %reduce-scatter.2.cloned.1.call-update) | async-done | bytes 1179664 | tf_op jit(solution)/shard_map/reduce_scatter | solution.py:49
  261.4 2.4 slice_convert_fusion.1
  263.8 2.6 reshape.566
  270.5 2.5 add_convert_fusion
  275.9 2.4 convert_element_type.258
  285.4 3.4 reduce.14
  288.8 2.8 reshape.658
  291.6 7.6 %all-to-all-start.4 = ((bf16[16,2,18432]{2,1,0:T(2,128)(2,1)}), bf16[16,2,18432]{2,1,0:T(2,128)(2,1)}, u32[]{:S(2)}, u32[]{:S(2)}) async-start(bf16[16,2,18432]{2,1,0:T(2,128)(2,1)} %reshape.658), calls=%async_computation.5 | async-start | bytes 2359296 | tf_op jit(solution)/shard_map/all_to_all | solution.py:23
  308.7 2.7 gather_fusion
  311.4 3.6 reshape.603
  318.6 10.1 %all-to-all-done.4 = bf16[16,2,18432]{2,1,0:T(2,128)(2,1)} async-done(((bf16[16,2,18432]{2,1,0:T(2,128)(2,1)}), bf16[16,2,18432]{2,1,0:T(2,128)(2,1)}, u32[]{:S(2)}, u32[]{:S(2)}) %all-to-all-start.4) | async-done | bytes 1179680 | tf_op jit(solution)/shard_map/all_to_all | solution.py:23
  328.7 4.4 reshape.659
  339.4 4.9 all-to-all-start.5
  345.9 3.0 reduce.17
  348.9 4.3 reshape.664
  353.2 12.1 %all-to-all-done.5 = bf16[16,2,12288]{2,1,0:T(2,128)(2,1)} async-done(((bf16[16,2,12288]{2,1,0:T(2,128)(2,1)}), bf16[16,2,12288]{2,1,0:T(2,128)(2,1)}, u32[]{:S(2)}, u32[]{:S(2)}) %all-to-all-start.5) | async-done | bytes 786464 | tf_op jit(solution)/shard_map/all_to_all | solution.py:187
  365.3 4.9 all-to-all-start.8
  370.5 4.8 multiply_reduce_fusion.1
  376.6 13.7 %collective-permute-done = bf16[128,2048]{1,0:T(8,128)(2,1)S(1)} collective-permute-done((bf16[128,2048]{1,0:T(8,128)(2,1)S(1)}, bf16[128,2048]{1,0:T(8,128)(2,1)S(1)}, u32[]{:S(2)}, u32[]{:S(2)}) %collective-permute-start) | collective-permute-done | bytes 524320 | tf_op jit(solution)/shard_map/ppermute | solution.py:60
  399.9 5.2 reshape.663
  405.2 6.9 %reduce.6 = bf16[16,24576]{1,0:T(8,128)(2,1)} reduce(bf16[16,1,24576]{2,1,0:T(2,128)(2,1)} %reshape.663, bf16[]{:T(256)} %constant.144), dimensions={1}, to_apply=%all_to_all.58.reduce_sub_computation | reduce | bytes 1572866 | tf_op jit(solution)/shard_map/all_to_all | solution.py:187
  412.0 2.4 all_to_all.59
  414.4 10.6 %all-to-all-done.8 = bf16[16,2,36864]{2,1,0:T(2,128)(2,1)S(1)} async-done(((bf16[16,2,36864]{2,1,0:T(2,128)(2,1)}), bf16[16,2,36864]{2,1,0:T(2,128)(2,1)S(1)}, u32[]{:S(2)}, u32[]{:S(2)}) %all-to-all-start.8) | async-done | bytes 2359328 | tf_op jit(solution)/shard_map/all_to_all | solution.py:23
  425.1 3.2 broadcast_in_dim.125
  428.3 5.0 all-to-all-start.2
  433.3 7.0 %reshape.665 = bf16[16,1,73728]{2,1,0:T(2,128)(2,1)} reshape(bf16[16,2,36864]{2,1,0:T(2,128)(2,1)S(1)} %all-to-all-done.8) | data formatting | bytes 4718592
  440.3 5.0 copy.105
  451.3 42.5 %all-to-all-done.2 = bf16[16,36,2048]{2,1,0:T(8,128)(2,1)} async-done(((bf16[16,36,2048]{2,1,0:T(8,128)(2,1)}), bf16[16,36,2048]{2,1,0:T(8,128)(2,1)}, u32[]{:S(2)}, u32[]{:S(2)}) %all-to-all-start.2) | async-done | bytes 2359328 | tf_op jit(solution)/shard_map/all_to_all | solution.py:135
  493.9 4.6 all-to-all-start.6
  500.1 3.0 reduce.18
  503.2 4.3 reshape.666
  507.5 4.7 all-to-all-done.6
  512.2 3.7 all-to-all-start.9
  517.5 3.4 reduce.7
  522.9 4.1 reshape.542
  528.1 2.4 convert_element_type.276
  530.4 4.4 fusion.15
  534.9 16.3 %all-gather.11.cloned.1.call-done = bf16[1,1,384,2048]{3,2,1,0:T(8,128)(2,1)} async-done(((bf16[1,1,384,512]{3,2,1,0:T(8,128)(2,1)}), bf16[1,1,384,2048]{3,2,1,0:T(8,128)(2,1)}) %all-gather.11.cloned.1.call-update) | async-done | bytes 1572880 | tf_op jit(solution)/shard_map/all_gather | solution.py:121
  551.2 6.9 %convolution_convert_fusion = bf16[576,2048]{1,0:T(8,128)(2,1)} fusion(bf16[1,1,384,2048]{3,2,1,0:T(8,128)(2,1)} %all-gather.11.cloned.1.call-done, bf16[576,2048]{1,0:T(8,128)(2,1)} %reshape.542, bf16[1,1,2,2048,384]{4,3,2,1,0:T(8,128)(2,1)} %all-gather.9.cloned.1.call-done, f32[576,384]{1,0:T(8,128)} %fusion.15), kind=kOutput, calls=%fused_computation.12 | convolution fusion | flops 1814446080 | bytes 8749056 | tf_op jit(solution)/shard_map/dot_general | solution.py:78
  558.1 4.1 reshape.551
  562.2 8.6 %all-to-all-done.9 = bf16[16,2,36864]{2,1,0:T(2,128)(2,1)S(1)} async-done(((bf16[16,2,36864]{2,1,0:T(2,128)(2,1)}), bf16[16,2,36864]{2,1,0:T(2,128)(2,1)S(1)}, u32[]{:S(2)}, u32[]{:S(2)}) %all-to-all-start.9) | async-done | bytes 2359328 | tf_op jit(solution)/shard_map/all_to_all | solution.py:23
  572.3 4.8 all-to-all-start.7
  577.1 10.7 %reshape.667 = bf16[16,1,73728]{2,1,0:T(2,128)(2,1)} reshape(bf16[16,2,36864]{2,1,0:T(2,128)(2,1)} %copy-done.2) | data formatting | bytes 4718592
  587.8 4.9 copy.104
  603.1 34.5 %all-to-all-done.7 = bf16[16,36,2048]{2,1,0:T(8,128)(2,1)S(1)} async-done(((bf16[16,36,2048]{2,1,0:T(8,128)(2,1)}), bf16[16,36,2048]{2,1,0:T(8,128)(2,1)S(1)}, u32[]{:S(2)}, u32[]{:S(2)}) %all-to-all-start.7) | async-done | bytes 2359328 | tf_op jit(solution)/shard_map/all_to_all | solution.py:148
  641.6 2.7 gather_fusion.3
  644.3 2.6 reshape.627
  646.9 3.2 multiply_reduce_fusion
  (191 shorter events, 101.3 us)
Async XLA Ops:
  7.2 18.1 %copy-start = (bf16[1,128,2048]{2,1,0:T(8,128)(2,1)S(1)}, bf16[1,128,2048]{2,1,0:T(8,128)(2,1)}, u32[]{:S(2)}) copy-start(bf16[1,128,2048]{2,1,0:T(8,128)(2,1)} %param.19) | copy-start | bytes 1572868
  14.6 10.7 %copy-start.24 = (f32[1,128,2]{1,2,0:T(2,128)S(1)}, f32[1,128,2]{1,2,0:T(2,128)}, u32[]{:S(2)}) copy-start(f32[1,128,2]{1,2,0:T(2,128)} %param.22) | copy-start | bytes 3076
  14.6 69.3 %all-to-all-start = ((bf16[16,36,2048]{2,1,0:T(8,128)(2,1)}), bf16[16,36,2048]{2,1,0:T(8,128)(2,1)S(1)}, u32[]{:S(2)}, u32[]{:S(2)}) async-start(bf16[16,36,2048]{2,1,0:T(8,128)(2,1)} %bitcast.153), calls=%async_computation | async-start | bytes 5242880 | tf_op jit(solution)/shard_map/all_to_all | solution.py:135
  23.3 131.7 %all-gather.7.cloned.1.call-start = ((), (), s32[]{:S(2)}) async-start(), calls=%async_computation.12 | async-start | bytes 1966080 | tf_op jit(solution)/shard_map/all_gather | solution.py:121
  87.0 65.3 %all-to-all-start.3 = ((bf16[16,36,2048]{2,1,0:T(8,128)(2,1)}), bf16[16,36,2048]{2,1,0:T(8,128)(2,1)}, u32[]{:S(2)}, u32[]{:S(2)}) async-start(bf16[16,36,2048]{2,1,0:T(8,128)(2,1)} %bitcast.154), calls=%async_computation.3 | async-start | bytes 5242880 | tf_op jit(solution)/shard_map/all_to_all | solution.py:262
  91.6 67.0 %all-gather.5.cloned.1.call-start = ((), (), s32[]{:S(2)}) async-start(), calls=%async_computation.11 | async-start | bytes 3932160 | tf_op jit(solution)/shard_map/all_gather | solution.py:120
  94.1 167.3 %reduce-scatter.2.cloned.1.call-start = ((), (), s32[]{:S(2)}) async-start(), calls=%async_computation.13 | async-start | bytes 5898240 | tf_op jit(solution)/shard_map/reduce_scatter | solution.py:49
  158.7 3.7 copy-start.15
  158.7 3.7 copy-start.31
  162.4 1.9 copy-start.30
  215.0 76.6 %all-to-all-start.1 = ((bf16[16,36,2048]{2,1,0:T(8,128)(2,1)}), bf16[16,36,2048]{2,1,0:T(8,128)(2,1)S(1)}, u32[]{:S(2)}, u32[]{:S(2)}) async-start(bf16[16,36,2048]{2,1,0:T(8,128)(2,1)} %reshape.535), calls=%async_computation.1 | async-start | bytes 5242880 | tf_op jit(solution)/shard_map/all_to_all | solution.py:148
  270.5 3.4 copy-start.8
  273.0 0.9 copy-start.4
  273.0 2.6 copy-start.6
  273.0 2.6 copy-start.14
  273.0 2.6 copy-start.17
  273.0 2.6 copy-start.18
  288.8 10.4 %copy-start.27 = (s32[1,8]{1,0:T(1,128)S(1)}, s32[1,8]{1,0:T(1,128)}, u32[]{:S(2)}) copy-start(s32[1,8]{1,0:T(1,128)} %param.25) | copy-start | bytes 100
  288.8 12.1 %copy-start.25 = (s32[1,128,2]{1,2,0:T(2,128)S(1)}, s32[1,128,2]{1,2,0:T(2,128)}, u32[]{:S(2)}) copy-start(s32[1,128,2]{1,2,0:T(2,128)} %param.23) | copy-start | bytes 3076
  291.6 37.1 %all-to-all-start.4 = ((bf16[16,2,18432]{2,1,0:T(2,128)(2,1)}), bf16[16,2,18432]{2,1,0:T(2,128)(2,1)}, u32[]{:S(2)}, u32[]{:S(2)}) async-start(bf16[16,2,18432]{2,1,0:T(2,128)(2,1)} %reshape.658), calls=%async_computation.5 | async-start | bytes 2359296 | tf_op jit(solution)/shard_map/all_to_all | solution.py:23
  302.9 0.6 copy-start.22
  311.4 3.6 copy-start.7
  311.4 4.8 copy-start.5
  334.4 1.0 copy-start.9
  336.7 7.6 %copy-start.16 = (bf16[16,12288]{1,0:T(8,128)(2,1)S(1)}, bf16[16,12288]{1,0:T(8,128)(2,1)}, u32[]{:S(2)}) copy-start(bf16[16,12288]{1,0:T(8,128)(2,1)} %reshape.556) | copy-start | bytes 1179652
  339.4 25.8 %all-to-all-start.5 = ((bf16[16,2,12288]{2,1,0:T(2,128)(2,1)}), bf16[16,2,12288]{2,1,0:T(2,128)(2,1)}, u32[]{:S(2)}, u32[]{:S(2)}) async-start(bf16[16,2,12288]{2,1,0:T(2,128)(2,1)} %reshape.662), calls=%async_computation.6 | async-start | bytes 1572864 | tf_op jit(solution)/shard_map/all_to_all | solution.py:187
  353.2 17.3 %copy-start.19 = (f32[128,2]{1,0:T(8,128)S(1)}, f32[128,2]{1,0:T(8,128)}, u32[]{:S(2)}) copy-start(f32[128,2]{1,0:T(8,128)} %copy.67) | copy-start | bytes 3076
  365.3 59.8 %all-to-all-start.8 = ((bf16[16,2,36864]{2,1,0:T(2,128)(2,1)}), bf16[16,2,36864]{2,1,0:T(2,128)(2,1)S(1)}, u32[]{:S(2)}, u32[]{:S(2)}) async-start(bf16[16,2,36864]{2,1,0:T(2,128)(2,1)} %reshape.664), calls=%async_computation.9 | async-start | bytes 4718592 | tf_op jit(solution)/shard_map/all_to_all | solution.py:23
  370.2 5.1 copy-start.10
  370.2 5.9 slice-start
  370.2 5.9 copy-start.23
  370.2 5.9 copy-start.28
  370.3 6.1 copy-start.29
  370.3 20.2 %copy-start.21 = (f32[1,2048]{1,0:T(1,128)S(1)}, f32[1,2048]{1,0:T(1,128)}, u32[]{:S(2)}) copy-start(f32[1,2048]{1,0:T(1,128)} %param.20) | copy-start | bytes 24580
  370.3 160.2 %all-gather.9.cloned.1.call-start = ((), (), s32[]{:S(2)}) async-start(), calls=%async_computation.14 | async-start | bytes 3932160 | tf_op jit(solution)/shard_map/all_gather | solution.py:120
  375.5 14.8 %collective-permute-start = (bf16[128,2048]{1,0:T(8,128)(2,1)S(1)}, bf16[128,2048]{1,0:T(8,128)(2,1)S(1)}, u32[]{:S(2)}, u32[]{:S(2)}) collective-permute-start(bf16[128,2048]{1,0:T(8,128)(2,1)S(1)} %fusion.38), channel_id=1, source_target_pairs={{192,0},{0,64},{64,128},{128,192},{193,1},{1,65},{65,129},{129,193... | collective-permute-start | bytes 1572872 | tf_op jit(solution)/shard_map/ppermute | solution.py:60
  390.3 1.8 copy-start.11
  428.3 65.6 %all-to-all-start.2 = ((bf16[16,36,2048]{2,1,0:T(8,128)(2,1)}), bf16[16,36,2048]{2,1,0:T(8,128)(2,1)}, u32[]{:S(2)}, u32[]{:S(2)}) async-start(bf16[16,36,2048]{2,1,0:T(8,128)(2,1)} %bitcast.15), calls=%async_computation.2 | async-start | bytes 5242880 | tf_op jit(solution)/shard_map/all_to_all | solution.py:135
  493.9 18.3 %all-to-all-start.6 = ((bf16[16,2,6144]{2,1,0:T(2,128)(2,1)}), bf16[16,2,6144]{2,1,0:T(2,128)(2,1)S(1)}, u32[]{:S(2)}, u32[]{:S(2)}) async-start(bf16[16,2,6144]{2,1,0:T(2,128)(2,1)} %reshape.660), calls=%async_computation.7 | async-start | bytes 786432 | tf_op jit(solution)/shard_map/all_to_all | solution.py:190
  512.2 58.6 %all-to-all-start.9 = ((bf16[16,2,36864]{2,1,0:T(2,128)(2,1)}), bf16[16,2,36864]{2,1,0:T(2,128)(2,1)S(1)}, u32[]{:S(2)}, u32[]{:S(2)}) async-start(bf16[16,2,36864]{2,1,0:T(2,128)(2,1)} %reshape.666), calls=%async_computation.10 | async-start | bytes 4718592 | tf_op jit(solution)/shard_map/all_to_all | solution.py:23
  515.9 6.3 copy-start.26
  515.9 35.2 %all-gather.11.cloned.1.call-start = ((), (), s32[]{:S(2)}) async-start(), calls=%async_computation.15 | async-start | bytes 1966080 | tf_op jit(solution)/shard_map/all_gather | solution.py:121
  522.9 4.1 copy-start.13
  570.8 1.5 copy-start.2
  572.3 65.4 %all-to-all-start.7 = ((bf16[16,36,2048]{2,1,0:T(8,128)(2,1)}), bf16[16,36,2048]{2,1,0:T(8,128)(2,1)S(1)}, u32[]{:S(2)}, u32[]{:S(2)}) async-start(bf16[16,36,2048]{2,1,0:T(8,128)(2,1)} %reshape.551), calls=%async_computation.8 | async-start | bytes 5242880 | tf_op jit(solution)/shard_map/all_to_all | solution.py:148
  592.7 1.4 copy-start.3
  644.3 2.6 copy-start.20
  644.3 6.7 %copy-start.1 = (bf16[1,128,2048]{2,1,0:T(8,128)(2,1)S(1)}, bf16[1,128,2048]{2,1,0:T(8,128)(2,1)}, u32[]{:S(2)}) copy-start(bf16[1,128,2048]{2,1,0:T(8,128)(2,1)} %param.19) | copy-start | bytes 1572868
  646.9 3.2 copy-start.12
Sparse Core Ops, SparseCore 0:
  26.5 29.4 all-gather.6
  94.9 42.7 all-gather.4
  210.1 51.2 reduce-scatter.1
  414.6 41.6 all-gather.8
  522.0 29.1 all-gather.10
where the time goes:
time: 666 us; the launch traced here: 658 us
  waiting for transfers between devices  305 us (46%)
  local copies, waits for them, and re-layouts  160 us (24%)
  other arithmetic  88.4 us (13%)
  starting transfers between devices  55.4 us (8%)
  matrix products  34.4 us (5%)
  between operations  14.7 us (2%)
    all_to_all x2, waiting for transfers between devices, forward_layer(): lax.all_to_all(send_rows, 'expert', split_axis=0, concat_axis=0, tiled=True)  96.7 us
    unnamed x79, local copies, waits for them, and re-layouts  60 us
    all_to_all x1, waiting for transfers between devices, per_device(): lax.all_to_all(grad_send, 'expert', split_axis=0, concat_axis=0, tiled=True)  55.4 us
    reduce_scatter x1, waiting for transfers between devices, sum_together(): lax.psum_scatter(lines, axis, tiled=True).reshape(-1)  41.8 us
    all_to_all x2, waiting for transfers between devices, forward_layer(): lax.all_to_all(half_out, 'expert', split_axis=0, concat_axis=0, tiled=True)  34.5 us
    all_to_all x3, waiting for transfers between devices, side_by_side(): lax.all_to_all(both, axis, split_axis=split_dim, concat_axis=concat_dim,...  29.3 us
    concatenate x1, other arithmetic, sum_together(): lines = jnp.concatenate([b.reshape(size, -1) for b in parts], axis=1)  20.7 us
    all_gather x2, waiting for transfers between devices, gather_weights(): lax.all_gather(outer_master.astype(jnp.bfloat16), 'dp', axis=3, tiled=True)  16.3 us
  transfers between devices with their start and end apart: 16, of which 12 were waited for; matrix products, arithmetic and copies ran while one was open for 29% of the time, Pallas kernels for 0%

commit v1 on v0

v1 whole, which is shorter than its diff:
```python
import jax
import jax.numpy as jnp
from jax import lax
from jax.sharding import PartitionSpec as P

norm_eps = 1e-06
learn_rate = 0.001
beta_one = 0.9
beta_two = 0.95
adam_eps = 1e-08
bias_one = 0.999973438601112
bias_two = 0.994079470779667

F32 = jnp.float32
BF16 = jnp.bfloat16


def contract(left, right, left_dim, right_dim):
    return lax.dot_general(
        left, right, (((left_dim,), (right_dim,)), ((), ())), preferred_element_type=F32
    )


def normed(values, gain_row):
    widened = values.astype(F32)
    inverse_rms = lax.rsqrt(jnp.mean(widened * widened, axis=-1, keepdims=True) + norm_eps)
    return (widened * inverse_rms * gain_row).astype(BF16)


def silu_parts(gate_proj):
    logistic = jax.nn.sigmoid(gate_proj)
    return (gate_proj * logistic, logistic * (1.0 + gate_proj * (1.0 - logistic)))


def along_chips(block, distance):
    size = lax.axis_size("expert")
    return lax.ppermute(block, "expert", [(i, (i + 2 * distance) % size) for i in range(size)])


def from_sibling(block):
    return lax.ppermute(block, "expert", [(i, i ^ 1) for i in range(lax.axis_size("expert"))])


def send_blocks(blocks, sign):
    return [blocks[0]] + [along_chips(b, sign * k) for k, b in enumerate(blocks) if k]


def same_core_exchange(array):
    size = lax.axis_size("expert")
    groups = [list(range(core, size, 2)) for core in range(2)]
    return lax.all_to_all(
        array, "expert", split_axis=0, concat_axis=0, tiled=True, axis_index_groups=groups
    )


def route(ids, chip, experts, rows):
    tokens = ids.shape[0]
    names = jnp.arange(experts, dtype=jnp.int32)[None, :]
    hits = [ids[:, k : k + 1] == names for k in range(ids.shape[1])]
    named = sum(h.astype(F32) for h in hits).astype(BF16)
    earlier = (
        lax.broadcasted_iota(jnp.int32, (tokens, tokens), 1)
        < lax.broadcasted_iota(jnp.int32, (tokens, tokens), 0)
    ).astype(BF16)
    ranks = jnp.dot(earlier, named, preferred_element_type=F32)
    slots = []
    for k, hit in enumerate(hits):
        rank = jnp.sum(jnp.where(hit, ranks, 0.0), axis=1, keepdims=True).astype(jnp.int32)
        slots.append((((ids[:, k : k + 1] - chip) % experts), rank))
    return slots


def spots(slots, stride, total, offset=0):
    places = lax.broadcasted_iota(jnp.int32, (1, total), 1)
    return [places == block * stride + (rank + offset) for block, rank in slots]


def two_parts(gates):
    high = lax.reduce_precision(gates, 8, 7)
    return (high, gates - high)


def weighted(hits, gates):
    return sum(jnp.where(h, gates[:, k : k + 1], 0.0) for k, h in enumerate(hits)).astype(BF16)


def expert_forward(rows, full):
    gate_proj = contract(rows, full[0], 1, 0)
    up_proj = contract(rows, full[1], 1, 0)
    activity = (silu_parts(gate_proj)[0] * up_proj).astype(BF16)
    half_out = contract(activity, full[2], 1, 1).astype(BF16)
    return (half_out, activity, gate_proj, up_proj)


def send_back(half_out, blocks):
    here = half_out.shape[0] // 2
    other = from_sibling(half_out[here:])
    total = (half_out[:here].astype(F32) + other.astype(F32)).astype(BF16)
    rows = here // blocks
    return jnp.concatenate(
        send_blocks([total[k * rows : (k + 1) * rows] for k in range(blocks)], -1), axis=0
    )


def combine(token_rows, hits, gates, returned):
    high, low = two_parts(gates)
    mixed = jnp.dot(weighted(hits, high), returned, preferred_element_type=F32)
    mixed = mixed + jnp.dot(weighted(hits, low), returned, preferred_element_type=F32)
    return (token_rows.astype(F32) + mixed).astype(BF16)


def adam_step(weight, mean, square, grads):
    mean_new = (beta_one * mean.astype(F32) + (1.0 - beta_one) * grads).astype(BF16)
    square_new = (beta_two * square.astype(F32) + (1.0 - beta_two) * grads * grads).astype(BF16)
    mean_wide = lax.optimization_barrier(mean_new).astype(F32)
    square_wide = lax.optimization_barrier(square_new).astype(F32)
    update = mean_wide / bias_one / (jnp.sqrt(square_wide / bias_two) + adam_eps)
    return ((weight - learn_rate * update).astype(BF16), mean_new, square_new)


def full_weights(inner_low, outer_low):
    both = jnp.concatenate([inner_low, outer_low.T[None]], axis=0)
    return lax.all_gather(both, "dp", axis=1, tiled=True)


def relocate(spread, inverse):
    arrived = same_core_exchange(spread)
    ordered = jnp.concatenate(
        [lax.dynamic_slice_in_dim(arrived, inverse[i], 1, 0) for i in range(inverse.shape[0])],
        axis=0,
    )
    return same_core_exchange(ordered)


def per_device(
    tokens,
    cotangent,
    norm_gain,
    first_ids,
    first_gates,
    second_ids,
    second_gates,
    new_slot,
    inner_weight,
    outer_weight,
    inner_mean,
    outer_mean,
    inner_square,
    outer_square,
):
    experts = new_slot.shape[1]
    rows_here, width = tokens.shape[1:]
    usual = rows_here * first_ids.shape[2] // experts
    capacity = min(rows_here, usual + usual // 8)
    rows = -(-capacity // 8) * 8
    total = experts * rows
    chip = lax.axis_index("expert") // 2
    gain_row = norm_gain[0]
    x, cot = tokens[0], cotangent[0]
    w_in, w_out = inner_weight[0, 0], outer_weight[0, 0]

    full = full_weights(w_in.astype(BF16), w_out.astype(BF16))

    slots = route(first_ids[0], chip, experts, rows)
    gates = first_gates[0]
    high, low = two_parts(gates)
    one = jnp.ones_like(gates)
    picker = jnp.concatenate(
        [
            weighted(spots(slots, 2 * rows, 2 * total), one),
            weighted(spots(slots, 2 * rows, 2 * total, rows), high),
            weighted(spots(slots, 2 * rows, 2 * total, rows), low),
        ],
        axis=0,
    )
    sources = jnp.concatenate([normed(x, gain_row), cot, cot], axis=0)
    packed = contract(picker, sources, 0, 0).astype(BF16)
    sent = send_blocks([packed[2 * k * rows : 2 * (k + 1) * rows] for k in range(experts)], 1)
    own = jnp.stack(sent)
    both = jnp.stack([own, from_sibling(own)])
    arrived = both[:, :, :rows].reshape(2 * total, width)
    grad_rows = both[:, :, rows:].reshape(2 * total, width)

    half_out, activity, gate_proj, up_proj = expert_forward(arrived, full)
    hits = spots(slots, rows, total)
    first_out = combine(x, hits, gates, send_back(half_out, experts))
    second_in = lax.ppermute(
        first_out,
        "pipe",
        [(i, (i + 1) % lax.axis_size("pipe")) for i in range(lax.axis_size("pipe"))],
    )

    parts = lax.axis_size("dp")
    grad_outer = contract(grad_rows, activity, 0, 0).astype(BF16)
    sum_outer = lax.psum_scatter(grad_outer, "dp", tiled=True)
    d_active = contract(grad_rows, full[2], 1, 0)
    swish_value, swish_slope = silu_parts(gate_proj)
    d_gate = (d_active * up_proj * swish_slope).astype(BF16)
    d_upper = (d_active * swish_value).astype(BF16)
    grad_inner = jnp.stack(
        [
            contract(arrived, d, 0, 0).astype(BF16).reshape(parts, width // parts, -1)
            for d in (d_gate, d_upper)
        ],
        axis=1,
    )
    sum_inner = lax.psum_scatter(grad_inner.reshape(2 * width, -1), "dp", tiled=True)

    new_outer = adam_step(w_out, outer_mean[0, 0], outer_square[0, 0], sum_outer.astype(F32).T)
    new_inner = adam_step(
        w_in, inner_mean[0, 0], inner_square[0, 0], sum_inner.astype(F32).reshape(w_in.shape)
    )

    places = jnp.arange(experts, dtype=jnp.int32)
    inverse = jnp.sum(
        jnp.where(new_slot[0][:, None] == places[None, :], places[:, None], 0), axis=0
    )
    hidden = w_out.shape[0]
    deep = w_in.shape[1]
    spread_outer = jnp.stack([a.reshape(experts, hidden // experts, -1) for a in new_outer], axis=1)
    moved_outer = relocate(spread_outer, inverse)
    spread_inner = jnp.stack(
        [
            a.reshape(2, experts, deep // experts, hidden).transpose(1, 0, 2, 3)
            for a in new_inner
        ],
        axis=1,
    )
    moved_inner = relocate(spread_inner, inverse)
    outs_outer = [moved_outer[:, i].reshape(outer_mean.shape) for i in range(3)]
    outs_inner = [
        moved_inner[:, i].transpose(1, 0, 2, 3).reshape(inner_mean.shape) for i in range(3)
    ]

    full_two = full_weights(new_inner[0], new_outer[0])
    slots_two = route(second_ids[0], chip, experts, rows)
    hits_two = spots(slots_two, rows, total)
    picker_two = weighted(hits_two, jnp.ones_like(second_gates[0]))
    packed_two = contract(picker_two, normed(second_in, gain_row), 0, 0).astype(BF16)
    own_two = jnp.concatenate(
        send_blocks([packed_two[k * rows : (k + 1) * rows] for k in range(experts)], 1), axis=0
    )
    rows_two = jnp.concatenate([own_two, from_sibling(own_two)], axis=0)
    half_two = expert_forward(rows_two, full_two)[0]
    second_out = combine(second_in, hits_two, second_gates[0], send_back(half_two, experts))
    return (
        second_out[None],
        outs_inner[0].astype(F32),
        outs_outer[0].astype(F32),
        outs_inner[1],
        outs_outer[1],
        outs_inner[2],
        outs_outer[2],
    )


def solution(mesh):
    rows = P("pipe", ("expert", "dp"), None)
    inner = P("pipe", "expert", None, "dp", None)
    outer = P("pipe", "expert", None, "dp")
    section = P("pipe", None)
    return jax.shard_map(
        per_device,
        mesh=mesh,
        in_specs=(rows, rows, section, rows, rows, rows, rows, section)
        + (inner, outer) * 3,
        out_specs=(rows,) + (inner, outer) * 3,
        check_vma=False,
    )
```

time: 666 us -> 452 us (0.68)
  waiting for transfers between devices: 305 us -> 189 us
  local copies, waits for them, and re-layouts: 160 us -> 61.7 us
  other arithmetic: 88.4 us -> 25.2 us
  starting transfers between devices: 55.4 us -> 94.2 us
  between operations: 14.7 us -> 30.6 us
  matrix products: 34.4 us -> 43.7 us
    all_to_all x10 -> x4, waiting for transfers between devices: 233 us -> 50.2 us  [same_core_exchange(): lax.all_to_all(array, 'expert', split_axis=0, concat_axis=0, tiled=True,...]
    ppermute x1 -> x33, waiting for transfers between devices: 13.7 us -> 139 us  [the longest x28 122 us: along_chips(): lax.ppermute(block, 'expert', [(i, (i + 2 * distance) % size) for i in ra...]
    ppermute x1 -> x33, starting transfers between devices: 0.63 us -> 73 us  [the longest x28 71.2 us: along_chips(): lax.ppermute(block, 'expert', [(i, (i + 2 * distance) % size) for i in ra...]
    reshape x21 -> x0, local copies, waits for them, and re-layouts: 50.7 us -> none  [the longest x1 9.17 us: sum_together(): jnp.pad(lines, ((0, 0), (0, rows * 128 - lines.shape[1]))).reshape(-1, 128)]
    reduce_scatter x1 -> x2, waiting for transfers between devices: 41.8 us -> 0.01 us  [the longest x1 0.01 us: per_device(): sum_outer = lax.psum_scatter(grad_outer, 'dp', tiled=True)]
    all_to_all x10 -> x4, starting transfers between devices: 53.4 us -> 20.9 us  [same_core_exchange(): lax.all_to_all(array, 'expert', split_axis=0, concat_axis=0, tiled=True,...]
    all_to_all x8 -> x0, other arithmetic: 25.3 us -> none  [the longest x6 15 us: side_by_side(): lax.all_to_all(both, axis, split_axis=split_dim, concat_axis=concat_dim,...]
    unnamed x79 -> x117, local copies, waits for them, and re-layouts: 60 us -> 41 us
  transfers between devices with their start and end apart: 16 -> 41, of which waited for: 12 -> 21; matrix products, arithmetic and copies ran while one was open for 29% -> 24% of each run, Pallas kernels for 0% -> 0%
where the time goes in v1:
time: 452 us; the launch traced here: 444 us
  waiting for transfers between devices  189 us (42%)
  starting transfers between devices  94.2 us (21%)
  local copies, waits for them, and re-layouts  61.7 us (14%)
  matrix products  43.7 us (10%)
  between operations  30.6 us (7%)
  other arithmetic  25.2 us (6%)
    ppermute x28, waiting for transfers between devices, along_chips(): lax.ppermute(block, 'expert', [(i, (i + 2 * distance) % size) for i in ra...  122 us
    ppermute x28, starting transfers between devices, along_chips(): lax.ppermute(block, 'expert', [(i, (i + 2 * distance) % size) for i in ra...  71.2 us
    all_to_all x4, waiting for transfers between devices, same_core_exchange(): lax.all_to_all(array, 'expert', split_axis=0, concat_axis=0, tiled=True,...  50.2 us
    unnamed x117, local copies, waits for them, and re-layouts  41 us
    dot_general x11, matrix products, contract(): lax.dot_general(left, right, (((left_dim,), (right_dim,)), ((), ())), pre...  36.8 us
    all_to_all x4, starting transfers between devices, same_core_exchange(): lax.all_to_all(array, 'expert', split_axis=0, concat_axis=0, tiled=True,...  20.9 us
  transfers between devices with their start and end apart: 41, of which 21 were waited for; matrix products, arithmetic and copies ran while one was open for 24% of the time, Pallas kernels for 0%

profile of v1, /device:TPU:14, one launch (start us, length us, event | category | flops | bytes accessed | tf_op | source)
XLA Modules:
  0.0 444.2 jit_solution(15708898486166967399)
XLA Ops:
  13.6 2.0 collective-permute-start
  15.6 3.3 collective-permute-start.1
  18.9 4.0 collective-permute-start.2
  23.4 4.9 %collective-permute-start.4 = (bf16[80,2048]{1,0:T(8,128)(2,1)S(1)}, bf16[80,2048]{1,0:T(8,128)(2,1)S(1)}, u32[]{:S(2)}, u32[]{:S(2)}) collective-permute-start(bf16[80,2048]{1,0:T(8,128)(2,1)S(1)} %get-tuple-element.19), channel_id=1, source_target_pairs={{0,40},{4,44},{8,48},{12,52},{16,56},{20,60},{24,0},{28,4},{32,8},... | collective-permute-start | bytes 983048 | tf_op jit(solution)/shard_map/ppermute | solution.py:37
  28.5 8.8 %collective-permute-start.5 = (bf16[80,2048]{1,0:T(8,128)(2,1)S(1)}, bf16[80,2048]{1,0:T(8,128)(2,1)S(1)}, u32[]{:S(2)}, u32[]{:S(2)}) collective-permute-start(bf16[80,2048]{1,0:T(8,128)(2,1)S(1)} %get-tuple-element.18), channel_id=1, source_target_pairs={{0,48},{4,52},{8,56},{12,60},{16,0},{20,4},{24,8},{28,12},{32,16},... | collective-permute-start | bytes 983048 | tf_op jit(solution)/shard_map/ppermute | solution.py:37
  37.3 7.9 %collective-permute-done.1 = bf16[80,2048]{1,0:T(8,128)(2,1)S(1)} collective-permute-done((bf16[80,2048]{1,0:T(8,128)(2,1)S(1)}, bf16[80,2048]{1,0:T(8,128)(2,1)S(1)}, u32[]{:S(2)}, u32[]{:S(2)}) %collective-permute-start.1) | collective-permute-done | bytes 327712 | tf_op jit(solution)/shard_map/ppermute | solution.py:37
  45.2 2.4 collective-permute-start.6
  47.6 22.2 %collective-permute-done.2 = bf16[80,2048]{1,0:T(8,128)(2,1)S(1)} collective-permute-done((bf16[80,2048]{1,0:T(8,128)(2,1)S(1)}, bf16[80,2048]{1,0:T(8,128)(2,1)S(1)}, u32[]{:S(2)}, u32[]{:S(2)}) %collective-permute-start.2) | collective-permute-done | bytes 327712 | tf_op jit(solution)/shard_map/ppermute | solution.py:37
  69.9 6.4 %collective-permute-done.5 = bf16[80,2048]{1,0:T(8,128)(2,1)S(1)} collective-permute-done((bf16[80,2048]{1,0:T(8,128)(2,1)S(1)}, bf16[80,2048]{1,0:T(8,128)(2,1)S(1)}, u32[]{:S(2)}, u32[]{:S(2)}) %collective-permute-start.5) | collective-permute-done | bytes 327712 | tf_op jit(solution)/shard_map/ppermute | solution.py:37
  76.3 4.9 %collective-permute-done.6 = bf16[80,2048]{1,0:T(8,128)(2,1)S(1)} collective-permute-done((bf16[80,2048]{1,0:T(8,128)(2,1)S(1)}, bf16[80,2048]{1,0:T(8,128)(2,1)S(1)}, u32[]{:S(2)}, u32[]{:S(2)}) %collective-permute-start.6) | collective-permute-done | bytes 327712 | tf_op jit(solution)/shard_map/ppermute | solution.py:37
  81.8 4.9 %collective-permute-done.7 = bf16[8,80,2048]{2,1,0:T(8,128)(2,1)S(1)} collective-permute-done((bf16[8,80,2048]{2,1,0:T(8,128)(2,1)S(1)}, bf16[8,80,2048]{2,1,0:T(8,128)(2,1)S(1)}, u32[]{:S(2)}, u32[]{:S(2)}) %collective-permute-start.7) | collective-permute-done | bytes 2621472 | tf_op jit(solution)/shard_map/ppermute | solution.py:41
  86.7 2.5 fusion
  89.2 3.9 fusion.13
  93.1 4.3 multiply_convert_fusion.3
  97.4 2.9 convolution_convert_fusion.3
  100.4 3.9 fusion.21
  104.3 1.8 convolution_convert_fusion.4
  106.1 1.8 convolution_convert_fusion.5
  107.9 2.0 pad_maximum_fusion
  110.0 3.0 convolution_convert_fusion.1
  128.2 1.9 copy.64
  136.7 3.3 add_convert_fusion.1
  146.3 5.5 %all-to-all-start.2 = ((bf16[8,3,48,512]{3,2,1,0:T(8,128)(2,1)}), bf16[8,3,48,512]{3,2,1,0:T(8,128)(2,1)}, u32[]{:S(2)}, u32[]{:S(2)}) async-start(bf16[8,3,48,512]{3,2,1,0:T(8,128)(2,1)} %copy.70), calls=%async_computation.4 | async-start | bytes 2359296 | tf_op jit(solution)/shard_map/all_to_all | solution.py:51
  151.8 2.4 fusion.113
  154.3 3.2 collective-permute-start.9
  158.8 2.4 collective-permute-start.10
  162.6 3.6 collective-permute-start.12
  166.9 18.1 %collective-permute-done.9 = bf16[40,2048]{1,0:T(8,128)(2,1)S(1)} collective-permute-done((bf16[40,2048]{1,0:T(8,128)(2,1)S(1)}, bf16[40,2048]{1,0:T(8,128)(2,1)S(1)}, u32[]{:S(2)}, u32[]{:S(2)}) %collective-permute-start.9) | collective-permute-done | bytes 163872 | tf_op jit(solution)/shard_map/ppermute | solution.py:37
  185.0 1.7 collective-permute-start.14
  194.7 2.6 collective-permute-start.15
  197.3 8.2 %all-to-all-start = ((bf16[8,3,2,64,384]{4,3,2,1,0:T(8,128)(2,1)}), bf16[8,3,2,64,384]{4,3,2,1,0:T(8,128)(2,1)S(1)}, u32[]{:S(2)}, u32[]{:S(2)}) async-start(bf16[8,3,2,64,384]{4,3,2,1,0:T(8,128)(2,1)} %copy.65), calls=%async_computation.2 | async-start | bytes 4718592 | tf_op jit(solution)/shard_map/all_to_all | solution.py:51
  215.4 2.8 fusion.50
  220.6 2.0 fusion.3
  223.3 8.5 %collective-permute-done.16 = bf16[128,2048]{1,0:T(8,128)(2,1)S(1)} collective-permute-done((bf16[128,2048]{1,0:T(8,128)(2,1)S(1)}, bf16[128,2048]{1,0:T(8,128)(2,1)S(1)}, u32[]{:S(2)}, u32[]{:S(2)}) %collective-permute-start.16) | collective-permute-done | bytes 524320 | tf_op jit(solution)/shard_map/ppermute | solution.py:187
  242.3 20.4 %all-to-all-done = bf16[8,3,2,64,384]{4,3,2,1,0:T(8,128)(2,1)S(1)} async-done(((bf16[8,3,2,64,384]{4,3,2,1,0:T(8,128)(2,1)}), bf16[8,3,2,64,384]{4,3,2,1,0:T(8,128)(2,1)S(1)}, u32[]{:S(2)}, u32[]{:S(2)}) %all-to-all-start) | async-done | bytes 2359328 | tf_op jit(solution)/shard_map/all_to_all | solution.py:51
  262.7 3.6 all-to-all-start.3
  266.3 2.3 slice_dynamic-update-slice_fusion.3
  268.6 1.9 collective-permute-start.17
  270.5 2.4 collective-permute-start.18
  272.9 2.7 collective-permute-start.19
  275.6 2.3 collective-permute-start.20
  277.9 2.7 collective-permute-start.21
  280.6 19.9 %collective-permute-done.17 = bf16[40,2048]{1,0:T(8,128)(2,1)S(1)} collective-permute-done((bf16[40,2048]{1,0:T(8,128)(2,1)S(1)}, bf16[40,2048]{1,0:T(8,128)(2,1)S(1)}, u32[]{:S(2)}, u32[]{:S(2)}) %collective-permute-start.17) | collective-permute-done | bytes 163872 | tf_op jit(solution)/shard_map/ppermute | solution.py:37
  300.5 1.8 collective-permute-start.22
  303.0 5.5 %collective-permute-done.18 = bf16[40,2048]{1,0:T(8,128)(2,1)S(1)} collective-permute-done((bf16[40,2048]{1,0:T(8,128)(2,1)S(1)}, bf16[40,2048]{1,0:T(8,128)(2,1)S(1)}, u32[]{:S(2)}, u32[]{:S(2)}) %collective-permute-start.18) | collective-permute-done | bytes 163872 | tf_op jit(solution)/shard_map/ppermute | solution.py:37
  310.5 7.9 %collective-permute-done.19 = bf16[40,2048]{1,0:T(8,128)(2,1)S(1)} collective-permute-done((bf16[40,2048]{1,0:T(8,128)(2,1)S(1)}, bf16[40,2048]{1,0:T(8,128)(2,1)S(1)}, u32[]{:S(2)}, u32[]{:S(2)}) %collective-permute-start.19) | collective-permute-done | bytes 163872 | tf_op jit(solution)/shard_map/ppermute | solution.py:37
  319.1 7.4 %collective-permute-done.20 = bf16[40,2048]{1,0:T(8,128)(2,1)S(1)} collective-permute-done((bf16[40,2048]{1,0:T(8,128)(2,1)S(1)}, bf16[40,2048]{1,0:T(8,128)(2,1)S(1)}, u32[]{:S(2)}, u32[]{:S(2)}) %collective-permute-start.20) | collective-permute-done | bytes 163872 | tf_op jit(solution)/shard_map/ppermute | solution.py:37
  333.2 3.6 all-to-all-start.1
  336.8 1.7 constant_dynamic-update-slice_fusion.9
  342.1 3.2 collective-permute-done.24
  346.6 4.7 %fusion.10 = f32[640,384]{1,0:T(8,128)} fusion(bf16[640,2048]{1,0:T(8,128)(2,1)} %constant_dynamic-update-slice_fusion.14, bf16[3,2048,384]{2,1,0:T(8,128)(2,1)} %all-gather.5.cloned.1.call-done), kind=kOutput, calls=%fused_computation.30 | convolution fusion | flops 1006632960 | bytes 5177344 | tf_op jit(solution)/shard_map/dot_general | solution.py:19
  351.2 7.4 %convolution_convert_fusion = bf16[640,2048]{1,0:T(8,128)(2,1)} fusion(bf16[3,2048,384]{2,1,0:T(8,128)(2,1)} %all-gather.5.cloned.1.call-done, f32[640,384]{1,0:T(8,128)} %fusion.10, bf16[640,2048]{1,0:T(8,128)(2,1)} %constant_dynamic-update-slice_fusion.14), kind=kOutput, calls=%fused_computation.2 | convolution fusion | flops 2016051200 | bytes 9371648 | tf_op jit(solution)/shard_map/dot_general | solution.py:19
  358.7 2.5 slice.332
  364.4 29.7 %all-to-all-done.1 = bf16[8,3,2,64,384]{4,3,2,1,0:T(8,128)(2,1)S(1)} async-done(((bf16[8,3,2,64,384]{4,3,2,1,0:T(8,128)(2,1)}), bf16[8,3,2,64,384]{4,3,2,1,0:T(8,128)(2,1)S(1)}, u32[]{:S(2)}, u32[]{:S(2)}) %all-to-all-start.1) | async-done | bytes 2359328 | tf_op jit(solution)/shard_map/all_to_all | solution.py:51
  396.4 1.8 add_convert_fusion
  400.7 3.6 collective-permute-start.28
  404.3 2.3 collective-permute-start.29
  406.6 2.5 collective-permute-start.30
  409.2 2.3 collective-permute-done.27
  411.5 5.1 %collective-permute-start.32 = (bf16[40,2048]{1,0:T(8,128)(2,1)S(1)}, bf16[40,2048]{1,0:T(8,128)(2,1)S(1)}, u32[]{:S(2)}, u32[]{:S(2)}) collective-permute-start(bf16[40,2048]{1,0:T(8,128)(2,1)S(1)} %get-tuple-element.31), channel_id=1, source_target_pairs={{0,8},{4,12},{8,16},{12,20},{16,24},{20,28},{24,32},{28,36},{32,40... | collective-permute-start | bytes 491528 | tf_op jit(solution)/shard_map/ppermute | solution.py:37
  416.6 5.8 %collective-permute-done.28 = bf16[40,2048]{1,0:T(8,128)(2,1)S(1)} collective-permute-done((bf16[40,2048]{1,0:T(8,128)(2,1)S(1)}, bf16[40,2048]{1,0:T(8,128)(2,1)S(1)}, u32[]{:S(2)}, u32[]{:S(2)}) %collective-permute-start.28) | collective-permute-done | bytes 163872 | tf_op jit(solution)/shard_map/ppermute | solution.py:37
  422.4 6.1 %collective-permute-done.30 = bf16[40,2048]{1,0:T(8,128)(2,1)S(1)} collective-permute-done((bf16[40,2048]{1,0:T(8,128)(2,1)S(1)}, bf16[40,2048]{1,0:T(8,128)(2,1)S(1)}, u32[]{:S(2)}, u32[]{:S(2)}) %collective-permute-start.30) | collective-permute-done | bytes 163872 | tf_op jit(solution)/shard_map/ppermute | solution.py:37
  428.6 3.2 collective-permute-done.31
  431.8 3.5 collective-permute-done.32
  (214 shorter events, 80.0 us)
Async XLA Ops:
  7.2 82.0 %all-gather.3.cloned.1.call-start = ((), (), s32[]{:S(2)}) async-start(), calls=%async_computation.6 | async-start | bytes 5898240 | tf_op jit(solution)/shard_map/all_gather | solution.py:123
  10.1 129.9 %reduce-scatter.5.cloned.1.call-start = ((), (), s32[]{:S(2)}) async-start(), calls=%async_computation.8 | async-start | bytes 1966080 | tf_op jit(solution)/shard_map/reduce_scatter | solution.py:195
  11.2 2.1 copy-start.20
  11.2 2.1 copy-start.22
  13.6 14.9 %collective-permute-start = (bf16[80,2048]{1,0:T(8,128)(2,1)S(1)}, bf16[80,2048]{1,0:T(8,128)(2,1)S(1)}, u32[]{:S(2)}, u32[]{:S(2)}) collective-permute-start(bf16[80,2048]{1,0:T(8,128)(2,1)S(1)} %get-tuple-element.23), channel_id=1, source_target_pairs={{0,8},{4,12},{8,16},{12,20},{16,24},{20,28},{24,32},{28,36},{32,40... | collective-permute-start | bytes 983048 | tf_op jit(solution)/shard_map/ppermute | solution.py:37
  15.6 29.6 %collective-permute-start.1 = (bf16[80,2048]{1,0:T(8,128)(2,1)S(1)}, bf16[80,2048]{1,0:T(8,128)(2,1)S(1)}, u32[]{:S(2)}, u32[]{:S(2)}) collective-permute-start(bf16[80,2048]{1,0:T(8,128)(2,1)S(1)} %get-tuple-element.22), channel_id=1, source_target_pairs={{0,16},{4,20},{8,24},{12,28},{16,32},{20,36},{24,40},{28,44},{32,4... | collective-permute-start | bytes 983048 | tf_op jit(solution)/shard_map/ppermute | solution.py:37
  18.9 50.9 %collective-permute-start.2 = (bf16[80,2048]{1,0:T(8,128)(2,1)S(1)}, bf16[80,2048]{1,0:T(8,128)(2,1)S(1)}, u32[]{:S(2)}, u32[]{:S(2)}) collective-permute-start(bf16[80,2048]{1,0:T(8,128)(2,1)S(1)} %get-tuple-element.21), channel_id=1, source_target_pairs={{0,24},{4,28},{8,32},{12,36},{16,40},{20,44},{24,48},{28,52},{32,5... | collective-permute-start | bytes 983048 | tf_op jit(solution)/shard_map/ppermute | solution.py:37
  22.9 46.9 %collective-permute-start.3 = (bf16[80,2048]{1,0:T(8,128)(2,1)S(1)}, bf16[80,2048]{1,0:T(8,128)(2,1)S(1)}, u32[]{:S(2)}, u32[]{:S(2)}) collective-permute-start(bf16[80,2048]{1,0:T(8,128)(2,1)S(1)} %get-tuple-element.20), channel_id=1, source_target_pairs={{0,32},{4,36},{8,40},{12,44},{16,48},{20,52},{24,56},{28,60},{32,0... | collective-permute-start | bytes 983048 | tf_op jit(solution)/shard_map/ppermute | solution.py:37
  23.4 46.4 %collective-permute-start.4 = (bf16[80,2048]{1,0:T(8,128)(2,1)S(1)}, bf16[80,2048]{1,0:T(8,128)(2,1)S(1)}, u32[]{:S(2)}, u32[]{:S(2)}) collective-permute-start(bf16[80,2048]{1,0:T(8,128)(2,1)S(1)} %get-tuple-element.19), channel_id=1, source_target_pairs={{0,40},{4,44},{8,48},{12,52},{16,56},{20,60},{24,0},{28,4},{32,8},... | collective-permute-start | bytes 983048 | tf_op jit(solution)/shard_map/ppermute | solution.py:37
  28.5 47.7 %collective-permute-start.5 = (bf16[80,2048]{1,0:T(8,128)(2,1)S(1)}, bf16[80,2048]{1,0:T(8,128)(2,1)S(1)}, u32[]{:S(2)}, u32[]{:S(2)}) collective-permute-start(bf16[80,2048]{1,0:T(8,128)(2,1)S(1)} %get-tuple-element.18), channel_id=1, source_target_pairs={{0,48},{4,52},{8,56},{12,60},{16,0},{20,4},{24,8},{28,12},{32,16},... | collective-permute-start | bytes 983048 | tf_op jit(solution)/shard_map/ppermute | solution.py:37
  45.2 36.0 %collective-permute-start.6 = (bf16[80,2048]{1,0:T(8,128)(2,1)S(1)}, bf16[80,2048]{1,0:T(8,128)(2,1)S(1)}, u32[]{:S(2)}, u32[]{:S(2)}) collective-permute-start(bf16[80,2048]{1,0:T(8,128)(2,1)S(1)} %get-tuple-element.17), channel_id=1, source_target_pairs={{0,56},{4,60},{8,0},{12,4},{16,8},{20,12},{24,16},{28,20},{32,24},... | collective-permute-start | bytes 983048 | tf_op jit(solution)/shard_map/ppermute | solution.py:37
  81.2 5.5 %collective-permute-start.7 = (bf16[8,80,2048]{2,1,0:T(8,128)(2,1)S(1)}, bf16[8,80,2048]{2,1,0:T(8,128)(2,1)S(1)}, u32[]{:S(2)}, u32[]{:S(2)}) collective-permute-start(bf16[8,80,2048]{2,1,0:T(8,128)(2,1)S(1)} %bitcast_dynamic-update-slice_fusion), channel_id=1, source_target_pairs={{0,4},{4,0},{8,12},{12,8},{16,20},{20,16},{24,28},{28,24},{32,36},... | collective-permute-start | bytes 7864328 | tf_op jit(solution)/shard_map/ppermute | solution.py:41
  89.2 3.9 copy-start.10
  93.1 4.3 copy-start.33
  93.1 4.3 copy-start.12
  100.3 87.1 %reduce-scatter.3.cloned.1.call-start = ((), (), s32[]{:S(2)}) async-start(), calls=%async_computation.7 | async-start | bytes 3932160 | tf_op jit(solution)/shard_map/reduce_scatter | solution.py:207
  100.4 3.9 copy-start.11
  100.4 3.9 copy-start.34
  114.4 20.9 %copy-start.7 = (bf16[1,1,2,512,384]{4,3,2,1,0:T(8,128)(2,1)S(1)}, bf16[1,1,2,512,384]{4,3,2,1,0:T(8,128)(2,1)}, u32[]{:S(2)}) copy-start(bf16[1,1,2,512,384]{4,3,2,1,0:T(8,128)(2,1)} %param.24) | copy-start | bytes 2359300
  115.6 21.1 %collective-permute-start.8 = (bf16[320,2048]{1,0:T(8,128)(2,1)}, bf16[320,2048]{1,0:T(8,128)(2,1)}, u32[]{:S(2)}, u32[]{:S(2)}) collective-permute-start(bf16[320,2048]{1,0:T(8,128)(2,1)} %slice.311), channel_id=1, source_target_pairs={{0,4},{4,0},{8,12},{12,8},{16,20},{20,16},{24,28},{28,24},{32,36},... | collective-permute-start | bytes 3932168 | tf_op jit(solution)/shard_map/ppermute | solution.py:41
  146.3 51.0 %all-to-all-start.2 = ((bf16[8,3,48,512]{3,2,1,0:T(8,128)(2,1)}), bf16[8,3,48,512]{3,2,1,0:T(8,128)(2,1)}, u32[]{:S(2)}, u32[]{:S(2)}) async-start(bf16[8,3,48,512]{3,2,1,0:T(8,128)(2,1)} %copy.70), calls=%async_computation.4 | async-start | bytes 2359296 | tf_op jit(solution)/shard_map/all_to_all | solution.py:51
  151.8 5.7 %copy-start.9 = (bf16[1,1,2,512,384]{4,3,2,1,0:T(8,128)(2,1)S(1)}, bf16[1,1,2,512,384]{4,3,2,1,0:T(8,128)(2,1)}, u32[]{:S(2)}) copy-start(bf16[1,1,2,512,384]{4,3,2,1,0:T(8,128)(2,1)} %param.26) | copy-start | bytes 2359300
  154.3 30.7 %collective-permute-start.9 = (bf16[40,2048]{1,0:T(8,128)(2,1)S(1)}, bf16[40,2048]{1,0:T(8,128)(2,1)S(1)}, u32[]{:S(2)}, u32[]{:S(2)}) collective-permute-start(bf16[40,2048]{1,0:T(8,128)(2,1)S(1)} %get-tuple-element.54), channel_id=1, source_target_pairs={{0,56},{4,60},{8,0},{12,4},{16,8},{20,12},{24,16},{28,20},{32,24},... | collective-permute-start | bytes 491528 | tf_op jit(solution)/shard_map/ppermute | solution.py:37
  158.8 29.8 %copy-start.8 = (bf16[1,1,2,512,384]{4,3,2,1,0:T(8,128)(2,1)S(1)}, bf16[1,1,2,512,384]{4,3,2,1,0:T(8,128)(2,1)}, u32[]{:S(2)}) copy-start(bf16[1,1,2,512,384]{4,3,2,1,0:T(8,128)(2,1)} %param.24) | copy-start | bytes 2359300
  158.8 35.9 %collective-permute-start.10 = (bf16[40,2048]{1,0:T(8,128)(2,1)}, bf16[40,2048]{1,0:T(8,128)(2,1)}, u32[]{:S(2)}, u32[]{:S(2)}) collective-permute-start(bf16[40,2048]{1,0:T(8,128)(2,1)} %get-tuple-element.53), channel_id=1, source_target_pairs={{0,48},{4,52},{8,56},{12,60},{16,0},{20,4},{24,8},{28,12},{32,16},... | collective-permute-start | bytes 491528 | tf_op jit(solution)/shard_map/ppermute | solution.py:37
  161.2 46.2 %collective-permute-start.11 = (bf16[40,2048]{1,0:T(8,128)(2,1)}, bf16[40,2048]{1,0:T(8,128)(2,1)}, u32[]{:S(2)}, u32[]{:S(2)}) collective-permute-start(bf16[40,2048]{1,0:T(8,128)(2,1)} %get-tuple-element.52), channel_id=1, source_target_pairs={{0,40},{4,44},{8,48},{12,52},{16,56},{20,60},{24,0},{28,4},{32,8},... | collective-permute-start | bytes 491528 | tf_op jit(solution)/shard_map/ppermute | solution.py:37
  162.6 46.3 %collective-permute-start.12 = (bf16[40,2048]{1,0:T(8,128)(2,1)}, bf16[40,2048]{1,0:T(8,128)(2,1)}, u32[]{:S(2)}, u32[]{:S(2)}) collective-permute-start(bf16[40,2048]{1,0:T(8,128)(2,1)} %get-tuple-element.51), channel_id=1, source_target_pairs={{0,32},{4,36},{8,40},{12,44},{16,48},{20,52},{24,56},{28,60},{32,0... | collective-permute-start | bytes 491528 | tf_op jit(solution)/shard_map/ppermute | solution.py:37
  166.2 44.4 %collective-permute-start.13 = (bf16[40,2048]{1,0:T(8,128)(2,1)}, bf16[40,2048]{1,0:T(8,128)(2,1)}, u32[]{:S(2)}, u32[]{:S(2)}) collective-permute-start(bf16[40,2048]{1,0:T(8,128)(2,1)} %get-tuple-element.50), channel_id=1, source_target_pairs={{0,24},{4,28},{8,32},{12,36},{16,40},{20,44},{24,48},{28,52},{32,5... | collective-permute-start | bytes 491528 | tf_op jit(solution)/shard_map/ppermute | solution.py:37
  185.0 27.1 %collective-permute-start.14 = (bf16[40,2048]{1,0:T(8,128)(2,1)}, bf16[40,2048]{1,0:T(8,128)(2,1)}, u32[]{:S(2)}, u32[]{:S(2)}) collective-permute-start(bf16[40,2048]{1,0:T(8,128)(2,1)} %get-tuple-element.49), channel_id=1, source_target_pairs={{0,16},{4,20},{8,24},{12,28},{16,32},{20,36},{24,40},{28,44},{32,4... | collective-permute-start | bytes 491528 | tf_op jit(solution)/shard_map/ppermute | solution.py:37
  194.7 19.0 %collective-permute-start.15 = (bf16[40,2048]{1,0:T(8,128)(2,1)}, bf16[40,2048]{1,0:T(8,128)(2,1)}, u32[]{:S(2)}, u32[]{:S(2)}) collective-permute-start(bf16[40,2048]{1,0:T(8,128)(2,1)} %get-tuple-element.48), channel_id=1, source_target_pairs={{0,8},{4,12},{8,16},{12,20},{16,24},{20,28},{24,32},{28,36},{32,40... | collective-permute-start | bytes 491528 | tf_op jit(solution)/shard_map/ppermute | solution.py:37
  197.3 65.4 %all-to-all-start = ((bf16[8,3,2,64,384]{4,3,2,1,0:T(8,128)(2,1)}), bf16[8,3,2,64,384]{4,3,2,1,0:T(8,128)(2,1)S(1)}, u32[]{:S(2)}, u32[]{:S(2)}) async-start(bf16[8,3,2,64,384]{4,3,2,1,0:T(8,128)(2,1)} %copy.65), calls=%async_computation.2 | async-start | bytes 4718592 | tf_op jit(solution)/shard_map/all_to_all | solution.py:51
  205.5 141.1 %all-gather.5.cloned.1.call-start = ((), (), s32[]{:S(2)}) async-start(), calls=%async_computation.9 | async-start | bytes 5898240 | tf_op jit(solution)/shard_map/all_gather | solution.py:123
  205.7 9.7 %copy-start.18 = (s32[128]{0:T(128)S(1)}, s32[128]{0:T(128)}, u32[]{:S(2)}) copy-start(s32[128]{0:T(128)} %get-tuple-element.11) | copy-start | bytes 1540
  205.7 9.7 %copy-start.19 = (s32[128]{0:T(128)S(1)}, s32[128]{0:T(128)}, u32[]{:S(2)}) copy-start(s32[128]{0:T(128)} %get-tuple-element.95) | copy-start | bytes 1540
  205.7 9.6 %copy-start.21 = (f32[128]{0:T(128)S(1)}, f32[128]{0:T(128)}, u32[]{:S(2)}) copy-start(f32[128]{0:T(128)} %copy-done.20) | copy-start | bytes 1540
  205.8 9.6 %copy-start.23 = (f32[128]{0:T(128)S(1)}, f32[128]{0:T(128)}, u32[]{:S(2)}) copy-start(f32[128]{0:T(128)} %copy-done.22) | copy-start | bytes 1540
  220.6 2.5 copy-start.24
  222.6 9.3 %collective-permute-start.16 = (bf16[128,2048]{1,0:T(8,128)(2,1)S(1)}, bf16[128,2048]{1,0:T(8,128)(2,1)S(1)}, u32[]{:S(2)}, u32[]{:S(2)}) collective-permute-start(bf16[128,2048]{1,0:T(8,128)(2,1)S(1)} %fusion.3), channel_id=1, source_target_pairs={{0,64},{64,128},{128,192},{192,0},{1,65},{65,129},{129,193},{193,1... | collective-permute-start | bytes 1572872 | tf_op jit(solution)/shard_map/ppermute | solution.py:187
  231.8 4.7 %copy-start.4 = (bf16[128,2048]{1,0:T(8,128)(2,1)}, bf16[128,2048]{1,0:T(8,128)(2,1)S(1)}, u32[]{:S(2)}) copy-start(bf16[128,2048]{1,0:T(8,128)(2,1)S(1)} %collective-permute-done.16) | copy-start | bytes 1572868
  262.7 70.5 %all-to-all-start.3 = ((bf16[8,3,48,512]{3,2,1,0:T(8,128)(2,1)}), bf16[8,3,48,512]{3,2,1,0:T(8,128)(2,1)S(1)}, u32[]{:S(2)}, u32[]{:S(2)}) async-start(bf16[8,3,48,512]{3,2,1,0:T(8,128)(2,1)} %copy-done.15), calls=%async_computation.5 | async-start | bytes 2359296 | tf_op jit(solution)/shard_map/all_to_all | solution.py:51
  268.6 31.9 %collective-permute-start.17 = (bf16[40,2048]{1,0:T(8,128)(2,1)S(1)}, bf16[40,2048]{1,0:T(8,128)(2,1)S(1)}, u32[]{:S(2)}, u32[]{:S(2)}) collective-permute-start(bf16[40,2048]{1,0:T(8,128)(2,1)S(1)} %get-tuple-element.47), channel_id=1, source_target_pairs={{0,8},{4,12},{8,16},{12,20},{16,24},{20,28},{24,32},{28,36},{32,40... | collective-permute-start | bytes 491528 | tf_op jit(solution)/shard_map/ppermute | solution.py:37
  270.5 38.0 %collective-permute-start.18 = (bf16[40,2048]{1,0:T(8,128)(2,1)S(1)}, bf16[40,2048]{1,0:T(8,128)(2,1)S(1)}, u32[]{:S(2)}, u32[]{:S(2)}) collective-permute-start(bf16[40,2048]{1,0:T(8,128)(2,1)S(1)} %get-tuple-element.46), channel_id=1, source_target_pairs={{0,16},{4,20},{8,24},{12,28},{16,32},{20,36},{24,40},{28,44},{32,4... | collective-permute-start | bytes 491528 | tf_op jit(solution)/shard_map/ppermute | solution.py:37
  272.9 45.5 %collective-permute-start.19 = (bf16[40,2048]{1,0:T(8,128)(2,1)S(1)}, bf16[40,2048]{1,0:T(8,128)(2,1)S(1)}, u32[]{:S(2)}, u32[]{:S(2)}) collective-permute-start(bf16[40,2048]{1,0:T(8,128)(2,1)S(1)} %get-tuple-element.45), channel_id=1, source_target_pairs={{0,24},{4,28},{8,32},{12,36},{16,40},{20,44},{24,48},{28,52},{32,5... | collective-permute-start | bytes 491528 | tf_op jit(solution)/shard_map/ppermute | solution.py:37
  275.6 50.8 %collective-permute-start.20 = (bf16[40,2048]{1,0:T(8,128)(2,1)S(1)}, bf16[40,2048]{1,0:T(8,128)(2,1)S(1)}, u32[]{:S(2)}, u32[]{:S(2)}) collective-permute-start(bf16[40,2048]{1,0:T(8,128)(2,1)S(1)} %get-tuple-element.44), channel_id=1, source_target_pairs={{0,32},{4,36},{8,40},{12,44},{16,48},{20,52},{24,56},{28,60},{32,0... | collective-permute-start | bytes 491528 | tf_op jit(solution)/shard_map/ppermute | solution.py:37
  277.9 58.9 %collective-permute-start.21 = (bf16[40,2048]{1,0:T(8,128)(2,1)}, bf16[40,2048]{1,0:T(8,128)(2,1)}, u32[]{:S(2)}, u32[]{:S(2)}) collective-permute-start(bf16[40,2048]{1,0:T(8,128)(2,1)} %get-tuple-element.43), channel_id=1, source_target_pairs={{0,40},{4,44},{8,48},{12,52},{16,56},{20,60},{24,0},{28,4},{32,8},... | collective-permute-start | bytes 491528 | tf_op jit(solution)/shard_map/ppermute | solution.py:37
  300.5 38.0 %collective-permute-start.22 = (bf16[40,2048]{1,0:T(8,128)(2,1)}, bf16[40,2048]{1,0:T(8,128)(2,1)}, u32[]{:S(2)}, u32[]{:S(2)}) collective-permute-start(bf16[40,2048]{1,0:T(8,128)(2,1)} %get-tuple-element.42), channel_id=1, source_target_pairs={{0,48},{4,52},{8,56},{12,60},{16,0},{20,4},{24,8},{28,12},{32,16},... | collective-permute-start | bytes 491528 | tf_op jit(solution)/shard_map/ppermute | solution.py:37
  308.5 31.6 %collective-permute-start.23 = (bf16[40,2048]{1,0:T(8,128)(2,1)}, bf16[40,2048]{1,0:T(8,128)(2,1)}, u32[]{:S(2)}, u32[]{:S(2)}) collective-permute-start(bf16[40,2048]{1,0:T(8,128)(2,1)} %get-tuple-element.41), channel_id=1, source_target_pairs={{0,56},{4,60},{8,0},{12,4},{16,8},{20,12},{24,16},{28,20},{32,24},... | collective-permute-start | bytes 491528 | tf_op jit(solution)/shard_map/ppermute | solution.py:37
  327.1 4.6 %copy-start.17 = (bf16[320,2048]{1,0:T(8,128)(2,1)}, bf16[320,2048]{1,0:T(8,128)(2,1)S(1)}, u32[]{:S(2)}) copy-start(bf16[320,2048]{1,0:T(8,128)(2,1)S(1)} %get-tuple-element.67) | copy-start | bytes 3932164
  333.2 60.9 %all-to-all-start.1 = ((bf16[8,3,2,64,384]{4,3,2,1,0:T(8,128)(2,1)}), bf16[8,3,2,64,384]{4,3,2,1,0:T(8,128)(2,1)S(1)}, u32[]{:S(2)}, u32[]{:S(2)}) async-start(bf16[8,3,2,64,384]{4,3,2,1,0:T(8,128)(2,1)} %dynamic-slice_dynamic-update-slice_fusion), calls=%async_computation.3 | async-start | bytes 4718592 | tf_op jit(solution)/shard_map/all_to_all | solution.py:51
  341.8 3.5 collective-permute-start.24
  358.7 2.7 copy-start.30
  361.2 35.1 %collective-permute-start.25 = (bf16[320,2048]{1,0:T(8,128)(2,1)}, bf16[320,2048]{1,0:T(8,128)(2,1)}, u32[]{:S(2)}, u32[]{:S(2)}) collective-permute-start(bf16[320,2048]{1,0:T(8,128)(2,1)} %slice.332), channel_id=1, source_target_pairs={{0,4},{4,0},{8,12},{12,8},{16,20},{20,16},{24,28},{28,24},{32,36},... | collective-permute-start | bytes 3932168 | tf_op jit(solution)/shard_map/ppermute | solution.py:41
  394.4 2.0 copy-start.14
  398.3 10.7 %collective-permute-start.26 = (bf16[40,2048]{1,0:T(8,128)(2,1)S(1)}, bf16[40,2048]{1,0:T(8,128)(2,1)S(1)}, u32[]{:S(2)}, u32[]{:S(2)}) collective-permute-start(bf16[40,2048]{1,0:T(8,128)(2,1)S(1)} %get-tuple-element.37), channel_id=1, source_target_pairs={{0,56},{4,60},{8,0},{12,4},{16,8},{20,12},{24,16},{28,20},{32,24},... | collective-permute-start | bytes 491528 | tf_op jit(solution)/shard_map/ppermute | solution.py:37
  399.7 35.6 %copy-start.27 = (f32[128]{0:T(128)S(1)}, f32[128]{0:T(128)}, u32[]{:S(2)}) copy-start(f32[128]{0:T(128)} %get-tuple-element.79) | copy-start | bytes 1540
  399.7 35.7 %copy-start.28 = (f32[128]{0:T(128)S(1)}, f32[128]{0:T(128)}, u32[]{:S(2)}) copy-start(f32[128]{0:T(128)} %get-tuple-element.80) | copy-start | bytes 1540
  399.7 11.8 %collective-permute-start.27 = (bf16[40,2048]{1,0:T(8,128)(2,1)S(1)}, bf16[40,2048]{1,0:T(8,128)(2,1)S(1)}, u32[]{:S(2)}, u32[]{:S(2)}) collective-permute-start(bf16[40,2048]{1,0:T(8,128)(2,1)S(1)} %get-tuple-element.36), channel_id=1, source_target_pairs={{0,48},{4,52},{8,56},{12,60},{16,0},{20,4},{24,8},{28,12},{32,16},... | collective-permute-start | bytes 491528 | tf_op jit(solution)/shard_map/ppermute | solution.py:37
  400.7 21.6 %collective-permute-start.28 = (bf16[40,2048]{1,0:T(8,128)(2,1)S(1)}, bf16[40,2048]{1,0:T(8,128)(2,1)S(1)}, u32[]{:S(2)}, u32[]{:S(2)}) collective-permute-start(bf16[40,2048]{1,0:T(8,128)(2,1)S(1)} %get-tuple-element.35), channel_id=1, source_target_pairs={{0,40},{4,44},{8,48},{12,52},{16,56},{20,60},{24,0},{28,4},{32,8},... | collective-permute-start | bytes 491528 | tf_op jit(solution)/shard_map/ppermute | solution.py:37
  404.3 18.1 %collective-permute-start.29 = (bf16[40,2048]{1,0:T(8,128)(2,1)S(1)}, bf16[40,2048]{1,0:T(8,128)(2,1)S(1)}, u32[]{:S(2)}, u32[]{:S(2)}) collective-permute-start(bf16[40,2048]{1,0:T(8,128)(2,1)S(1)} %get-tuple-element.34), channel_id=1, source_target_pairs={{0,32},{4,36},{8,40},{12,44},{16,48},{20,52},{24,56},{28,60},{32,0... | collective-permute-start | bytes 491528 | tf_op jit(solution)/shard_map/ppermute | solution.py:37
  406.6 22.0 %collective-permute-start.30 = (bf16[40,2048]{1,0:T(8,128)(2,1)S(1)}, bf16[40,2048]{1,0:T(8,128)(2,1)S(1)}, u32[]{:S(2)}, u32[]{:S(2)}) collective-permute-start(bf16[40,2048]{1,0:T(8,128)(2,1)S(1)} %get-tuple-element.33), channel_id=1, source_target_pairs={{0,24},{4,28},{8,32},{12,36},{16,40},{20,44},{24,48},{28,52},{32,5... | collective-permute-start | bytes 491528 | tf_op jit(solution)/shard_map/ppermute | solution.py:37
  409.1 22.7 %collective-permute-start.31 = (bf16[40,2048]{1,0:T(8,128)(2,1)S(1)}, bf16[40,2048]{1,0:T(8,128)(2,1)S(1)}, u32[]{:S(2)}, u32[]{:S(2)}) collective-permute-start(bf16[40,2048]{1,0:T(8,128)(2,1)S(1)} %get-tuple-element.32), channel_id=1, source_target_pairs={{0,16},{4,20},{8,24},{12,28},{16,32},{20,36},{24,40},{28,44},{32,4... | collective-permute-start | bytes 491528 | tf_op jit(solution)/shard_map/ppermute | solution.py:37
  411.5 23.8 %collective-permute-start.32 = (bf16[40,2048]{1,0:T(8,128)(2,1)S(1)}, bf16[40,2048]{1,0:T(8,128)(2,1)S(1)}, u32[]{:S(2)}, u32[]{:S(2)}) collective-permute-start(bf16[40,2048]{1,0:T(8,128)(2,1)S(1)} %get-tuple-element.31), channel_id=1, source_target_pairs={{0,8},{4,12},{8,16},{12,20},{16,24},{20,28},{24,32},{28,36},{32,40... | collective-permute-start | bytes 491528 | tf_op jit(solution)/shard_map/ppermute | solution.py:37
  428.6 7.3 %copy-start.5 = (bf16[128,2048]{1,0:T(8,128)(2,1)S(1)}, bf16[128,2048]{1,0:T(8,128)(2,1)}, u32[]{:S(2)}) copy-start(bf16[128,2048]{1,0:T(8,128)(2,1)} %copy-done.4) | copy-start | bytes 1572868
  428.6 7.3 %copy-start.26 = (f32[128]{0:T(128)S(1)}, f32[128]{0:T(128)}, u32[]{:S(2)}) copy-start(f32[128]{0:T(128)} %get-tuple-element.76) | copy-start | bytes 1540
  (13 other events, 18.7 us)
Sparse Core Ops, SparseCore 0:
  10.4 57.4 all-gather.2
  100.5 26.6 reduce-scatter.4
  129.7 40.6 reduce-scatter.2
  219.5 56.1 all-gather.4

commit v2 on v1

--- a/solution.py
+++ b/solution.py
@@ -1,6 +1,8 @@
 import jax
 import jax.numpy as jnp
 from jax import lax
+from jax.experimental import pallas as pl
+from jax.experimental.pallas import tpu as pltpu
 from jax.sharding import PartitionSpec as P
 
 norm_eps = 1e-06
@@ -42,7 +44,12 @@
 
 
 def send_blocks(blocks, sign):
-    return [blocks[0]] + [along_chips(b, sign * k) for k, b in enumerate(blocks) if k]
+    count = len(blocks)
+    moved = {0: blocks[0]}
+    for near in range(1, count // 2 + 1):
+        for k in sorted({near, count - near}):
+            moved[k] = along_chips(blocks[k], sign * k)
+    return [moved[k] for k in range(count)]
 
 
 def same_core_exchange(array):
@@ -92,14 +99,27 @@
     return (half_out, activity, gate_proj, up_proj)
 
 
-def send_back(half_out, blocks):
+def in_blocks(array, count):
+    rows = array.shape[0] // count
+    return [array[k * rows : (k + 1) * rows] for k in range(count)]
+
+
+def in_step(arrays, blocks, names):
+    tied = lax.optimization_barrier((*arrays, *[blocks[k] for k in names]))
+    for k, block in zip(names, tied[len(arrays) :]):
+        blocks[k] = block
+    return tied[: len(arrays)]
+
+
+def both_cores(blocks):
+    own = jnp.concatenate(blocks, axis=0)
+    return jnp.concatenate([own, from_sibling(own)], axis=0)
+
+
+def merged_halves(half_out):
     here = half_out.shape[0] // 2
     other = from_sibling(half_out[here:])
-    total = (half_out[:here].astype(F32) + other.astype(F32)).astype(BF16)
-    rows = here // blocks
-    return jnp.concatenate(
-        send_blocks([total[k * rows : (k + 1) * rows] for k in range(blocks)], -1), axis=0
-    )
+    return (half_out[:here].astype(F32) + other.astype(F32)).astype(BF16)
 
 
 def combine(token_rows, hits, gates, returned):
@@ -110,6 +130,7 @@
 
 
 def adam_step(weight, mean, square, grads):
+    grads = grads.astype(F32)
     mean_new = (beta_one * mean.astype(F32) + (1.0 - beta_one) * grads).astype(BF16)
     square_new = (beta_two * square.astype(F32) + (1.0 - beta_two) * grads * grads).astype(BF16)
     mean_wide = lax.optimization_barrier(mean_new).astype(F32)
@@ -118,18 +139,53 @@
     return ((weight - learn_rate * update).astype(BF16), mean_new, square_new)
 
 
-def full_weights(inner_low, outer_low):
-    both = jnp.concatenate([inner_low, outer_low.T[None]], axis=0)
-    return lax.all_gather(both, "dp", axis=1, tiled=True)
-
-
-def relocate(spread, inverse):
-    arrived = same_core_exchange(spread)
-    ordered = jnp.concatenate(
-        [lax.dynamic_slice_in_dim(arrived, inverse[i], 1, 0) for i in range(inverse.shape[0])],
-        axis=0,
-    )
-    return same_core_exchange(ordered)
+def side_by_side(inner, outer):
+    return jnp.concatenate([inner, outer.T[None]], axis=0)
+
+
+def in_eighths(array, count):
+    kinds, deep, hidden = array.shape
+    pieces = array.reshape(kinds, count, deep // count, hidden).transpose(1, 0, 2, 3)
+    return pieces.reshape(count, kinds * (deep // count), hidden)
+
+
+def from_eighths(pieces, kinds):
+    count, rows, hidden = pieces.shape
+    array = pieces.reshape(count, kinds, rows // kinds, hidden).transpose(1, 0, 2, 3)
+    return array.reshape(kinds, count * (rows // kinds), hidden)
+
+
+def full_weights(low):
+    return lax.all_gather(low, "dp", axis=1, tiled=True)
+
+
+def order_kernel(order_ref, inner_ref, outer_ref, out_ref):
+    deep = inner_ref.shape[2]
+    out_ref[:, :, :deep] = inner_ref[...]
+    out_ref[:, :, deep:] = outer_ref[...]
+
+
+def in_order(inner, outer, order):
+    count, items, deep, hidden = inner.shape
+    rows = deep + outer.shape[2]
+
+    def block(rows):
+        return pl.BlockSpec((1, items, rows, hidden), lambda i, order: (order[i], 0, 0, 0))
+
+    return pl.pallas_call(
+        order_kernel,
+        grid_spec=pltpu.PrefetchScalarGridSpec(
+            num_scalar_prefetch=1,
+            grid=(count,),
+            in_specs=[block(deep), block(rows - deep)],
+            out_specs=pl.BlockSpec((1, items, rows, hidden), lambda i, order: (i, 0, 0, 0)),
+        ),
+        out_shape=jax.ShapeDtypeStruct((count, items, rows, hidden), inner.dtype),
+        cost_estimate=pl.CostEstimate(
+            flops=0, bytes_accessed=4 * count * items * rows * hidden, transcendentals=0
+        ),
+        name="in_order",
+    )(order, inner, outer)
 
 
 def per_device(
@@ -159,15 +215,21 @@
     x, cot = tokens[0], cotangent[0]
     w_in, w_out = inner_weight[0, 0], outer_weight[0, 0]
 
-    full = full_weights(w_in.astype(BF16), w_out.astype(BF16))
+    hidden = w_out.shape[0]
+    parts = lax.axis_size("dp")
+    weight = side_by_side(w_in, w_out)
+    mean = side_by_side(inner_mean[0, 0], outer_mean[0, 0])
+    square = side_by_side(inner_square[0, 0], outer_square[0, 0])
+    kinds = weight.shape[0]
+
+    full = full_weights(weight.astype(BF16))
 
     slots = route(first_ids[0], chip, experts, rows)
     gates = first_gates[0]
     high, low = two_parts(gates)
-    one = jnp.ones_like(gates)
     picker = jnp.concatenate(
         [
-            weighted(spots(slots, 2 * rows, 2 * total), one),
+            weighted(spots(slots, 2 * rows, 2 * total), jnp.ones_like(gates)),
             weighted(spots(slots, 2 * rows, 2 * total, rows), high),
             weighted(spots(slots, 2 * rows, 2 * total, rows), low),
         ],
@@ -175,22 +237,18 @@
     )
     sources = jnp.concatenate([normed(x, gain_row), cot, cot], axis=0)
     packed = contract(picker, sources, 0, 0).astype(BF16)
-    sent = send_blocks([packed[2 * k * rows : 2 * (k + 1) * rows] for k in range(experts)], 1)
-    own = jnp.stack(sent)
+    own = jnp.stack(send_blocks(in_blocks(packed, experts), 1))
+
     both = jnp.stack([own, from_sibling(own)])
     arrived = both[:, :, :rows].reshape(2 * total, width)
     grad_rows = both[:, :, rows:].reshape(2 * total, width)
-
     half_out, activity, gate_proj, up_proj = expert_forward(arrived, full)
+
+    leaving = in_blocks(merged_halves(half_out), experts)
+    grad_rows, at_home = lax.optimization_barrier((grad_rows, leaving[0]))
+    returned = send_blocks(leaving, -1)
+    returned[0] = at_home
     hits = spots(slots, rows, total)
-    first_out = combine(x, hits, gates, send_back(half_out, experts))
-    second_in = lax.ppermute(
-        first_out,
-        "pipe",
-        [(i, (i + 1) % lax.axis_size("pipe")) for i in range(lax.axis_size("pipe"))],
-    )
-
-    parts = lax.axis_size("dp")
     grad_outer = contract(grad_rows, activity, 0, 0).astype(BF16)
     sum_outer = lax.psum_scatter(grad_outer, "dp", tiled=True)
     d_active = contract(grad_rows, full[2], 1, 0)
@@ -205,53 +263,54 @@
         axis=1,
     )
     sum_inner = lax.psum_scatter(grad_inner.reshape(2 * width, -1), "dp", tiled=True)
-
-    new_outer = adam_step(w_out, outer_mean[0, 0], outer_square[0, 0], sum_outer.astype(F32).T)
-    new_inner = adam_step(
-        w_in, inner_mean[0, 0], inner_square[0, 0], sum_inner.astype(F32).reshape(w_in.shape)
-    )
-
-    places = jnp.arange(experts, dtype=jnp.int32)
-    inverse = jnp.sum(
-        jnp.where(new_slot[0][:, None] == places[None, :], places[:, None], 0), axis=0
-    )
-    hidden = w_out.shape[0]
-    deep = w_in.shape[1]
-    spread_outer = jnp.stack([a.reshape(experts, hidden // experts, -1) for a in new_outer], axis=1)
-    moved_outer = relocate(spread_outer, inverse)
-    spread_inner = jnp.stack(
-        [
-            a.reshape(2, experts, deep // experts, hidden).transpose(1, 0, 2, 3)
-            for a in new_inner
-        ],
-        axis=1,
-    )
-    moved_inner = relocate(spread_inner, inverse)
-    outs_outer = [moved_outer[:, i].reshape(outer_mean.shape) for i in range(3)]
-    outs_inner = [
-        moved_inner[:, i].transpose(1, 0, 2, 3).reshape(inner_mean.shape) for i in range(3)
-    ]
-
-    full_two = full_weights(new_inner[0], new_outer[0])
+    hits = spots(slots, rows, total)
+    first_out = combine(x, hits, gates, jnp.concatenate(returned, axis=0))
+    second_in = lax.ppermute(
+        first_out,
+        "pipe",
+        [(i, (i + 1) % lax.axis_size("pipe")) for i in range(lax.axis_size("pipe"))],
+    )
+
+    old = (weight, mean, square)
+    new_outer = adam_step(*[a[2:] for a in old], sum_outer[None])
+    outer_pieces = same_core_exchange(
+        jnp.stack([in_eighths(a, experts) for a in new_outer], axis=1)
+    )
+    sum_inner, outer_pieces, second_rest = lax.optimization_barrier(
+        (sum_inner, outer_pieces, second_in)
+    )
+    new_inner = adam_step(*[a[:2] for a in old], sum_inner.reshape(2, width // parts, hidden))
+    inner_pieces = same_core_exchange(
+        jnp.stack([in_eighths(a, experts) for a in new_inner], axis=1)
+    )
+    full_two = full_weights(jnp.concatenate([new_inner[0], new_outer[0]], axis=0))
+
     slots_two = route(second_ids[0], chip, experts, rows)
     hits_two = spots(slots_two, rows, total)
     picker_two = weighted(hits_two, jnp.ones_like(second_gates[0]))
     packed_two = contract(picker_two, normed(second_in, gain_row), 0, 0).astype(BF16)
-    own_two = jnp.concatenate(
-        send_blocks([packed_two[k * rows : (k + 1) * rows] for k in range(experts)], 1), axis=0
-    )
-    rows_two = jnp.concatenate([own_two, from_sibling(own_two)], axis=0)
-    half_two = expert_forward(rows_two, full_two)[0]
-    second_out = combine(second_in, hits_two, second_gates[0], send_back(half_two, experts))
-    return (
-        second_out[None],
-        outs_inner[0].astype(F32),
-        outs_outer[0].astype(F32),
-        outs_inner[1],
-        outs_outer[1],
-        outs_inner[2],
-        outs_outer[2],
-    )
+    own_two = send_blocks(in_blocks(packed_two, experts), 1)
+
+    places = jnp.arange(experts, dtype=jnp.int32)
+    inverse = jnp.sum(
+        jnp.where(new_slot[0][:, None] == places[None, :], places[:, None], 0), axis=0
+    )
+    ordered = in_order(inner_pieces, outer_pieces, inverse)
+    (ordered,) = in_step([ordered], own_two, range(1, experts))
+    moved = same_core_exchange(ordered)
+
+    half_two = expert_forward(both_cores(own_two), full_two)[0]
+    leaving_two = in_blocks(merged_halves(half_two), experts)
+    returned_two = send_blocks(leaving_two, -1)
+    (moved,) = in_step([moved], returned_two, (1, 2, experts - 2, experts - 1))
+    second_out = combine(
+        second_rest, hits_two, second_gates[0], jnp.concatenate(returned_two, axis=0)
+    )
+    outs = []
+    for item in range(moved.shape[1]):
+        array = from_eighths(moved[:, item], kinds)
+        outs += [array[:-1].reshape(inner_mean.shape), array[-1].T.reshape(outer_mean.shape)]
+    return (second_out[None], outs[0].astype(F32), outs[1].astype(F32), *outs[2:])
 
 
 def solution(mesh):

time: 452 us -> 424 us (0.938)
  between operations: 30.6 us -> 14.9 us
  local copies, waits for them, and re-layouts: 61.7 us -> 46.3 us
  Pallas kernels: 0 us -> 7 us
  waiting for transfers between devices: 189 us -> 183 us
    all_to_all x4 -> x3, waiting for transfers between devices: 50.2 us -> 7.68 us  [same_core_exchange(): lax.all_to_all(array, 'expert', split_axis=0, concat_axis=0, tiled=True,...]
    ppermute x28, waiting for transfers between devices: 122 us -> 153 us  [along_chips(): lax.ppermute(block, 'expert', [(i, (i + 2 * distance) % size) for i in ra...]
    unnamed x117 -> x143, local copies, waits for them, and re-layouts: 41 us -> 33.8 us
    pallas_call x0 -> x1, Pallas kernels: none -> 7 us  [in_order(): pl.pallas_call(order_kernel, grid_spec=pltpu.PrefetchScalarGridSpec(num_s...]
    ppermute x28, starting transfers between devices: 71.2 us -> 76.3 us  [along_chips(): lax.ppermute(block, 'expert', [(i, (i + 2 * distance) % size) for i in ra...]
    convert_element_type x6 -> x5, other arithmetic: 8.74 us -> 4.06 us  [the longest x1 1.71 us: adam_step(): grads = grads.astype(F32)]
    ppermute x4, waiting for transfers between devices: 8.12 us -> 12.7 us  [from_sibling(): lax.ppermute(block, 'expert', [(i, i ^ 1) for i in range(lax.axis_size('e...]
    all_to_all x4 -> x3, starting transfers between devices: 20.9 us -> 19.7 us  [same_core_exchange(): lax.all_to_all(array, 'expert', split_axis=0, concat_axis=0, tiled=True,...]
  transfers between devices with their start and end apart: 41 -> 40, of which waited for: 21 -> 19; matrix products, arithmetic and copies ran while one was open for 24% -> 19% of each run, Pallas kernels for 0% -> 2%
where the time goes in v2:
time: 424 us; the launch traced here: 416 us
  waiting for transfers between devices  183 us (43%)
  starting transfers between devices  97.5 us (23%)
  local copies, waits for them, and re-layouts  46.3 us (11%)
  matrix products  40.5 us (10%)
  other arithmetic  26.4 us (6%)
  between operations  14.9 us (4%)
  Pallas kernels  7 us (2%)
    ppermute x28, waiting for transfers between devices, along_chips(): lax.ppermute(block, 'expert', [(i, (i + 2 * distance) % size) for i in ra...  153 us
    ppermute x28, starting transfers between devices, along_chips(): lax.ppermute(block, 'expert', [(i, (i + 2 * distance) % size) for i in ra...  76.3 us
    unnamed x143, local copies, waits for them, and re-layouts  33.8 us
    dot_general x11, matrix products, contract(): lax.dot_general(left, right, (((left_dim,), (right_dim,)), ((), ())), pre...  33.6 us
    all_to_all x3, starting transfers between devices, same_core_exchange(): lax.all_to_all(array, 'expert', split_axis=0, concat_axis=0, tiled=True,...  19.7 us
    ppermute x4, waiting for transfers between devices, from_sibling(): lax.ppermute(block, 'expert', [(i, i ^ 1) for i in range(lax.axis_size('e...  12.7 us
    ppermute x1, waiting for transfers between devices, per_device(): lax.ppermute(first_out, 'pipe', [(i, (i + 1) % lax.axis_size('pipe')) for...  9.86 us
  transfers between devices with their start and end apart: 40, of which 19 were waited for; matrix products, arithmetic and copies ran while one was open for 19% of the time, Pallas kernels for 2%

profile of v2, /device:TPU:14, one launch (start us, length us, event | category | flops | bytes accessed | tf_op | source)
XLA Modules:
  0.0 415.9 jit_solution(11406615248866903929)
XLA Ops:
  13.6 2.0 collective-permute-start
  15.6 3.3 collective-permute-start.1
  18.9 4.0 collective-permute-start.2
  23.5 4.9 %collective-permute-start.4 = (bf16[80,2048]{1,0:T(8,128)(2,1)S(1)}, bf16[80,2048]{1,0:T(8,128)(2,1)S(1)}, u32[]{:S(2)}, u32[]{:S(2)}) collective-permute-start(bf16[80,2048]{1,0:T(8,128)(2,1)S(1)} %get-tuple-element.72), channel_id=1, source_target_pairs={{0,40},{4,44},{8,48},{12,52},{16,56},{20,60},{24,0},{28,4},{32,8},... | collective-permute-start | bytes 983048 | tf_op jit(solution)/shard_map/ppermute | solution.py:39
  28.6 8.8 %collective-permute-start.5 = (bf16[80,2048]{1,0:T(8,128)(2,1)S(1)}, bf16[80,2048]{1,0:T(8,128)(2,1)S(1)}, u32[]{:S(2)}, u32[]{:S(2)}) collective-permute-start(bf16[80,2048]{1,0:T(8,128)(2,1)S(1)} %get-tuple-element.71), channel_id=1, source_target_pairs={{0,48},{4,52},{8,56},{12,60},{16,0},{20,4},{24,8},{28,12},{32,16},... | collective-permute-start | bytes 983048 | tf_op jit(solution)/shard_map/ppermute | solution.py:39
  37.4 7.9 %collective-permute-done.1 = bf16[80,2048]{1,0:T(8,128)(2,1)S(1)} collective-permute-done((bf16[80,2048]{1,0:T(8,128)(2,1)S(1)}, bf16[80,2048]{1,0:T(8,128)(2,1)S(1)}, u32[]{:S(2)}, u32[]{:S(2)}) %collective-permute-start.1) | collective-permute-done | bytes 327712 | tf_op jit(solution)/shard_map/ppermute | solution.py:39
  45.2 2.4 collective-permute-start.6
  47.6 22.1 %collective-permute-done.2 = bf16[80,2048]{1,0:T(8,128)(2,1)S(1)} collective-permute-done((bf16[80,2048]{1,0:T(8,128)(2,1)S(1)}, bf16[80,2048]{1,0:T(8,128)(2,1)S(1)}, u32[]{:S(2)}, u32[]{:S(2)}) %collective-permute-start.2) | collective-permute-done | bytes 327712 | tf_op jit(solution)/shard_map/ppermute | solution.py:39
  69.9 6.4 %collective-permute-done.5 = bf16[80,2048]{1,0:T(8,128)(2,1)S(1)} collective-permute-done((bf16[80,2048]{1,0:T(8,128)(2,1)S(1)}, bf16[80,2048]{1,0:T(8,128)(2,1)S(1)}, u32[]{:S(2)}, u32[]{:S(2)}) %collective-permute-start.5) | collective-permute-done | bytes 327712 | tf_op jit(solution)/shard_map/ppermute | solution.py:39
  76.3 4.9 %collective-permute-done.6 = bf16[80,2048]{1,0:T(8,128)(2,1)S(1)} collective-permute-done((bf16[80,2048]{1,0:T(8,128)(2,1)S(1)}, bf16[80,2048]{1,0:T(8,128)(2,1)S(1)}, u32[]{:S(2)}, u32[]{:S(2)}) %collective-permute-start.6) | collective-permute-done | bytes 327712 | tf_op jit(solution)/shard_map/ppermute | solution.py:39
  81.5 4.9 %collective-permute-done.7 = bf16[8,80,2048]{2,1,0:T(8,128)(2,1)S(1)} collective-permute-done((bf16[8,80,2048]{2,1,0:T(8,128)(2,1)S(1)}, bf16[8,80,2048]{2,1,0:T(8,128)(2,1)S(1)}, u32[]{:S(2)}, u32[]{:S(2)}) %collective-permute-start.7) | collective-permute-done | bytes 2621472 | tf_op jit(solution)/shard_map/ppermute | solution.py:43
  86.4 2.5 pad_maximum_fusion.1
  89.0 3.9 fusion.10
  93.4 2.5 multiply_convert_fusion.3
  97.8 2.9 collective-permute-done.8
  103.3 2.9 convolution_convert_fusion.3
  106.3 3.9 fusion.18
  110.2 1.8 convolution_convert_fusion.4
  112.0 1.8 convolution_convert_fusion.5
  113.8 2.0 pad_maximum_fusion
  118.3 3.0 collective-permute-start.9
  122.5 4.0 collective-permute-start.11
  127.6 3.6 collective-permute-start.13
  131.8 2.3 collective-permute-start.14
  134.8 5.2 %collective-permute-done.10 = bf16[40,2048]{1,0:T(8,128)(2,1)S(1)} collective-permute-done((bf16[40,2048]{1,0:T(8,128)(2,1)}, bf16[40,2048]{1,0:T(8,128)(2,1)S(1)}, u32[]{:S(2)}, u32[]{:S(2)}) %collective-permute-start.10) | collective-permute-done | bytes 163872 | tf_op jit(solution)/shard_map/ppermute | solution.py:39
  140.7 3.4 collective-permute-done.11
  148.5 12.3 %all-to-all-start = ((bf16[8,3,64,384]{3,2,1,0:T(8,128)(2,1)}), bf16[8,3,64,384]{3,2,1,0:T(8,128)(2,1)S(1)}, u32[]{:S(2)}, u32[]{:S(2)}) async-start(bf16[8,3,64,384]{3,2,1,0:T(8,128)(2,1)} %pad_maximum_fusion.4), calls=%async_computation.2 | async-start | bytes 2359296 | tf_op jit(solution)/shard_map/all_to_all | solution.py:58
  163.9 1.7 constant_dynamic-update-slice_fusion.1
  167.2 1.8 fusion.46
  169.1 1.9 fusion.2
  174.2 9.9 %collective-permute-done.16 = bf16[128,2048]{1,0:T(8,128)(2,1)} collective-permute-done((bf16[128,2048]{1,0:T(8,128)(2,1)S(1)}, bf16[128,2048]{1,0:T(8,128)(2,1)}, u32[]{:S(2)}, u32[]{:S(2)}) %collective-permute-start.16) | collective-permute-done | bytes 524320 | tf_op jit(solution)/shard_map/ppermute | solution.py:268
  184.0 7.7 %all-to-all-done.outer_ref = bf16[8,3,64,384]{3,2,1,0:T(8,128)(2,1)S(1)} async-done(((bf16[8,3,64,384]{3,2,1,0:T(8,128)(2,1)}), bf16[8,3,64,384]{3,2,1,0:T(8,128)(2,1)S(1)}, u32[]{:S(2)}, u32[]{:S(2)}) %all-to-all-start) | async-done | bytes 1179680 | tf_op jit(solution)/shard_map/all_to_all | solution.py:58
  191.7 1.7 convert_element_type.371
  193.8 2.0 fusion.30
  198.5 1.8 pad_maximum_fusion.2
  200.2 3.7 all-to-all-start.1
  207.5 1.7 convolution_convert_fusion.6
  210.1 2.0 collective-permute-start.17
  212.1 2.4 collective-permute-start.18
  214.4 2.7 collective-permute-start.19
  217.1 2.3 collective-permute-start.20
  219.5 2.7 collective-permute-start.21
  222.2 41.5 %collective-permute-done.17 = bf16[40,2048]{1,0:T(8,128)(2,1)S(1)} collective-permute-done((bf16[40,2048]{1,0:T(8,128)(2,1)S(1)}, bf16[40,2048]{1,0:T(8,128)(2,1)S(1)}, u32[]{:S(2)}, u32[]{:S(2)}) %collective-permute-start.17) | collective-permute-done | bytes 163872 | tf_op jit(solution)/shard_map/ppermute | solution.py:39
  264.3 1.8 collective-permute-start.22
  266.1 5.3 %collective-permute-done.18 = bf16[40,2048]{1,0:T(8,128)(2,1)S(1)} collective-permute-done((bf16[40,2048]{1,0:T(8,128)(2,1)S(1)}, bf16[40,2048]{1,0:T(8,128)(2,1)S(1)}, u32[]{:S(2)}, u32[]{:S(2)}) %collective-permute-start.18) | collective-permute-done | bytes 163872 | tf_op jit(solution)/shard_map/ppermute | solution.py:39
  272.1 2.2 collective-permute-start.23
  276.3 7.0 %in_order.1 = bf16[8,3,192,384]{3,2,1,0:T(8,128)(2,1)} custom-call(s32[8]{0:T(128)} %select_reduce_fusion.order_ref, bf16[8,3,128,384]{3,2,1,0:T(8,128)(2,1)} %copy-done, bf16[8,3,64,384]{3,2,1,0:T(8,128)(2,1)} %copy-done.4), custom_call_target="tpu_custom_call" | custom-call | bytes 7077888 | tf_op jit(solution)/shard_map/in_order/pallas_call | solution.py:175
  283.3 6.1 %collective-permute-done.20 = bf16[40,2048]{1,0:T(8,128)(2,1)S(1)} collective-permute-done((bf16[40,2048]{1,0:T(8,128)(2,1)}, bf16[40,2048]{1,0:T(8,128)(2,1)S(1)}, u32[]{:S(2)}, u32[]{:S(2)}) %collective-permute-start.20) | collective-permute-done | bytes 163872 | tf_op jit(solution)/shard_map/ppermute | solution.py:39
  290.2 3.7 all-to-all-start.2
  293.9 1.7 constant_dynamic-update-slice_fusion.14
  295.7 1.7 constant_dynamic-update-slice_fusion.13
  297.3 1.7 constant_dynamic-update-slice_fusion.12
  302.0 3.2 collective-permute-done.24
  306.5 4.7 %fusion.7 = f32[640,384]{1,0:T(8,128)} fusion(bf16[640,2048]{1,0:T(8,128)(2,1)} %constant_dynamic-update-slice_fusion.15, bf16[3,2048,384]{2,1,0:T(8,128)(2,1)} %all-gather.5.cloned.1.call-done), kind=kOutput, calls=%fused_computation.27 | convolution fusion | flops 1006632960 | bytes 5177344 | tf_op jit(solution)/shard_map/dot_general | solution.py:21
  311.1 7.4 %convolution_convert_fusion = bf16[640,2048]{1,0:T(8,128)(2,1)} fusion(bf16[3,2048,384]{2,1,0:T(8,128)(2,1)} %all-gather.5.cloned.1.call-done, f32[640,384]{1,0:T(8,128)} %fusion.7, bf16[640,2048]{1,0:T(8,128)(2,1)} %constant_dynamic-update-slice_fusion.15), kind=kOutput, calls=%fused_computation.2 | convolution fusion | flops 2016051200 | bytes 9371648 | tf_op jit(solution)/shard_map/dot_general | solution.py:21
  324.6 3.1 collective-permute-start.26
  327.8 2.3 collective-permute-start.27
  331.4 5.1 %collective-permute-start.30 = (bf16[40,2048]{1,0:T(8,128)(2,1)}, bf16[40,2048]{1,0:T(8,128)(2,1)}, u32[]{:S(2)}, u32[]{:S(2)}) collective-permute-start(bf16[40,2048]{1,0:T(8,128)(2,1)} %get-tuple-element.83), channel_id=1, source_target_pairs={{0,40},{4,44},{8,48},{12,52},{16,56},{20,60},{24,0},{28,4},{32,8},... | collective-permute-start | bytes 491528 | tf_op jit(solution)/shard_map/ppermute | solution.py:39
  336.5 41.0 %collective-permute-done.26 = bf16[40,2048]{1,0:T(8,128)(2,1)S(1)} collective-permute-done((bf16[40,2048]{1,0:T(8,128)(2,1)S(1)}, bf16[40,2048]{1,0:T(8,128)(2,1)S(1)}, u32[]{:S(2)}, u32[]{:S(2)}) %collective-permute-start.26) | collective-permute-done | bytes 163872 | tf_op jit(solution)/shard_map/ppermute | solution.py:39
  377.5 5.7 %collective-permute-start.31 = (bf16[40,2048]{1,0:T(8,128)(2,1)}, bf16[40,2048]{1,0:T(8,128)(2,1)}, u32[]{:S(2)}, u32[]{:S(2)}) collective-permute-start(bf16[40,2048]{1,0:T(8,128)(2,1)} %get-tuple-element.82), channel_id=1, source_target_pairs={{0,32},{4,36},{8,40},{12,44},{16,48},{20,52},{24,56},{28,60},{32,0... | collective-permute-start | bytes 491528 | tf_op jit(solution)/shard_map/ppermute | solution.py:39
  383.2 4.5 %collective-permute-done.27 = bf16[40,2048]{1,0:T(8,128)(2,1)S(1)} collective-permute-done((bf16[40,2048]{1,0:T(8,128)(2,1)S(1)}, bf16[40,2048]{1,0:T(8,128)(2,1)S(1)}, u32[]{:S(2)}, u32[]{:S(2)}) %collective-permute-start.27) | collective-permute-done | bytes 163872 | tf_op jit(solution)/shard_map/ppermute | solution.py:39
  387.7 2.1 collective-permute-start.32
  399.8 4.6 %collective-permute-done.32 = bf16[40,2048]{1,0:T(8,128)(2,1)} collective-permute-done((bf16[40,2048]{1,0:T(8,128)(2,1)}, bf16[40,2048]{1,0:T(8,128)(2,1)}, u32[]{:S(2)}, u32[]{:S(2)}) %collective-permute-start.32) | collective-permute-done | bytes 163872 | tf_op jit(solution)/shard_map/ppermute | solution.py:39
  406.8 2.4 fusion.33
  (242 shorter events, 66.8 us)
Async XLA Ops:
  7.2 81.8 %all-gather.3.cloned.1.call-start = ((), (), s32[]{:S(2)}) async-start(), calls=%async_computation.5 | async-start | bytes 5898240 | tf_op jit(solution)/shard_map/all_gather | solution.py:159
  10.1 134.7 %reduce-scatter.5.cloned.1.call-start = ((), (), s32[]{:S(2)}) async-start(), calls=%async_computation.7 | async-start | bytes 1966080 | tf_op jit(solution)/shard_map/reduce_scatter | solution.py:253
  13.6 14.9 %collective-permute-start = (bf16[80,2048]{1,0:T(8,128)(2,1)S(1)}, bf16[80,2048]{1,0:T(8,128)(2,1)S(1)}, u32[]{:S(2)}, u32[]{:S(2)}) collective-permute-start(bf16[80,2048]{1,0:T(8,128)(2,1)S(1)} %get-tuple-element.76), channel_id=1, source_target_pairs={{0,8},{4,12},{8,16},{12,20},{16,24},{20,28},{24,32},{28,36},{32,40... | collective-permute-start | bytes 983048 | tf_op jit(solution)/shard_map/ppermute | solution.py:39
  15.6 29.6 %collective-permute-start.1 = (bf16[80,2048]{1,0:T(8,128)(2,1)S(1)}, bf16[80,2048]{1,0:T(8,128)(2,1)S(1)}, u32[]{:S(2)}, u32[]{:S(2)}) collective-permute-start(bf16[80,2048]{1,0:T(8,128)(2,1)S(1)} %get-tuple-element.75), channel_id=1, source_target_pairs={{0,16},{4,20},{8,24},{12,28},{16,32},{20,36},{24,40},{28,44},{32,4... | collective-permute-start | bytes 983048 | tf_op jit(solution)/shard_map/ppermute | solution.py:39
  18.9 50.9 %collective-permute-start.2 = (bf16[80,2048]{1,0:T(8,128)(2,1)S(1)}, bf16[80,2048]{1,0:T(8,128)(2,1)S(1)}, u32[]{:S(2)}, u32[]{:S(2)}) collective-permute-start(bf16[80,2048]{1,0:T(8,128)(2,1)S(1)} %get-tuple-element.74), channel_id=1, source_target_pairs={{0,24},{4,28},{8,32},{12,36},{16,40},{20,44},{24,48},{28,52},{32,5... | collective-permute-start | bytes 983048 | tf_op jit(solution)/shard_map/ppermute | solution.py:39
  22.9 46.9 %collective-permute-start.3 = (bf16[80,2048]{1,0:T(8,128)(2,1)S(1)}, bf16[80,2048]{1,0:T(8,128)(2,1)S(1)}, u32[]{:S(2)}, u32[]{:S(2)}) collective-permute-start(bf16[80,2048]{1,0:T(8,128)(2,1)S(1)} %get-tuple-element.73), channel_id=1, source_target_pairs={{0,32},{4,36},{8,40},{12,44},{16,48},{20,52},{24,56},{28,60},{32,0... | collective-permute-start | bytes 983048 | tf_op jit(solution)/shard_map/ppermute | solution.py:39
  23.5 46.4 %collective-permute-start.4 = (bf16[80,2048]{1,0:T(8,128)(2,1)S(1)}, bf16[80,2048]{1,0:T(8,128)(2,1)S(1)}, u32[]{:S(2)}, u32[]{:S(2)}) collective-permute-start(bf16[80,2048]{1,0:T(8,128)(2,1)S(1)} %get-tuple-element.72), channel_id=1, source_target_pairs={{0,40},{4,44},{8,48},{12,52},{16,56},{20,60},{24,0},{28,4},{32,8},... | collective-permute-start | bytes 983048 | tf_op jit(solution)/shard_map/ppermute | solution.py:39
  28.6 47.7 %collective-permute-start.5 = (bf16[80,2048]{1,0:T(8,128)(2,1)S(1)}, bf16[80,2048]{1,0:T(8,128)(2,1)S(1)}, u32[]{:S(2)}, u32[]{:S(2)}) collective-permute-start(bf16[80,2048]{1,0:T(8,128)(2,1)S(1)} %get-tuple-element.71), channel_id=1, source_target_pairs={{0,48},{4,52},{8,56},{12,60},{16,0},{20,4},{24,8},{28,12},{32,16},... | collective-permute-start | bytes 983048 | tf_op jit(solution)/shard_map/ppermute | solution.py:39
  45.2 36.0 %collective-permute-start.6 = (bf16[80,2048]{1,0:T(8,128)(2,1)S(1)}, bf16[80,2048]{1,0:T(8,128)(2,1)S(1)}, u32[]{:S(2)}, u32[]{:S(2)}) collective-permute-start(bf16[80,2048]{1,0:T(8,128)(2,1)S(1)} %get-tuple-element.70), channel_id=1, source_target_pairs={{0,56},{4,60},{8,0},{12,4},{16,8},{20,12},{24,16},{28,20},{32,24},... | collective-permute-start | bytes 983048 | tf_op jit(solution)/shard_map/ppermute | solution.py:39
  81.2 5.2 %collective-permute-start.7 = (bf16[8,80,2048]{2,1,0:T(8,128)(2,1)S(1)}, bf16[8,80,2048]{2,1,0:T(8,128)(2,1)S(1)}, u32[]{:S(2)}, u32[]{:S(2)}) collective-permute-start(bf16[8,80,2048]{2,1,0:T(8,128)(2,1)S(1)} %bitcast_dynamic-update-slice_fusion), channel_id=1, source_target_pairs={{0,4},{4,0},{8,12},{12,8},{16,20},{20,16},{24,28},{28,24},{32,36},... | collective-permute-start | bytes 7864328 | tf_op jit(solution)/shard_map/ppermute | solution.py:43
  89.0 3.9 copy-start.12
  89.0 4.4 %copy-start.49 = (bf16[3,2048,384]{2,1,0:T(8,128)(2,1)S(1)}, bf16[3,2048,384]{2,1,0:T(8,128)(2,1)}, u32[]{:S(2)}) copy-start(bf16[3,2048,384]{2,1,0:T(8,128)(2,1)} %all-gather.3.cloned.1.call-done) | copy-start | bytes 14155780
  97.6 3.1 collective-permute-start.8
  106.2 85.5 %reduce-scatter.3.cloned.1.call-start = ((), (), s32[]{:S(2)}) async-start(), calls=%async_computation.6 | async-start | bytes 3932160 | tf_op jit(solution)/shard_map/reduce_scatter | solution.py:265
  106.2 3.9 copy-start.13
  106.3 3.9 copy-start.53
  118.3 13.5 %collective-permute-start.9 = (bf16[40,2048]{1,0:T(8,128)(2,1)}, bf16[40,2048]{1,0:T(8,128)(2,1)S(1)}, u32[]{:S(2)}, u32[]{:S(2)}) collective-permute-start(bf16[40,2048]{1,0:T(8,128)(2,1)} %get-tuple-element.104), channel_id=1, source_target_pairs={{0,56},{4,60},{8,0},{12,4},{16,8},{20,12},{24,16},{28,20},{32,24},... | collective-permute-start | bytes 491528 | tf_op jit(solution)/shard_map/ppermute | solution.py:39
  121.3 18.7 %collective-permute-start.10 = (bf16[40,2048]{1,0:T(8,128)(2,1)}, bf16[40,2048]{1,0:T(8,128)(2,1)S(1)}, u32[]{:S(2)}, u32[]{:S(2)}) collective-permute-start(bf16[40,2048]{1,0:T(8,128)(2,1)} %get-tuple-element.103), channel_id=1, source_target_pairs={{0,48},{4,52},{8,56},{12,60},{16,0},{20,4},{24,8},{28,12},{32,16},... | collective-permute-start | bytes 491528 | tf_op jit(solution)/shard_map/ppermute | solution.py:39
  122.5 21.6 %collective-permute-start.11 = (bf16[40,2048]{1,0:T(8,128)(2,1)S(1)}, bf16[40,2048]{1,0:T(8,128)(2,1)S(1)}, u32[]{:S(2)}, u32[]{:S(2)}) collective-permute-start(bf16[40,2048]{1,0:T(8,128)(2,1)S(1)} %get-tuple-element.102), channel_id=1, source_target_pairs={{0,40},{4,44},{8,48},{12,52},{16,56},{20,60},{24,0},{28,4},{32,8},... | collective-permute-start | bytes 491528 | tf_op jit(solution)/shard_map/ppermute | solution.py:39
  126.5 34.2 %collective-permute-start.12 = (bf16[40,2048]{1,0:T(8,128)(2,1)}, bf16[40,2048]{1,0:T(8,128)(2,1)}, u32[]{:S(2)}, u32[]{:S(2)}) collective-permute-start(bf16[40,2048]{1,0:T(8,128)(2,1)} %get-tuple-element.101), channel_id=1, source_target_pairs={{0,32},{4,36},{8,40},{12,44},{16,48},{20,52},{24,56},{28,60},{32,0... | collective-permute-start | bytes 491528 | tf_op jit(solution)/shard_map/ppermute | solution.py:39
  127.6 34.8 %collective-permute-start.13 = (bf16[40,2048]{1,0:T(8,128)(2,1)}, bf16[40,2048]{1,0:T(8,128)(2,1)}, u32[]{:S(2)}, u32[]{:S(2)}) collective-permute-start(bf16[40,2048]{1,0:T(8,128)(2,1)} %get-tuple-element.100), channel_id=1, source_target_pairs={{0,24},{4,28},{8,32},{12,36},{16,40},{20,44},{24,48},{28,52},{32,5... | collective-permute-start | bytes 491528 | tf_op jit(solution)/shard_map/ppermute | solution.py:39
  131.8 32.1 %collective-permute-start.14 = (bf16[40,2048]{1,0:T(8,128)(2,1)}, bf16[40,2048]{1,0:T(8,128)(2,1)}, u32[]{:S(2)}, u32[]{:S(2)}) collective-permute-start(bf16[40,2048]{1,0:T(8,128)(2,1)} %get-tuple-element.99), channel_id=1, source_target_pairs={{0,16},{4,20},{8,24},{12,28},{16,32},{20,36},{24,40},{28,44},{32,4... | collective-permute-start | bytes 491528 | tf_op jit(solution)/shard_map/ppermute | solution.py:39
  140.0 25.6 %collective-permute-start.15 = (bf16[40,2048]{1,0:T(8,128)(2,1)}, bf16[40,2048]{1,0:T(8,128)(2,1)}, u32[]{:S(2)}, u32[]{:S(2)}) collective-permute-start(bf16[40,2048]{1,0:T(8,128)(2,1)} %get-tuple-element.98), channel_id=1, source_target_pairs={{0,8},{4,12},{8,16},{12,20},{16,24},{20,28},{24,32},{28,36},{32,40... | collective-permute-start | bytes 491528 | tf_op jit(solution)/shard_map/ppermute | solution.py:39
  148.4 18.7 %copy-start.35 = (s32[128]{0:T(128)S(1)}, s32[128]{0:T(128)}, u32[]{:S(2)}) copy-start(s32[128]{0:T(128)} %get-tuple-element.61) | copy-start | bytes 1540
  148.4 18.7 %copy-start.37 = (s32[128]{0:T(128)S(1)}, s32[128]{0:T(128)}, u32[]{:S(2)}) copy-start(s32[128]{0:T(128)} %get-tuple-element.142) | copy-start | bytes 1540
  148.4 18.7 %copy-start.40 = (f32[128]{0:T(128)S(1)}, f32[128]{0:T(128)}, u32[]{:S(2)}) copy-start(f32[128]{0:T(128)} %copy-done.39) | copy-start | bytes 1540
  148.5 18.7 %copy-start.42 = (f32[128]{0:T(128)S(1)}, f32[128]{0:T(128)}, u32[]{:S(2)}) copy-start(f32[128]{0:T(128)} %copy-done.41) | copy-start | bytes 1540
  148.5 43.3 %all-to-all-start = ((bf16[8,3,64,384]{3,2,1,0:T(8,128)(2,1)}), bf16[8,3,64,384]{3,2,1,0:T(8,128)(2,1)S(1)}, u32[]{:S(2)}, u32[]{:S(2)}) async-start(bf16[8,3,64,384]{3,2,1,0:T(8,128)(2,1)} %pad_maximum_fusion.4), calls=%async_computation.2 | async-start | bytes 2359296 | tf_op jit(solution)/shard_map/all_to_all | solution.py:58
  163.9 5.1 %copy-start.6 = (bf16[1,128,2048]{2,1,0:T(8,128)(2,1)S(1)}, bf16[1,128,2048]{2,1,0:T(8,128)(2,1)}, u32[]{:S(2)}) copy-start(bf16[1,128,2048]{2,1,0:T(8,128)(2,1)} %param.14) | copy-start | bytes 1572868
  163.9 5.1 %copy-start.36 = (s32[128]{0:T(128)S(1)}, s32[128]{0:T(128)}, u32[]{:S(2)}) copy-start(s32[128]{0:T(128)} %get-tuple-element.61) | copy-start | bytes 1540
  163.9 5.1 %copy-start.38 = (s32[128]{0:T(128)S(1)}, s32[128]{0:T(128)}, u32[]{:S(2)}) copy-start(s32[128]{0:T(128)} %get-tuple-element.142) | copy-start | bytes 1540
  171.0 13.0 %collective-permute-start.16 = (bf16[128,2048]{1,0:T(8,128)(2,1)S(1)}, bf16[128,2048]{1,0:T(8,128)(2,1)}, u32[]{:S(2)}, u32[]{:S(2)}) collective-permute-start(bf16[128,2048]{1,0:T(8,128)(2,1)S(1)} %fusion.2), channel_id=1, source_target_pairs={{0,64},{64,128},{128,192},{192,0},{1,65},{65,129},{129,193},{193,1... | collective-permute-start | bytes 1572872 | tf_op jit(solution)/shard_map/ppermute | solution.py:268
  191.7 4.0 copy-start.4
  200.2 3.8 copy-start.8
  200.2 74.6 %all-to-all-start.1 = ((bf16[8,3,128,384]{3,2,1,0:T(8,128)(2,1)}), bf16[8,3,128,384]{3,2,1,0:T(8,128)(2,1)S(1)}, u32[]{:S(2)}, u32[]{:S(2)}) async-start(bf16[8,3,128,384]{3,2,1,0:T(8,128)(2,1)} %pad_maximum_fusion.2), calls=%async_computation.3 | async-start | bytes 4718592 | tf_op jit(solution)/shard_map/all_to_all | solution.py:58
  204.0 102.5 %all-gather.5.cloned.1.call-start = ((), (), s32[]{:S(2)}) async-start(), calls=%async_computation.8 | async-start | bytes 5898240 | tf_op jit(solution)/shard_map/all_gather | solution.py:159
  209.1 65.1 %copy-start.51 = (s32[1,8]{1,0:T(1,128)S(1)}, s32[1,8]{1,0:T(1,128)}, u32[]{:S(2)}) copy-start(s32[1,8]{1,0:T(1,128)} %param.21) | copy-start | bytes 100
  210.1 53.6 %collective-permute-start.17 = (bf16[40,2048]{1,0:T(8,128)(2,1)S(1)}, bf16[40,2048]{1,0:T(8,128)(2,1)S(1)}, u32[]{:S(2)}, u32[]{:S(2)}) collective-permute-start(bf16[40,2048]{1,0:T(8,128)(2,1)S(1)} %get-tuple-element.97), channel_id=1, source_target_pairs={{0,8},{4,12},{8,16},{12,20},{16,24},{20,28},{24,32},{28,36},{32,40... | collective-permute-start | bytes 491528 | tf_op jit(solution)/shard_map/ppermute | solution.py:39
  212.1 59.3 %collective-permute-start.18 = (bf16[40,2048]{1,0:T(8,128)(2,1)S(1)}, bf16[40,2048]{1,0:T(8,128)(2,1)S(1)}, u32[]{:S(2)}, u32[]{:S(2)}) collective-permute-start(bf16[40,2048]{1,0:T(8,128)(2,1)S(1)} %get-tuple-element.96), channel_id=1, source_target_pairs={{0,16},{4,20},{8,24},{12,28},{16,32},{20,36},{24,40},{28,44},{32,4... | collective-permute-start | bytes 491528 | tf_op jit(solution)/shard_map/ppermute | solution.py:39
  214.4 68.8 %collective-permute-start.19 = (bf16[40,2048]{1,0:T(8,128)(2,1)}, bf16[40,2048]{1,0:T(8,128)(2,1)S(1)}, u32[]{:S(2)}, u32[]{:S(2)}) collective-permute-start(bf16[40,2048]{1,0:T(8,128)(2,1)} %get-tuple-element.95), channel_id=1, source_target_pairs={{0,24},{4,28},{8,32},{12,36},{16,40},{20,44},{24,48},{28,52},{32,5... | collective-permute-start | bytes 491528 | tf_op jit(solution)/shard_map/ppermute | solution.py:39
  217.1 72.3 %collective-permute-start.20 = (bf16[40,2048]{1,0:T(8,128)(2,1)}, bf16[40,2048]{1,0:T(8,128)(2,1)S(1)}, u32[]{:S(2)}, u32[]{:S(2)}) collective-permute-start(bf16[40,2048]{1,0:T(8,128)(2,1)} %get-tuple-element.94), channel_id=1, source_target_pairs={{0,32},{4,36},{8,40},{12,44},{16,48},{20,52},{24,56},{28,60},{32,0... | collective-permute-start | bytes 491528 | tf_op jit(solution)/shard_map/ppermute | solution.py:39
  219.5 69.9 %collective-permute-start.21 = (bf16[40,2048]{1,0:T(8,128)(2,1)}, bf16[40,2048]{1,0:T(8,128)(2,1)S(1)}, u32[]{:S(2)}, u32[]{:S(2)}) collective-permute-start(bf16[40,2048]{1,0:T(8,128)(2,1)} %get-tuple-element.93), channel_id=1, source_target_pairs={{0,40},{4,44},{8,48},{12,52},{16,56},{20,60},{24,0},{28,4},{32,8},... | collective-permute-start | bytes 491528 | tf_op jit(solution)/shard_map/ppermute | solution.py:39
  264.3 25.1 %collective-permute-start.22 = (bf16[40,2048]{1,0:T(8,128)(2,1)S(1)}, bf16[40,2048]{1,0:T(8,128)(2,1)S(1)}, u32[]{:S(2)}, u32[]{:S(2)}) collective-permute-start(bf16[40,2048]{1,0:T(8,128)(2,1)S(1)} %get-tuple-element.92), channel_id=1, source_target_pairs={{0,48},{4,52},{8,56},{12,60},{16,0},{20,4},{24,8},{28,12},{32,16},... | collective-permute-start | bytes 491528 | tf_op jit(solution)/shard_map/ppermute | solution.py:39
  272.1 17.4 %collective-permute-start.23 = (bf16[40,2048]{1,0:T(8,128)(2,1)S(1)}, bf16[40,2048]{1,0:T(8,128)(2,1)S(1)}, u32[]{:S(2)}, u32[]{:S(2)}) collective-permute-start(bf16[40,2048]{1,0:T(8,128)(2,1)S(1)} %get-tuple-element.91), channel_id=1, source_target_pairs={{0,56},{4,60},{8,0},{12,4},{16,8},{20,12},{24,16},{28,20},{32,24},... | collective-permute-start | bytes 491528 | tf_op jit(solution)/shard_map/ppermute | solution.py:39
  283.3 6.2 %copy-start.31 = (bf16[40,2048]{1,0:T(8,128)(2,1)}, bf16[40,2048]{1,0:T(8,128)(2,1)S(1)}, u32[]{:S(2)}) copy-start(bf16[40,2048]{1,0:T(8,128)(2,1)S(1)} %collective-permute-done.19) | copy-start | bytes 491524
  290.2 100.3 %all-to-all-start.2 = ((bf16[8,3,192,384]{3,2,1,0:T(8,128)(2,1)}), bf16[8,3,192,384]{3,2,1,0:T(8,128)(2,1)S(1)}, u32[]{:S(2)}, u32[]{:S(2)}) async-start(bf16[8,3,192,384]{3,2,1,0:T(8,128)(2,1)} %in_order.1), calls=%async_computation.4 | async-start | bytes 7077888 | tf_op jit(solution)/shard_map/all_to_all | solution.py:58
  293.9 5.1 %copy-start.30 = (bf16[40,2048]{1,0:T(8,128)(2,1)S(1)}, bf16[40,2048]{1,0:T(8,128)(2,1)}, u32[]{:S(2)}) copy-start(bf16[40,2048]{1,0:T(8,128)(2,1)} %copy-done.29) | copy-start | bytes 491524
  293.9 5.8 %copy-start.24 = (bf16[40,2048]{1,0:T(8,128)(2,1)S(1)}, bf16[40,2048]{1,0:T(8,128)(2,1)}, u32[]{:S(2)}) copy-start(bf16[40,2048]{1,0:T(8,128)(2,1)} %copy-done.23) | copy-start | bytes 491524
  293.9 6.6 %copy-start.26 = (bf16[40,2048]{1,0:T(8,128)(2,1)S(1)}, bf16[40,2048]{1,0:T(8,128)(2,1)}, u32[]{:S(2)}) copy-start(bf16[40,2048]{1,0:T(8,128)(2,1)} %copy-done.25) | copy-start | bytes 491524
  293.9 7.3 %copy-start.28 = (bf16[40,2048]{1,0:T(8,128)(2,1)S(1)}, bf16[40,2048]{1,0:T(8,128)(2,1)}, u32[]{:S(2)}) copy-start(bf16[40,2048]{1,0:T(8,128)(2,1)} %copy-done.27) | copy-start | bytes 491524
  302.0 3.2 collective-permute-start.24
  318.5 4.7 %copy-start.15 = (bf16[640,2048]{1,0:T(8,128)(2,1)S(1)}, bf16[640,2048]{1,0:T(8,128)(2,1)}, u32[]{:S(2)}) copy-start(bf16[640,2048]{1,0:T(8,128)(2,1)} %convolution_convert_fusion) | copy-start | bytes 7864324
  320.1 3.1 collective-permute-start.25
  324.6 52.9 %collective-permute-start.26 = (bf16[40,2048]{1,0:T(8,128)(2,1)S(1)}, bf16[40,2048]{1,0:T(8,128)(2,1)S(1)}, u32[]{:S(2)}, u32[]{:S(2)}) collective-permute-start(bf16[40,2048]{1,0:T(8,128)(2,1)S(1)} %get-tuple-element.87), channel_id=1, source_target_pairs={{0,56},{4,60},{8,0},{12,4},{16,8},{20,12},{24,16},{28,20},{32,24},... | collective-permute-start | bytes 491528 | tf_op jit(solution)/shard_map/ppermute | solution.py:39
  327.8 60.0 %collective-permute-start.27 = (bf16[40,2048]{1,0:T(8,128)(2,1)S(1)}, bf16[40,2048]{1,0:T(8,128)(2,1)S(1)}, u32[]{:S(2)}, u32[]{:S(2)}) collective-permute-start(bf16[40,2048]{1,0:T(8,128)(2,1)S(1)} %get-tuple-element.86), channel_id=1, source_target_pairs={{0,48},{4,52},{8,56},{12,60},{16,0},{20,4},{24,8},{28,12},{32,16},... | collective-permute-start | bytes 491528 | tf_op jit(solution)/shard_map/ppermute | solution.py:39
  330.1 59.7 %collective-permute-start.28 = (bf16[40,2048]{1,0:T(8,128)(2,1)S(1)}, bf16[40,2048]{1,0:T(8,128)(2,1)S(1)}, u32[]{:S(2)}, u32[]{:S(2)}) collective-permute-start(bf16[40,2048]{1,0:T(8,128)(2,1)S(1)} %get-tuple-element.85), channel_id=1, source_target_pairs={{0,16},{4,20},{8,24},{12,28},{16,32},{20,36},{24,40},{28,44},{32,4... | collective-permute-start | bytes 491528 | tf_op jit(solution)/shard_map/ppermute | solution.py:39
  330.7 59.8 %collective-permute-start.29 = (bf16[40,2048]{1,0:T(8,128)(2,1)S(1)}, bf16[40,2048]{1,0:T(8,128)(2,1)}, u32[]{:S(2)}, u32[]{:S(2)}) collective-permute-start(bf16[40,2048]{1,0:T(8,128)(2,1)S(1)} %get-tuple-element.84), channel_id=1, source_target_pairs={{0,8},{4,12},{8,16},{12,20},{16,24},{20,28},{24,32},{28,36},{32,40... | collective-permute-start | bytes 491528 | tf_op jit(solution)/shard_map/ppermute | solution.py:39
  331.4 66.5 %collective-permute-start.30 = (bf16[40,2048]{1,0:T(8,128)(2,1)}, bf16[40,2048]{1,0:T(8,128)(2,1)}, u32[]{:S(2)}, u32[]{:S(2)}) collective-permute-start(bf16[40,2048]{1,0:T(8,128)(2,1)} %get-tuple-element.83), channel_id=1, source_target_pairs={{0,40},{4,44},{8,48},{12,52},{16,56},{20,60},{24,0},{28,4},{32,8},... | collective-permute-start | bytes 491528 | tf_op jit(solution)/shard_map/ppermute | solution.py:39
  377.5 12.3 %copy-start.19 = (bf16[40,2048]{1,0:T(8,128)(2,1)}, bf16[40,2048]{1,0:T(8,128)(2,1)S(1)}, u32[]{:S(2)}) copy-start(bf16[40,2048]{1,0:T(8,128)(2,1)S(1)} %collective-permute-done.26) | copy-start | bytes 491524
  377.5 21.3 %collective-permute-start.31 = (bf16[40,2048]{1,0:T(8,128)(2,1)}, bf16[40,2048]{1,0:T(8,128)(2,1)}, u32[]{:S(2)}, u32[]{:S(2)}) collective-permute-start(bf16[40,2048]{1,0:T(8,128)(2,1)} %get-tuple-element.82), channel_id=1, source_target_pairs={{0,32},{4,36},{8,40},{12,44},{16,48},{20,52},{24,56},{28,60},{32,0... | collective-permute-start | bytes 491528 | tf_op jit(solution)/shard_map/ppermute | solution.py:39
  387.7 16.6 %collective-permute-start.32 = (bf16[40,2048]{1,0:T(8,128)(2,1)}, bf16[40,2048]{1,0:T(8,128)(2,1)}, u32[]{:S(2)}, u32[]{:S(2)}) collective-permute-start(bf16[40,2048]{1,0:T(8,128)(2,1)} %get-tuple-element.81), channel_id=1, source_target_pairs={{0,24},{4,28},{8,32},{12,36},{16,40},{20,44},{24,48},{28,52},{32,5... | collective-permute-start | bytes 491528 | tf_op jit(solution)/shard_map/ppermute | solution.py:39
  396.0 9.3 %copy-start.18 = (bf16[40,2048]{1,0:T(8,128)(2,1)S(1)}, bf16[40,2048]{1,0:T(8,128)(2,1)}, u32[]{:S(2)}) copy-start(bf16[40,2048]{1,0:T(8,128)(2,1)} %copy-done.17) | copy-start | bytes 491524
  396.9 9.3 %copy-start.46 = (f32[128]{0:T(128)S(1)}, f32[128]{0:T(128)}, u32[]{:S(2)}) copy-start(f32[128]{0:T(128)} %get-tuple-element.126) | copy-start | bytes 1540
  396.9 9.3 %copy-start.47 = (f32[128]{0:T(128)S(1)}, f32[128]{0:T(128)}, u32[]{:S(2)}) copy-start(f32[128]{0:T(128)} %get-tuple-element.127) | copy-start | bytes 1540
  (31 other events, 48.8 us)
Sparse Core Ops, SparseCore 0:
  10.4 57.4 all-gather.2
  106.3 26.6 reduce-scatter.4
  135.6 40.6 reduce-scatter.2
  206.3 56.0 all-gather.4

commit v3 on v2

--- a/solution.py
+++ b/solution.py
@@ -129,24 +129,47 @@
     return (token_rows.astype(F32) + mixed).astype(BF16)
 
 
-def adam_step(weight, mean, square, grads):
-    grads = grads.astype(F32)
-    mean_new = (beta_one * mean.astype(F32) + (1.0 - beta_one) * grads).astype(BF16)
-    square_new = (beta_two * square.astype(F32) + (1.0 - beta_two) * grads * grads).astype(BF16)
-    mean_wide = lax.optimization_barrier(mean_new).astype(F32)
-    square_wide = lax.optimization_barrier(square_new).astype(F32)
-    update = mean_wide / bias_one / (jnp.sqrt(square_wide / bias_two) + adam_eps)
-    return ((weight - learn_rate * update).astype(BF16), mean_new, square_new)
+def step_kernel(weight_ref, mean_ref, square_ref, grad_ref, out_ref, low_ref):
+    rows = out_ref.shape[3]
+    for piece in range(out_ref.shape[0]):
+        here = (slice(None), slice(piece * rows, (piece + 1) * rows))
+        grads = grad_ref[here].astype(F32)
+        mean_new = (beta_one * mean_ref[here].astype(F32) + (1.0 - beta_one) * grads).astype(BF16)
+        square_new = beta_two * square_ref[here].astype(F32) + (1.0 - beta_two) * grads * grads
+        square_new = square_new.astype(BF16)
+        root = jnp.sqrt(square_new.astype(F32) * (1.0 / bias_two)) + adam_eps
+        update = mean_new.astype(F32) * (learn_rate / bias_one) / root
+        low = (weight_ref[here] - update).astype(BF16)
+        out_ref[piece, 0] = low
+        out_ref[piece, 1] = mean_new
+        out_ref[piece, 2] = square_new
+        low_ref[here] = low
+
+
+def stepped_eighths(weight, mean, square, grads, count):
+    kinds, deep, hidden = weight.shape
+    rows = deep // count
+    each = 2
+    here = pl.BlockSpec((kinds, each * rows, hidden), lambda i: (0, i, 0))
+    pieces, low = pl.pallas_call(
+        step_kernel,
+        grid=(count // each,),
+        in_specs=[here] * 4,
+        out_specs=[pl.BlockSpec((each, 3, kinds, rows, hidden), lambda i: (i, 0, 0, 0, 0)), here],
+        out_shape=[
+            jax.ShapeDtypeStruct((count, 3, kinds, rows, hidden), BF16),
+            jax.ShapeDtypeStruct(weight.shape, BF16),
+        ],
+        cost_estimate=pl.CostEstimate(
+            flops=16 * weight.size, bytes_accessed=18 * weight.size, transcendentals=2 * weight.size
+        ),
+        name="stepped_eighths",
+    )(weight, mean, square, grads)
+    return (pieces.reshape(count, 3, kinds * rows, hidden), low)
 
 
 def side_by_side(inner, outer):
     return jnp.concatenate([inner, outer.T[None]], axis=0)
-
-
-def in_eighths(array, count):
-    kinds, deep, hidden = array.shape
-    pieces = array.reshape(kinds, count, deep // count, hidden).transpose(1, 0, 2, 3)
-    return pieces.reshape(count, kinds * (deep // count), hidden)
 
 
 def from_eighths(pieces, kinds):
@@ -218,8 +241,6 @@
     hidden = w_out.shape[0]
     parts = lax.axis_size("dp")
     weight = side_by_side(w_in, w_out)
-    mean = side_by_side(inner_mean[0, 0], outer_mean[0, 0])
-    square = side_by_side(inner_square[0, 0], outer_square[0, 0])
     kinds = weight.shape[0]
 
     full = full_weights(weight.astype(BF16))
@@ -271,19 +292,21 @@
         [(i, (i + 1) % lax.axis_size("pipe")) for i in range(lax.axis_size("pipe"))],
     )
 
-    old = (weight, mean, square)
-    new_outer = adam_step(*[a[2:] for a in old], sum_outer[None])
-    outer_pieces = same_core_exchange(
-        jnp.stack([in_eighths(a, experts) for a in new_outer], axis=1)
-    )
+    outer_old = [a.T[None] for a in (w_out, outer_mean[0, 0], outer_square[0, 0])]
+    new_outer, low_outer = stepped_eighths(*outer_old, sum_outer[None], experts)
+    outer_pieces = same_core_exchange(new_outer)
     sum_inner, outer_pieces, second_rest = lax.optimization_barrier(
         (sum_inner, outer_pieces, second_in)
     )
-    new_inner = adam_step(*[a[:2] for a in old], sum_inner.reshape(2, width // parts, hidden))
-    inner_pieces = same_core_exchange(
-        jnp.stack([in_eighths(a, experts) for a in new_inner], axis=1)
-    )
-    full_two = full_weights(jnp.concatenate([new_inner[0], new_outer[0]], axis=0))
+    new_inner, low_inner = stepped_eighths(
+        w_in,
+        inner_mean[0, 0],
+        inner_square[0, 0],
+        sum_inner.reshape(2, width // parts, hidden),
+        experts,
+    )
+    inner_pieces = same_core_exchange(new_inner)
+    full_two = full_weights(jnp.concatenate([low_inner, low_outer], axis=0))
 
     slots_two = route(second_ids[0], chip, experts, rows)
     hits_two = spots(slots_two, rows, total)
@@ -296,7 +319,6 @@
         jnp.where(new_slot[0][:, None] == places[None, :], places[:, None], 0), axis=0
     )
     ordered = in_order(inner_pieces, outer_pieces, inverse)
-    (ordered,) = in_step([ordered], own_two, range(1, experts))
     moved = same_core_exchange(ordered)
 
     half_two = expert_forward(both_cores(own_two), full_two)[0]

time: 424 us -> 405 us (0.955)
  other arithmetic: 26.4 us -> 10.7 us
  Pallas kernels: 7 us -> 16.5 us
  starting transfers between devices: 97.5 us -> 89.4 us
  waiting for transfers between devices: 183 us -> 189 us
  local copies, waits for them, and re-layouts: 46.3 us -> 40.4 us
    pallas_call x0 -> x2, Pallas kernels: none -> 9.5 us  [stepped_eighths(): pl.pallas_call(step_kernel, grid=(count // each,), in_specs=[here] * 4, o...]
    all_to_all x3, starting transfers between devices: 19.7 us -> 12.2 us  [same_core_exchange(): lax.all_to_all(array, 'expert', split_axis=0, concat_axis=0, tiled=True,...]
    unnamed x143 -> x97, local copies, waits for them, and re-layouts: 33.8 us -> 26.4 us
    convert_element_type x5 -> x0, other arithmetic: 4.9 us -> none  [the longest x2 1.87 us: adam_step(): (beta_one * mean.astype(F32) + (1.0 - beta_one) * grads).astype(BF16)]
  transfers between devices with their start and end apart: 40 -> 40, of which waited for: 19 -> 20; matrix products, arithmetic and copies ran while one was open for 19% -> 15% of each run, Pallas kernels for 2% -> 3%
where the time goes in v3:
time: 405 us; the launch traced here: 397 us
  waiting for transfers between devices  189 us (47%)
  starting transfers between devices  89.4 us (22%)
  local copies, waits for them, and re-layouts  40.4 us (10%)
  matrix products  37 us (9%)
  Pallas kernels  16.5 us (4%)
  between operations  14.7 us (4%)
  other arithmetic  10.7 us (3%)
    ppermute x28, waiting for transfers between devices, along_chips(): lax.ppermute(block, 'expert', [(i, (i + 2 * distance) % size) for i in ra...  153 us
    ppermute x28, starting transfers between devices, along_chips(): lax.ppermute(block, 'expert', [(i, (i + 2 * distance) % size) for i in ra...  75.7 us
    dot_general x11, matrix products, contract(): lax.dot_general(left, right, (((left_dim,), (right_dim,)), ((), ())), pre...  32.8 us
    unnamed x97, local copies, waits for them, and re-layouts  26.4 us
    ppermute x4, waiting for transfers between devices, from_sibling(): lax.ppermute(block, 'expert', [(i, i ^ 1) for i in range(lax.axis_size('e...  13.4 us
    ppermute x1, waiting for transfers between devices, per_device(): lax.ppermute(first_out, 'pipe', [(i, (i + 1) % lax.axis_size('pipe')) for...  13.2 us
    all_to_all x3, starting transfers between devices, same_core_exchange(): lax.all_to_all(array, 'expert', split_axis=0, concat_axis=0, tiled=True,...  12.2 us
    pallas_call x2, Pallas kernels, stepped_eighths(): pl.pallas_call(step_kernel, grid=(count // each,), in_specs=[here] * 4, o...  9.5 us
  transfers between devices with their start and end apart: 40, of which 20 were waited for; matrix products, arithmetic and copies ran while one was open for 15% of the time, Pallas kernels for 3%

profile of v3, /device:TPU:14, one launch (start us, length us, event | category | flops | bytes accessed | tf_op | source)
XLA Modules:
  0.0 397.3 jit_solution(3268623091712342809)
XLA Ops:
  11.9 1.6 convolution_convert_fusion.2
  13.7 2.0 collective-permute-start
  15.7 3.3 collective-permute-start.1
  19.0 4.0 %collective-permute-start.2 = (bf16[80,2048]{1,0:T(8,128)(2,1)S(1)}, bf16[80,2048]{1,0:T(8,128)(2,1)S(1)}, u32[]{:S(2)}, u32[]{:S(2)}) collective-permute-start(bf16[80,2048]{1,0:T(8,128)(2,1)S(1)} %get-tuple-element.66), channel_id=1, source_target_pairs={{0,24},{4,28},{8,32},{12,36},{16,40},{20,44},{24,48},{28,52},{32,5... | collective-permute-start | bytes 983048 | tf_op jit(solution)/shard_map/ppermute | solution.py:39
  23.6 4.9 %collective-permute-start.4 = (bf16[80,2048]{1,0:T(8,128)(2,1)S(1)}, bf16[80,2048]{1,0:T(8,128)(2,1)S(1)}, u32[]{:S(2)}, u32[]{:S(2)}) collective-permute-start(bf16[80,2048]{1,0:T(8,128)(2,1)S(1)} %get-tuple-element.64), channel_id=1, source_target_pairs={{0,40},{4,44},{8,48},{12,52},{16,56},{20,60},{24,0},{28,4},{32,8},... | collective-permute-start | bytes 983048 | tf_op jit(solution)/shard_map/ppermute | solution.py:39
  28.7 8.7 %collective-permute-start.5 = (bf16[80,2048]{1,0:T(8,128)(2,1)S(1)}, bf16[80,2048]{1,0:T(8,128)(2,1)S(1)}, u32[]{:S(2)}, u32[]{:S(2)}) collective-permute-start(bf16[80,2048]{1,0:T(8,128)(2,1)S(1)} %get-tuple-element.63), channel_id=1, source_target_pairs={{0,48},{4,52},{8,56},{12,60},{16,0},{20,4},{24,8},{28,12},{32,16},... | collective-permute-start | bytes 983048 | tf_op jit(solution)/shard_map/ppermute | solution.py:39
  37.4 7.9 %collective-permute-done.1 = bf16[80,2048]{1,0:T(8,128)(2,1)S(1)} collective-permute-done((bf16[80,2048]{1,0:T(8,128)(2,1)S(1)}, bf16[80,2048]{1,0:T(8,128)(2,1)S(1)}, u32[]{:S(2)}, u32[]{:S(2)}) %collective-permute-start.1) | collective-permute-done | bytes 327712 | tf_op jit(solution)/shard_map/ppermute | solution.py:39
  45.3 2.3 collective-permute-start.6
  47.7 22.2 %collective-permute-done.2 = bf16[80,2048]{1,0:T(8,128)(2,1)S(1)} collective-permute-done((bf16[80,2048]{1,0:T(8,128)(2,1)S(1)}, bf16[80,2048]{1,0:T(8,128)(2,1)S(1)}, u32[]{:S(2)}, u32[]{:S(2)}) %collective-permute-start.2) | collective-permute-done | bytes 327712 | tf_op jit(solution)/shard_map/ppermute | solution.py:39
  70.0 6.4 %collective-permute-done.5 = bf16[80,2048]{1,0:T(8,128)(2,1)S(1)} collective-permute-done((bf16[80,2048]{1,0:T(8,128)(2,1)S(1)}, bf16[80,2048]{1,0:T(8,128)(2,1)S(1)}, u32[]{:S(2)}, u32[]{:S(2)}) %collective-permute-start.5) | collective-permute-done | bytes 327712 | tf_op jit(solution)/shard_map/ppermute | solution.py:39
  76.4 4.9 %collective-permute-done.6 = bf16[80,2048]{1,0:T(8,128)(2,1)S(1)} collective-permute-done((bf16[80,2048]{1,0:T(8,128)(2,1)S(1)}, bf16[80,2048]{1,0:T(8,128)(2,1)S(1)}, u32[]{:S(2)}, u32[]{:S(2)}) %collective-permute-start.6) | collective-permute-done | bytes 327712 | tf_op jit(solution)/shard_map/ppermute | solution.py:39
  81.6 4.9 %collective-permute-done.7 = bf16[8,80,2048]{2,1,0:T(8,128)(2,1)S(1)} collective-permute-done((bf16[8,80,2048]{2,1,0:T(8,128)(2,1)S(1)}, bf16[8,80,2048]{2,1,0:T(8,128)(2,1)S(1)}, u32[]{:S(2)}, u32[]{:S(2)}) %collective-permute-start.7) | collective-permute-done | bytes 2621472 | tf_op jit(solution)/shard_map/ppermute | solution.py:43
  86.5 1.8 pad_maximum_fusion.1
  88.3 3.1 fusion.6
  91.4 2.6 multiply_convert_fusion.3
  95.8 2.9 collective-permute-done.8
  101.3 2.9 convolution_convert_fusion.3
  104.3 3.8 fusion.12
  108.1 1.8 convolution_convert_fusion.4
  109.9 1.8 convolution_convert_fusion.5
  112.1 1.9 copy.42
  116.9 2.9 collective-permute-start.9
  120.9 4.0 %collective-permute-start.11 = (bf16[40,2048]{1,0:T(8,128)(2,1)}, bf16[40,2048]{1,0:T(8,128)(2,1)}, u32[]{:S(2)}, u32[]{:S(2)}) collective-permute-start(bf16[40,2048]{1,0:T(8,128)(2,1)} %get-tuple-element.90), channel_id=1, source_target_pairs={{0,40},{4,44},{8,48},{12,52},{16,56},{20,60},{24,0},{28,4},{32,8},... | collective-permute-start | bytes 491528 | tf_op jit(solution)/shard_map/ppermute | solution.py:39
  126.0 3.5 collective-permute-start.13
  129.6 2.4 collective-permute-start.14
  132.0 6.2 %collective-permute-done.10 = bf16[40,2048]{1,0:T(8,128)(2,1)S(1)} collective-permute-done((bf16[40,2048]{1,0:T(8,128)(2,1)S(1)}, bf16[40,2048]{1,0:T(8,128)(2,1)S(1)}, u32[]{:S(2)}, u32[]{:S(2)}) %collective-permute-start.10) | collective-permute-done | bytes 163872 | tf_op jit(solution)/shard_map/ppermute | solution.py:39
  138.2 4.0 %stepped_eighths.2 = (bf16[8,3,1,64,384]{4,3,2,1,0:T(8,128)(2,1)}, bf16[1,512,384]{2,1,0:T(8,128)(2,1)}) custom-call(f32[1,512,384]{2,1,0:T(8,128)} %bitcast.216, bf16[1,512,384]{2,1,0:T(8,128)(2,1)} %bitcast.241, bf16[1,512,384]{2,1,0:T(8,128)(2,1)} %bitcast.242, bf16[1,512,384]{2,1,0:T(8,128)(2,1)} %bitcast.249), custom_call_target="tpu_custom_call" | custom-call | flops 3145728 | bytes 3538944 | tf_op jit(solution)/shard_map/stepped_eighths/pallas_call | solution.py:154
  142.3 4.5 %all-to-all-start = ((bf16[8,3,64,384]{3,2,1,0:T(8,128)(2,1)}), bf16[8,3,64,384]{3,2,1,0:T(8,128)(2,1)S(1)}, u32[]{:S(2)}, u32[]{:S(2)}) async-start(bf16[8,3,64,384]{3,2,1,0:T(8,128)(2,1)} %bitcast.243), calls=%async_computation.2 | async-start | bytes 2359296 | tf_op jit(solution)/shard_map/all_to_all | solution.py:58
  151.3 6.4 %collective-permute-done.15 = bf16[40,2048]{1,0:T(8,128)(2,1)} collective-permute-done((bf16[40,2048]{1,0:T(8,128)(2,1)S(1)}, bf16[40,2048]{1,0:T(8,128)(2,1)}, u32[]{:S(2)}, u32[]{:S(2)}) %collective-permute-start.15) | collective-permute-done | bytes 163872 | tf_op jit(solution)/shard_map/ppermute | solution.py:39
  160.3 13.2 %collective-permute-done.16 = bf16[128,2048]{1,0:T(8,128)(2,1)} collective-permute-done((bf16[128,2048]{1,0:T(8,128)(2,1)S(1)}, bf16[128,2048]{1,0:T(8,128)(2,1)}, u32[]{:S(2)}, u32[]{:S(2)}) %collective-permute-start.16) | collective-permute-done | bytes 524320 | tf_op jit(solution)/shard_map/ppermute | solution.py:289
  173.5 9.2 %all-to-all-done.outer_ref = bf16[8,3,64,384]{3,2,1,0:T(8,128)(2,1)S(1)} async-done(((bf16[8,3,64,384]{3,2,1,0:T(8,128)(2,1)}), bf16[8,3,64,384]{3,2,1,0:T(8,128)(2,1)S(1)}, u32[]{:S(2)}, u32[]{:S(2)}) %all-to-all-start) | async-done | bytes 1179680 | tf_op jit(solution)/shard_map/all_to_all | solution.py:58
  182.7 5.5 %stepped_eighths.3 = (bf16[8,3,2,64,384]{4,3,2,1,0:T(8,128)(2,1)}, bf16[2,512,384]{2,1,0:T(8,128)(2,1)}) custom-call(f32[2,512,384]{2,1,0:T(8,128)} %bitcast.217, bf16[2,512,384]{2,1,0:T(8,128)(2,1)} %bitcast.246, bf16[2,512,384]{2,1,0:T(8,128)(2,1)} %bitcast.247, bf16[2,512,384]{2,1,0:T(8,128)(2,1)} %bitcast.248), custom_call_target="tpu_custom_call" | custom-call | flops 6291456 | bytes 7077888 | tf_op jit(solution)/shard_map/stepped_eighths/pallas_call | solution.py:154
  188.2 2.3 pad_maximum_fusion.3
  190.6 4.1 %all-to-all-start.1 = ((bf16[8,3,128,384]{3,2,1,0:T(8,128)(2,1)}), bf16[8,3,128,384]{3,2,1,0:T(8,128)(2,1)S(1)}, u32[]{:S(2)}, u32[]{:S(2)}) async-start(bf16[8,3,128,384]{3,2,1,0:T(8,128)(2,1)} %bitcast.236), calls=%async_computation.3 | async-start | bytes 4718592 | tf_op jit(solution)/shard_map/all_to_all | solution.py:58
  196.1 1.7 convolution_convert_fusion.6
  198.8 2.0 collective-permute-start.17
  201.4 2.4 collective-permute-start.18
  203.7 2.7 collective-permute-start.19
  206.4 2.4 collective-permute-start.20
  208.8 2.7 collective-permute-start.21
  211.4 42.6 %collective-permute-done.17 = bf16[40,2048]{1,0:T(8,128)(2,1)S(1)} collective-permute-done((bf16[40,2048]{1,0:T(8,128)(2,1)S(1)}, bf16[40,2048]{1,0:T(8,128)(2,1)S(1)}, u32[]{:S(2)}, u32[]{:S(2)}) %collective-permute-start.17) | collective-permute-done | bytes 163872 | tf_op jit(solution)/shard_map/ppermute | solution.py:39
  254.1 2.3 collective-permute-start.22
  257.2 4.5 %collective-permute-done.18 = bf16[40,2048]{1,0:T(8,128)(2,1)S(1)} collective-permute-done((bf16[40,2048]{1,0:T(8,128)(2,1)S(1)}, bf16[40,2048]{1,0:T(8,128)(2,1)S(1)}, u32[]{:S(2)}, u32[]{:S(2)}) %collective-permute-start.18) | collective-permute-done | bytes 163872 | tf_op jit(solution)/shard_map/ppermute | solution.py:39
  261.6 2.3 collective-permute-start.23
  266.2 7.0 %in_order.1 = bf16[8,3,192,384]{3,2,1,0:T(8,128)(2,1)} custom-call(s32[8]{0:T(128)} %select_reduce_fusion.order_ref, bf16[8,3,128,384]{3,2,1,0:T(8,128)(2,1)} %copy-done, bf16[8,3,64,384]{3,2,1,0:T(8,128)(2,1)} %copy-done.4), custom_call_target="tpu_custom_call" | custom-call | bytes 7077888 | tf_op jit(solution)/shard_map/in_order/pallas_call | solution.py:198
  273.2 3.7 all-to-all-start.2
  276.9 1.7 constant_dynamic-update-slice_fusion.12
  280.0 1.7 constant_dynamic-update-slice_fusion.11
  281.7 1.7 constant_dynamic-update-slice_fusion.10
  283.3 1.7 constant_dynamic-update-slice_fusion.9
  285.0 1.7 constant_dynamic-update-slice_fusion.8
  286.7 3.2 collective-permute-done.24
  291.1 4.7 %fusion.3 = f32[640,384]{1,0:T(8,128)} fusion(bf16[640,2048]{1,0:T(8,128)(2,1)} %constant_dynamic-update-slice_fusion.15, bf16[3,2048,384]{2,1,0:T(8,128)(2,1)} %all-gather.5.cloned.1.call-done), kind=kOutput, calls=%fused_computation.20 | convolution fusion | flops 1006632960 | bytes 5177344 | tf_op jit(solution)/shard_map/dot_general | solution.py:21
  295.8 7.4 %convolution_convert_fusion = bf16[640,2048]{1,0:T(8,128)(2,1)} fusion(bf16[3,2048,384]{2,1,0:T(8,128)(2,1)} %all-gather.5.cloned.1.call-done, f32[640,384]{1,0:T(8,128)} %fusion.3, bf16[640,2048]{1,0:T(8,128)(2,1)} %constant_dynamic-update-slice_fusion.15), kind=kOutput, calls=%fused_computation.2 | convolution fusion | flops 2016051200 | bytes 9371648 | tf_op jit(solution)/shard_map/dot_general | solution.py:21
  303.2 1.6 slice.310
  305.6 2.3 collective-permute-done.25
  309.3 1.7 collective-permute-start.26
  311.0 2.3 collective-permute-start.27
  314.3 4.7 %collective-permute-start.30 = (bf16[40,2048]{1,0:T(8,128)(2,1)}, bf16[40,2048]{1,0:T(8,128)(2,1)}, u32[]{:S(2)}, u32[]{:S(2)}) collective-permute-start(bf16[40,2048]{1,0:T(8,128)(2,1)} %get-tuple-element.71), channel_id=1, source_target_pairs={{0,40},{4,44},{8,48},{12,52},{16,56},{20,60},{24,0},{28,4},{32,8},... | collective-permute-start | bytes 491528 | tf_op jit(solution)/shard_map/ppermute | solution.py:39
  319.0 44.6 %collective-permute-done.26 = bf16[40,2048]{1,0:T(8,128)(2,1)S(1)} collective-permute-done((bf16[40,2048]{1,0:T(8,128)(2,1)S(1)}, bf16[40,2048]{1,0:T(8,128)(2,1)S(1)}, u32[]{:S(2)}, u32[]{:S(2)}) %collective-permute-start.26) | collective-permute-done | bytes 163872 | tf_op jit(solution)/shard_map/ppermute | solution.py:39
  363.6 4.0 %collective-permute-start.31 = (bf16[40,2048]{1,0:T(8,128)(2,1)}, bf16[40,2048]{1,0:T(8,128)(2,1)}, u32[]{:S(2)}, u32[]{:S(2)}) collective-permute-start(bf16[40,2048]{1,0:T(8,128)(2,1)} %get-tuple-element.70), channel_id=1, source_target_pairs={{0,32},{4,36},{8,40},{12,44},{16,48},{20,52},{24,56},{28,60},{32,0... | collective-permute-start | bytes 491528 | tf_op jit(solution)/shard_map/ppermute | solution.py:39
  367.6 3.8 collective-permute-done.27
  371.4 4.4 %collective-permute-start.32 = (bf16[40,2048]{1,0:T(8,128)(2,1)}, bf16[40,2048]{1,0:T(8,128)(2,1)}, u32[]{:S(2)}, u32[]{:S(2)}) collective-permute-start(bf16[40,2048]{1,0:T(8,128)(2,1)} %get-tuple-element.69), channel_id=1, source_target_pairs={{0,24},{4,28},{8,32},{12,36},{16,40},{20,44},{24,48},{28,52},{32,5... | collective-permute-start | bytes 491528 | tf_op jit(solution)/shard_map/ppermute | solution.py:39
  388.2 2.4 fusion.20
  (186 shorter events, 47.0 us)
Async XLA Ops:
  7.2 1.6 copy-start.2
  7.2 81.1 %all-gather.3.cloned.1.call-start = ((), (), s32[]{:S(2)}) async-start(), calls=%async_computation.5 | async-start | bytes 5898240 | tf_op jit(solution)/shard_map/all_gather | solution.py:182
  9.6 1.5 copy-start.19
  10.8 127.4 %reduce-scatter.5.cloned.1.call-start = ((), (), s32[]{:S(2)}) async-start(), calls=%async_computation.7 | async-start | bytes 1966080 | tf_op jit(solution)/shard_map/reduce_scatter | solution.py:274
  13.7 15.0 %collective-permute-start = (bf16[80,2048]{1,0:T(8,128)(2,1)S(1)}, bf16[80,2048]{1,0:T(8,128)(2,1)S(1)}, u32[]{:S(2)}, u32[]{:S(2)}) collective-permute-start(bf16[80,2048]{1,0:T(8,128)(2,1)S(1)} %get-tuple-element.68), channel_id=1, source_target_pairs={{0,8},{4,12},{8,16},{12,20},{16,24},{20,28},{24,32},{28,36},{32,40... | collective-permute-start | bytes 983048 | tf_op jit(solution)/shard_map/ppermute | solution.py:39
  15.7 29.6 %collective-permute-start.1 = (bf16[80,2048]{1,0:T(8,128)(2,1)S(1)}, bf16[80,2048]{1,0:T(8,128)(2,1)S(1)}, u32[]{:S(2)}, u32[]{:S(2)}) collective-permute-start(bf16[80,2048]{1,0:T(8,128)(2,1)S(1)} %get-tuple-element.67), channel_id=1, source_target_pairs={{0,16},{4,20},{8,24},{12,28},{16,32},{20,36},{24,40},{28,44},{32,4... | collective-permute-start | bytes 983048 | tf_op jit(solution)/shard_map/ppermute | solution.py:39
  19.0 50.9 %collective-permute-start.2 = (bf16[80,2048]{1,0:T(8,128)(2,1)S(1)}, bf16[80,2048]{1,0:T(8,128)(2,1)S(1)}, u32[]{:S(2)}, u32[]{:S(2)}) collective-permute-start(bf16[80,2048]{1,0:T(8,128)(2,1)S(1)} %get-tuple-element.66), channel_id=1, source_target_pairs={{0,24},{4,28},{8,32},{12,36},{16,40},{20,44},{24,48},{28,52},{32,5... | collective-permute-start | bytes 983048 | tf_op jit(solution)/shard_map/ppermute | solution.py:39
  23.0 46.9 %collective-permute-start.3 = (bf16[80,2048]{1,0:T(8,128)(2,1)S(1)}, bf16[80,2048]{1,0:T(8,128)(2,1)S(1)}, u32[]{:S(2)}, u32[]{:S(2)}) collective-permute-start(bf16[80,2048]{1,0:T(8,128)(2,1)S(1)} %get-tuple-element.65), channel_id=1, source_target_pairs={{0,32},{4,36},{8,40},{12,44},{16,48},{20,52},{24,56},{28,60},{32,0... | collective-permute-start | bytes 983048 | tf_op jit(solution)/shard_map/ppermute | solution.py:39
  23.6 46.4 %collective-permute-start.4 = (bf16[80,2048]{1,0:T(8,128)(2,1)S(1)}, bf16[80,2048]{1,0:T(8,128)(2,1)S(1)}, u32[]{:S(2)}, u32[]{:S(2)}) collective-permute-start(bf16[80,2048]{1,0:T(8,128)(2,1)S(1)} %get-tuple-element.64), channel_id=1, source_target_pairs={{0,40},{4,44},{8,48},{12,52},{16,56},{20,60},{24,0},{28,4},{32,8},... | collective-permute-start | bytes 983048 | tf_op jit(solution)/shard_map/ppermute | solution.py:39
  28.7 47.7 %collective-permute-start.5 = (bf16[80,2048]{1,0:T(8,128)(2,1)S(1)}, bf16[80,2048]{1,0:T(8,128)(2,1)S(1)}, u32[]{:S(2)}, u32[]{:S(2)}) collective-permute-start(bf16[80,2048]{1,0:T(8,128)(2,1)S(1)} %get-tuple-element.63), channel_id=1, source_target_pairs={{0,48},{4,52},{8,56},{12,60},{16,0},{20,4},{24,8},{28,12},{32,16},... | collective-permute-start | bytes 983048 | tf_op jit(solution)/shard_map/ppermute | solution.py:39
  45.3 36.0 %collective-permute-start.6 = (bf16[80,2048]{1,0:T(8,128)(2,1)S(1)}, bf16[80,2048]{1,0:T(8,128)(2,1)S(1)}, u32[]{:S(2)}, u32[]{:S(2)}) collective-permute-start(bf16[80,2048]{1,0:T(8,128)(2,1)S(1)} %get-tuple-element.62), channel_id=1, source_target_pairs={{0,56},{4,60},{8,0},{12,4},{16,8},{20,12},{24,16},{28,20},{32,24},... | collective-permute-start | bytes 983048 | tf_op jit(solution)/shard_map/ppermute | solution.py:39
  81.3 5.2 %collective-permute-start.7 = (bf16[8,80,2048]{2,1,0:T(8,128)(2,1)S(1)}, bf16[8,80,2048]{2,1,0:T(8,128)(2,1)S(1)}, u32[]{:S(2)}, u32[]{:S(2)}) collective-permute-start(bf16[8,80,2048]{2,1,0:T(8,128)(2,1)S(1)} %bitcast_dynamic-update-slice_fusion), channel_id=1, source_target_pairs={{0,4},{4,0},{8,12},{12,8},{16,20},{20,16},{24,28},{28,24},{32,36},... | collective-permute-start | bytes 7864328 | tf_op jit(solution)/shard_map/ppermute | solution.py:43
  88.3 3.1 copy-start.26
  91.4 2.6 copy-start.29
  95.6 3.1 collective-permute-start.8
  99.2 2.1 copy-start.6
  104.2 78.5 %reduce-scatter.3.cloned.1.call-start = ((), (), s32[]{:S(2)}) async-start(), calls=%async_computation.6 | async-start | bytes 3932160 | tf_op jit(solution)/shard_map/reduce_scatter | solution.py:286
  104.3 3.8 copy-start.30
  108.1 1.8 copy-start.31
  114.0 1.9 copy-start.10
  115.0 1.8 copy-start.12
  115.0 4.7 %copy-start.11 = (bf16[40,2048]{1,0:T(8,128)(2,1)S(1)}, bf16[40,2048]{1,0:T(8,128)(2,1)}, u32[]{:S(2)}) copy-start(bf16[40,2048]{1,0:T(8,128)(2,1)} %get-tuple-element.91) | copy-start | bytes 491524
  116.9 12.7 %collective-permute-start.9 = (bf16[40,2048]{1,0:T(8,128)(2,1)S(1)}, bf16[40,2048]{1,0:T(8,128)(2,1)S(1)}, u32[]{:S(2)}, u32[]{:S(2)}) collective-permute-start(bf16[40,2048]{1,0:T(8,128)(2,1)S(1)} %copy-done.12), channel_id=1, source_target_pairs={{0,56},{4,60},{8,0},{12,4},{16,8},{20,12},{24,16},{28,20},{32,24},... | collective-permute-start | bytes 491528 | tf_op jit(solution)/shard_map/ppermute | solution.py:39
  119.8 18.4 %collective-permute-start.10 = (bf16[40,2048]{1,0:T(8,128)(2,1)S(1)}, bf16[40,2048]{1,0:T(8,128)(2,1)S(1)}, u32[]{:S(2)}, u32[]{:S(2)}) collective-permute-start(bf16[40,2048]{1,0:T(8,128)(2,1)S(1)} %copy-done.11), channel_id=1, source_target_pairs={{0,48},{4,52},{8,56},{12,60},{16,0},{20,4},{24,8},{28,12},{32,16},... | collective-permute-start | bytes 491528 | tf_op jit(solution)/shard_map/ppermute | solution.py:39
  120.9 25.9 %collective-permute-start.11 = (bf16[40,2048]{1,0:T(8,128)(2,1)}, bf16[40,2048]{1,0:T(8,128)(2,1)}, u32[]{:S(2)}, u32[]{:S(2)}) collective-permute-start(bf16[40,2048]{1,0:T(8,128)(2,1)} %get-tuple-element.90), channel_id=1, source_target_pairs={{0,40},{4,44},{8,48},{12,52},{16,56},{20,60},{24,0},{28,4},{32,8},... | collective-permute-start | bytes 491528 | tf_op jit(solution)/shard_map/ppermute | solution.py:39
  124.9 22.9 %collective-permute-start.12 = (bf16[40,2048]{1,0:T(8,128)(2,1)}, bf16[40,2048]{1,0:T(8,128)(2,1)}, u32[]{:S(2)}, u32[]{:S(2)}) collective-permute-start(bf16[40,2048]{1,0:T(8,128)(2,1)} %get-tuple-element.89), channel_id=1, source_target_pairs={{0,32},{4,36},{8,40},{12,44},{16,48},{20,52},{24,56},{28,60},{32,0... | collective-permute-start | bytes 491528 | tf_op jit(solution)/shard_map/ppermute | solution.py:39
  126.0 24.2 %collective-permute-start.13 = (bf16[40,2048]{1,0:T(8,128)(2,1)}, bf16[40,2048]{1,0:T(8,128)(2,1)}, u32[]{:S(2)}, u32[]{:S(2)}) collective-permute-start(bf16[40,2048]{1,0:T(8,128)(2,1)} %get-tuple-element.88), channel_id=1, source_target_pairs={{0,24},{4,28},{8,32},{12,36},{16,40},{20,44},{24,48},{28,52},{32,5... | collective-permute-start | bytes 491528 | tf_op jit(solution)/shard_map/ppermute | solution.py:39
  129.6 21.7 %collective-permute-start.14 = (bf16[40,2048]{1,0:T(8,128)(2,1)}, bf16[40,2048]{1,0:T(8,128)(2,1)S(1)}, u32[]{:S(2)}, u32[]{:S(2)}) collective-permute-start(bf16[40,2048]{1,0:T(8,128)(2,1)} %get-tuple-element.87), channel_id=1, source_target_pairs={{0,16},{4,20},{8,24},{12,28},{16,32},{20,36},{24,40},{28,44},{32,4... | collective-permute-start | bytes 491528 | tf_op jit(solution)/shard_map/ppermute | solution.py:39
  138.2 19.5 %collective-permute-start.15 = (bf16[40,2048]{1,0:T(8,128)(2,1)S(1)}, bf16[40,2048]{1,0:T(8,128)(2,1)}, u32[]{:S(2)}, u32[]{:S(2)}) collective-permute-start(bf16[40,2048]{1,0:T(8,128)(2,1)S(1)} %get-tuple-element.86), channel_id=1, source_target_pairs={{0,8},{4,12},{8,16},{12,20},{16,24},{20,28},{24,32},{28,36},{32,40... | collective-permute-start | bytes 491528 | tf_op jit(solution)/shard_map/ppermute | solution.py:39
  142.3 40.4 %all-to-all-start = ((bf16[8,3,64,384]{3,2,1,0:T(8,128)(2,1)}), bf16[8,3,64,384]{3,2,1,0:T(8,128)(2,1)S(1)}, u32[]{:S(2)}, u32[]{:S(2)}) async-start(bf16[8,3,64,384]{3,2,1,0:T(8,128)(2,1)} %bitcast.243), calls=%async_computation.2 | async-start | bytes 2359296 | tf_op jit(solution)/shard_map/all_to_all | solution.py:58
  146.8 144.3 %all-gather.5.cloned.1.call-start = ((), (), s32[]{:S(2)}) async-start(), calls=%async_computation.8 | async-start | bytes 5898240 | tf_op jit(solution)/shard_map/all_gather | solution.py:182
  159.7 13.8 %collective-permute-start.16 = (bf16[128,2048]{1,0:T(8,128)(2,1)S(1)}, bf16[128,2048]{1,0:T(8,128)(2,1)}, u32[]{:S(2)}, u32[]{:S(2)}) collective-permute-start(bf16[128,2048]{1,0:T(8,128)(2,1)S(1)} %fusion.2), channel_id=1, source_target_pairs={{0,64},{64,128},{128,192},{192,0},{1,65},{65,129},{129,193},{193,1... | collective-permute-start | bytes 1572872 | tf_op jit(solution)/shard_map/ppermute | solution.py:289
  182.7 5.5 %copy-start.4 = (bf16[8,3,64,384]{3,2,1,0:T(8,128)(2,1)}, bf16[8,3,64,384]{3,2,1,0:T(8,128)(2,1)S(1)}, u32[]{:S(2)}) copy-start(bf16[8,3,64,384]{3,2,1,0:T(8,128)(2,1)S(1)} %all-to-all-done.outer_ref) | copy-start | bytes 3538948
  182.7 5.5 %copy-start.8 = (bf16[1,512,384]{2,1,0:T(8,128)(2,1)S(1)}, bf16[1,512,384]{2,1,0:T(8,128)(2,1)}, u32[]{:S(2)}) copy-start(bf16[1,512,384]{2,1,0:T(8,128)(2,1)} %get-tuple-element.27) | copy-start | bytes 1179652
  190.5 4.1 %copy-start.20 = (s32[1,128,2]{1,2,0:T(2,128)S(1)}, s32[1,128,2]{1,2,0:T(2,128)}, u32[]{:S(2)}) copy-start(s32[1,128,2]{1,2,0:T(2,128)} %param.19) | copy-start | bytes 3076
  190.6 74.2 %all-to-all-start.1 = ((bf16[8,3,128,384]{3,2,1,0:T(8,128)(2,1)}), bf16[8,3,128,384]{3,2,1,0:T(8,128)(2,1)S(1)}, u32[]{:S(2)}, u32[]{:S(2)}) async-start(bf16[8,3,128,384]{3,2,1,0:T(8,128)(2,1)} %bitcast.236), calls=%async_computation.3 | async-start | bytes 4718592 | tf_op jit(solution)/shard_map/all_to_all | solution.py:58
  197.7 3.0 copy-start.28
  198.8 55.3 %collective-permute-start.17 = (bf16[40,2048]{1,0:T(8,128)(2,1)S(1)}, bf16[40,2048]{1,0:T(8,128)(2,1)S(1)}, u32[]{:S(2)}, u32[]{:S(2)}) collective-permute-start(bf16[40,2048]{1,0:T(8,128)(2,1)S(1)} %get-tuple-element.85), channel_id=1, source_target_pairs={{0,8},{4,12},{8,16},{12,20},{16,24},{20,28},{24,32},{28,36},{32,40... | collective-permute-start | bytes 491528 | tf_op jit(solution)/shard_map/ppermute | solution.py:39
  201.4 60.3 %collective-permute-start.18 = (bf16[40,2048]{1,0:T(8,128)(2,1)S(1)}, bf16[40,2048]{1,0:T(8,128)(2,1)S(1)}, u32[]{:S(2)}, u32[]{:S(2)}) collective-permute-start(bf16[40,2048]{1,0:T(8,128)(2,1)S(1)} %get-tuple-element.84), channel_id=1, source_target_pairs={{0,16},{4,20},{8,24},{12,28},{16,32},{20,36},{24,40},{28,44},{32,4... | collective-permute-start | bytes 491528 | tf_op jit(solution)/shard_map/ppermute | solution.py:39
  203.7 73.1 %collective-permute-start.19 = (bf16[40,2048]{1,0:T(8,128)(2,1)}, bf16[40,2048]{1,0:T(8,128)(2,1)}, u32[]{:S(2)}, u32[]{:S(2)}) collective-permute-start(bf16[40,2048]{1,0:T(8,128)(2,1)} %get-tuple-element.83), channel_id=1, source_target_pairs={{0,24},{4,28},{8,32},{12,36},{16,40},{20,44},{24,48},{28,52},{32,5... | collective-permute-start | bytes 491528 | tf_op jit(solution)/shard_map/ppermute | solution.py:39
  206.4 73.6 %collective-permute-start.20 = (bf16[40,2048]{1,0:T(8,128)(2,1)}, bf16[40,2048]{1,0:T(8,128)(2,1)}, u32[]{:S(2)}, u32[]{:S(2)}) collective-permute-start(bf16[40,2048]{1,0:T(8,128)(2,1)} %get-tuple-element.82), channel_id=1, source_target_pairs={{0,32},{4,36},{8,40},{12,44},{16,48},{20,52},{24,56},{28,60},{32,0... | collective-permute-start | bytes 491528 | tf_op jit(solution)/shard_map/ppermute | solution.py:39
  208.8 72.9 %collective-permute-start.21 = (bf16[40,2048]{1,0:T(8,128)(2,1)}, bf16[40,2048]{1,0:T(8,128)(2,1)}, u32[]{:S(2)}, u32[]{:S(2)}) collective-permute-start(bf16[40,2048]{1,0:T(8,128)(2,1)} %get-tuple-element.81), channel_id=1, source_target_pairs={{0,40},{4,44},{8,48},{12,52},{16,56},{20,60},{24,0},{28,4},{32,8},... | collective-permute-start | bytes 491528 | tf_op jit(solution)/shard_map/ppermute | solution.py:39
  254.1 29.2 %collective-permute-start.22 = (bf16[40,2048]{1,0:T(8,128)(2,1)}, bf16[40,2048]{1,0:T(8,128)(2,1)}, u32[]{:S(2)}, u32[]{:S(2)}) collective-permute-start(bf16[40,2048]{1,0:T(8,128)(2,1)} %get-tuple-element.80), channel_id=1, source_target_pairs={{0,48},{4,52},{8,56},{12,60},{16,0},{20,4},{24,8},{28,12},{32,16},... | collective-permute-start | bytes 491528 | tf_op jit(solution)/shard_map/ppermute | solution.py:39
  261.6 23.4 %collective-permute-start.23 = (bf16[40,2048]{1,0:T(8,128)(2,1)}, bf16[40,2048]{1,0:T(8,128)(2,1)}, u32[]{:S(2)}, u32[]{:S(2)}) collective-permute-start(bf16[40,2048]{1,0:T(8,128)(2,1)} %get-tuple-element.79), channel_id=1, source_target_pairs={{0,56},{4,60},{8,0},{12,4},{16,8},{20,12},{24,16},{28,20},{32,24},... | collective-permute-start | bytes 491528 | tf_op jit(solution)/shard_map/ppermute | solution.py:39
  273.2 103.3 %all-to-all-start.2 = ((bf16[8,3,192,384]{3,2,1,0:T(8,128)(2,1)}), bf16[8,3,192,384]{3,2,1,0:T(8,128)(2,1)S(1)}, u32[]{:S(2)}, u32[]{:S(2)}) async-start(bf16[8,3,192,384]{3,2,1,0:T(8,128)(2,1)} %in_order.1), calls=%async_computation.4 | async-start | bytes 7077888 | tf_op jit(solution)/shard_map/all_to_all | solution.py:58
  286.6 3.2 collective-permute-start.24
  295.8 9.2 %copy-start.25 = (f32[1,128,2]{1,2,0:T(2,128)S(1)}, f32[1,128,2]{1,2,0:T(2,128)}, u32[]{:S(2)}) copy-start(f32[1,128,2]{1,2,0:T(2,128)} %param.20) | copy-start | bytes 3076
  303.2 4.7 %copy-start.7 = (bf16[640,2048]{1,0:T(8,128)(2,1)S(1)}, bf16[640,2048]{1,0:T(8,128)(2,1)}, u32[]{:S(2)}) copy-start(bf16[640,2048]{1,0:T(8,128)(2,1)} %convolution_convert_fusion) | copy-start | bytes 7864324
  304.8 3.1 collective-permute-start.25
  309.3 54.3 %collective-permute-start.26 = (bf16[40,2048]{1,0:T(8,128)(2,1)S(1)}, bf16[40,2048]{1,0:T(8,128)(2,1)S(1)}, u32[]{:S(2)}, u32[]{:S(2)}) collective-permute-start(bf16[40,2048]{1,0:T(8,128)(2,1)S(1)} %get-tuple-element.75), channel_id=1, source_target_pairs={{0,56},{4,60},{8,0},{12,4},{16,8},{20,12},{24,16},{28,20},{32,24},... | collective-permute-start | bytes 491528 | tf_op jit(solution)/shard_map/ppermute | solution.py:39
  311.0 60.4 %collective-permute-start.27 = (bf16[40,2048]{1,0:T(8,128)(2,1)S(1)}, bf16[40,2048]{1,0:T(8,128)(2,1)S(1)}, u32[]{:S(2)}, u32[]{:S(2)}) collective-permute-start(bf16[40,2048]{1,0:T(8,128)(2,1)S(1)} %get-tuple-element.74), channel_id=1, source_target_pairs={{0,48},{4,52},{8,56},{12,60},{16,0},{20,4},{24,8},{28,12},{32,16},... | collective-permute-start | bytes 491528 | tf_op jit(solution)/shard_map/ppermute | solution.py:39
  313.4 62.4 %collective-permute-start.28 = (bf16[40,2048]{1,0:T(8,128)(2,1)S(1)}, bf16[40,2048]{1,0:T(8,128)(2,1)S(1)}, u32[]{:S(2)}, u32[]{:S(2)}) collective-permute-start(bf16[40,2048]{1,0:T(8,128)(2,1)S(1)} %get-tuple-element.73), channel_id=1, source_target_pairs={{0,16},{4,20},{8,24},{12,28},{16,32},{20,36},{24,40},{28,44},{32,4... | collective-permute-start | bytes 491528 | tf_op jit(solution)/shard_map/ppermute | solution.py:39
  314.0 62.5 %collective-permute-start.29 = (bf16[40,2048]{1,0:T(8,128)(2,1)S(1)}, bf16[40,2048]{1,0:T(8,128)(2,1)}, u32[]{:S(2)}, u32[]{:S(2)}) collective-permute-start(bf16[40,2048]{1,0:T(8,128)(2,1)S(1)} %get-tuple-element.72), channel_id=1, source_target_pairs={{0,8},{4,12},{8,16},{12,20},{16,24},{20,28},{24,32},{28,36},{32,40... | collective-permute-start | bytes 491528 | tf_op jit(solution)/shard_map/ppermute | solution.py:39
  314.3 69.6 %collective-permute-start.30 = (bf16[40,2048]{1,0:T(8,128)(2,1)}, bf16[40,2048]{1,0:T(8,128)(2,1)}, u32[]{:S(2)}, u32[]{:S(2)}) collective-permute-start(bf16[40,2048]{1,0:T(8,128)(2,1)} %get-tuple-element.71), channel_id=1, source_target_pairs={{0,40},{4,44},{8,48},{12,52},{16,56},{20,60},{24,0},{28,4},{32,8},... | collective-permute-start | bytes 491528 | tf_op jit(solution)/shard_map/ppermute | solution.py:39
  363.6 12.2 %copy-start.15 = (bf16[40,2048]{1,0:T(8,128)(2,1)}, bf16[40,2048]{1,0:T(8,128)(2,1)S(1)}, u32[]{:S(2)}) copy-start(bf16[40,2048]{1,0:T(8,128)(2,1)S(1)} %collective-permute-done.26) | copy-start | bytes 491524
  363.6 21.2 %collective-permute-start.31 = (bf16[40,2048]{1,0:T(8,128)(2,1)}, bf16[40,2048]{1,0:T(8,128)(2,1)}, u32[]{:S(2)}, u32[]{:S(2)}) collective-permute-start(bf16[40,2048]{1,0:T(8,128)(2,1)} %get-tuple-element.70), channel_id=1, source_target_pairs={{0,32},{4,36},{8,40},{12,44},{16,48},{20,52},{24,56},{28,60},{32,0... | collective-permute-start | bytes 491528 | tf_op jit(solution)/shard_map/ppermute | solution.py:39
  371.4 4.4 %copy-start.17 = (bf16[40,2048]{1,0:T(8,128)(2,1)}, bf16[40,2048]{1,0:T(8,128)(2,1)S(1)}, u32[]{:S(2)}) copy-start(bf16[40,2048]{1,0:T(8,128)(2,1)S(1)} %collective-permute-done.27) | copy-start | bytes 491524
  371.4 14.4 %collective-permute-start.32 = (bf16[40,2048]{1,0:T(8,128)(2,1)}, bf16[40,2048]{1,0:T(8,128)(2,1)}, u32[]{:S(2)}, u32[]{:S(2)}) collective-permute-start(bf16[40,2048]{1,0:T(8,128)(2,1)} %get-tuple-element.69), channel_id=1, source_target_pairs={{0,24},{4,28},{8,32},{12,36},{16,40},{20,44},{24,48},{28,52},{32,5... | collective-permute-start | bytes 491528 | tf_op jit(solution)/shard_map/ppermute | solution.py:39
  380.8 3.1 copy-start.3
  380.8 3.1 copy-start.16
  380.8 3.1 copy-start.18
  382.0 4.8 %copy-start.14 = (bf16[40,2048]{1,0:T(8,128)(2,1)S(1)}, bf16[40,2048]{1,0:T(8,128)(2,1)}, u32[]{:S(2)}) copy-start(bf16[40,2048]{1,0:T(8,128)(2,1)} %copy-done.13) | copy-start | bytes 491524
  382.9 4.8 %copy-start.22 = (f32[128]{0:T(128)S(1)}, f32[128]{0:T(128)}, u32[]{:S(2)}) copy-start(f32[128]{0:T(128)} %get-tuple-element.112) | copy-start | bytes 1540
  382.9 4.8 %copy-start.23 = (f32[128]{0:T(128)S(1)}, f32[128]{0:T(128)}, u32[]{:S(2)}) copy-start(f32[128]{0:T(128)} %get-tuple-element.113) | copy-start | bytes 1540
  (8 other events, 9.2 us)
Sparse Core Ops, SparseCore 0:
  10.9 57.4 all-gather.2
  104.4 26.6 reduce-scatter.4
  133.6 40.6 reduce-scatter.2
  190.7 53.0 all-gather.4
